TPU v7x, 128 devices: a whole 4x4x4 slice. The times are simulated.
128 devices in a mesh: col: 32 (over x, z, core), leg: 4 (over y).
Axes of the slice: x: 4, y: 4, z: 4, core: 2. Of those that a mesh axis runs over, the one named last changes fastest.
Arguments:
- coeffs: float32 [2048, 4, 128, 128], P(('col', 'leg')), may hold values from -0.5 to 0.5
- block_ids: int32 [2048, 4], P(('col', 'leg')), may hold values from 0 to 127
- col_counts: int32 [2048], P(('col', 'leg')), may hold values from 1 to 128
- primal: float32 [2048, 128], P(('col', 'leg')), may hold values from 0.3 to 3
- slack: float32 [2048, 128], P(('col', 'leg')), may hold values from 0.3 to 3
- cost: float32 [2048, 128], P(('col', 'leg')), may hold values from -6 to 6
- duals: float32 [128, 128], P('leg'), may hold values from -6 to 6
- demand: float32 [128, 128], P('leg'), may hold values from -6 to 6
Outputs:
- step_dual: float32 [128, 128], P('leg')
- step_primal: float32 [2048, 128], P(('col', 'leg'))
Inputs may be any that keep to these rules, and one draw needn't show every extreme that they name: `block_ids`: leg block of each tile; many tiles may share a block, the tiles of one column group too. `col_counts`: columns at or after this count in a column group are padding.
All inputs are finite; a program needn't handle non-finite values.
Results may differ from a plain program's by a relative error of at most 0.0003.
Values sent between devices are 32-bit elements; how exact they have to be, the bound alone decides.
No kernel may reach another device: no remote copies, remote signals or barrier semaphores. Data moves between devices by JAX's collectives and lax.ppermute only.
A program may use at most 128 MiB of HBM per device.

v0:
```python
import jax
import jax.numpy as jnp
from jax import lax
from jax.sharding import PartitionSpec as P

ITERS = 3


SIGMA = 0.3
REGULAR = 1.0
PRECISE = lax.Precision.HIGHEST


def invert_blocks(blocks):
    identity = jnp.eye(blocks.shape[1], dtype=jnp.float32)

    def invert_one(matrix):
        factor = jnp.linalg.cholesky(matrix)
        return jax.scipy.linalg.cho_solve((factor, True), identity)

    return jax.vmap(invert_one)(blocks + REGULAR * identity)


def per_device(coeffs, block_ids, col_counts, primal, slack, cost, duals, demand):
    lb_dev = duals.shape[0]
    group_count = coeffs.shape[0]
    span = coeffs.shape[1]
    rows_tile = coeffs.shape[2]
    columns = coeffs.shape[3]
    tile_count = group_count * span
    leg_count = lax.axis_size("leg")
    total_blocks = lb_dev * leg_count
    valid = (jnp.arange(columns, dtype=jnp.int32)[None, :] < col_counts[:, None]).astype(
        jnp.float32
    )
    tile_vals = coeffs * valid[:, None, None, :]
    totals_pair = lax.psum((jnp.sum(valid * primal * slack), jnp.sum(valid)), ("col", "leg"))
    mean_comp = totals_pair[0] / totals_pair[1]
    scaling = primal / slack
    flat_ids = block_ids.reshape(tile_count)
    all_duals = lax.all_gather(duals, "leg", axis=0, tiled=True)
    natural_hot = (flat_ids[:, None] == jnp.arange(total_blocks, dtype=jnp.int32)[None, :]).astype(
        jnp.float32
    )
    dual_tiles = jnp.dot(natural_hot, all_duals, precision=PRECISE).reshape(
        group_count, span, rows_tile
    )
    dual_res = cost - jnp.einsum("gsij,gsi->gj", tile_vals, dual_tiles, precision=PRECISE) - slack
    comp_res = SIGMA * mean_comp - primal * slack
    shifted = primal - scaling * dual_res + comp_res / slack

    def widen_all(vector):
        return lax.all_gather(vector, "leg", axis=0, tiled=True)

    def inner_sum(left, right):
        return lax.psum(jnp.sum(left * right), "leg")

    onehot = (flat_ids[:, None] == jnp.arange(total_blocks, dtype=jnp.int32)[None, :]).astype(
        jnp.float32
    )

    def transpose_apply(whole):
        per_tile = jnp.dot(onehot, whole, precision=PRECISE).reshape(group_count, span, rows_tile)
        return jnp.einsum("gsij,gsi->gj", tile_vals, per_tile, precision=PRECISE)

    def forward_partial(colvec):
        per_tile = jnp.einsum("gsij,gj->gsi", tile_vals, colvec, precision=PRECISE)
        return jnp.dot(onehot.T, per_tile.reshape(tile_count, rows_tile), precision=PRECISE)

    rhs_part = -forward_partial(shifted)
    weighted = tile_vals * scaling[:, None, None, :]
    gram = jnp.einsum("gsij,gskj->gsik", weighted, tile_vals, precision=PRECISE)
    gram = gram.reshape(tile_count, rows_tile, rows_tile)
    block_part = jnp.einsum("tb,tik->bik", onehot, gram, precision=PRECISE)
    rhs_sum, block_sum = lax.psum(
        (
            lax.psum_scatter(rhs_part, "leg", scatter_dimension=0, tiled=True),
            lax.psum_scatter(block_part, "leg", scatter_dimension=0, tiled=True),
        ),
        "col",
    )
    rhs = demand + rhs_sum
    inverse = invert_blocks(block_sum)

    def precondition(vector):
        return jnp.einsum("bij,bj->bi", inverse, vector, precision=PRECISE)

    step_dual = jnp.zeros_like(rhs)
    residual = rhs
    smoothed = precondition(residual)
    direction = smoothed
    norm_now = inner_sum(residual, smoothed)
    for turn in range(ITERS):
        operate_whole = widen_all(direction)
        narrow_shares = lax.psum_scatter(
            forward_partial(scaling * transpose_apply(operate_whole)),
            "leg",
            scatter_dimension=0,
            tiled=True,
        )
        image = lax.psum(narrow_shares, "col") + REGULAR * direction
        step_len = norm_now / inner_sum(direction, image)
        step_dual = step_dual + step_len * direction
        residual = residual - step_len * image
        if turn + 1 < ITERS:
            smoothed = precondition(residual)
            norm_next = inner_sum(residual, smoothed)
            direction = smoothed + norm_next / norm_now * direction
            norm_now = norm_next
    whole_step = widen_all(step_dual)
    step_primal = valid * (
        scaling * transpose_apply(whole_step) + comp_res / slack - scaling * dual_res
    )
    return (
        lax.dynamic_slice_in_dim(whole_step, lax.axis_index("leg") * lb_dev, lb_dev, 0),
        step_primal,
    )


def solution(mesh):
    return jax.shard_map(
        per_device,
        mesh=mesh,
        in_specs=(
            P(("col", "leg"), None, None, None),
            P(("col", "leg"), None),
            P(("col", "leg")),
            P(("col", "leg"), None),
            P(("col", "leg"), None),
            P(("col", "leg"), None),
            P("leg", None),
            P("leg", None),
        ),
        out_specs=(P("leg", None), P(("col", "leg"), None)),
        check_vma=False,
    )
```

profile of v0, /device:TPU:1, one launch (start us, length us, event | category | flops | bytes accessed | tf_op | source)
XLA Modules:
  0.0 1629.3 jit_solution(10132136737136496447)
XLA Ops:
  8.1 10.6 all_gather.15
  19.6 1.4 fusion.43
  21.1 68.9 %all-reduce = (f32[]{:T(128)}, f32[]{:T(128)}) all-reduce(f32[]{:T(128)} %get-tuple-element.5, f32[]{:T(128)} %get-tuple-element.4), channel_id=1, replica_groups=mesh['col'=32,'leg'=4] {'col','leg'}, use_global_device_ids=true, to_apply=%region_1.0 | all-reduce | flops 2 | bytes 16 | tf_op jit(solution)/shard_map/psum | solution.py:37
  91.3 4.3 fusion.18
  95.7 8.9 fusion
  104.5 9.9 fusion.2
  114.4 9.3 copy.22
  123.8 5.9 fusion.17
  129.7 1.0 convolution_negate_fusion
  130.7 71.0 %reduce-scatter.8.cloned.1.call-done = f32[32,128,128]{1,2,0:T(8,128)} async-done(((f32[128,128,128]{1,2,0:T(8,128)}), f32[32,128,128]{1,2,0:T(8,128)}) %reduce-scatter.8.cloned.1.call-update) | async-done | bytes 2097168 | tf_op jit(solution)/shard_map/reduce_scatter | solution.py:78
  202.0 19.9 %reduce-scatter.6.cloned.1.call-done = f32[32,128]{1,0:T(8,128)} async-done(((f32[128,128]{1,0:T(8,128)}), f32[32,128]{1,0:T(8,128)}) %reduce-scatter.6.cloned.1.call-update) | async-done | bytes 16400 | tf_op jit(solution)/shard_map/reduce_scatter | solution.py:77
  221.9 123.6 %psum.93 = f32[32,128]{1,0:T(8,128)S(1)} all-reduce(f32[32,128]{1,0:T(8,128)} %reduce-scatter.6.cloned.1.call-done), channel_id=1, replica_groups=mesh['col'=32,'leg'=4] {'col'}, use_global_device_ids=true, to_apply=%region_5.0 | all-reduce | flops 4096 | bytes 32768 | tf_op jit(solution)/shard_map/psum | solution.py:75
  345.5 3.3 broadcast_add_fusion
  348.8 2.9 copy.24
  351.7 3.2 fusion.8
  354.9 375.8 %custom-call.11 = f32[32,128,128]{2,1,0:T(8,128)S(1)} custom-call(f32[32,128,128]{2,1,0:T(8,128)} %fusion.8), custom_call_target="Cholesky" | custom-call | tf_op jit(solution)/shard_map/vmap(jit(cholesky))/cholesky | solution.py:18
  731.0 1.7 select_bitcast_fusion
  732.6 315.3 %custom-call.12 = f32[32,1,128,128]{2,3,1,0:T(8,128)S(1)} custom-call(f32[32,1,128,128]{3,2,1,0:T(8,128)} %select_bitcast_fusion), custom_call_target="InvertDiagBlocksLowerTriangular" | custom-call | tf_op jit(solution)/shard_map/vmap(jit(_cho_solve))/triangular_solve | solution.py:19
  1047.9 1.3 copy-done.5
  1049.3 3.5 fusion.6
  1052.8 4.0 fusion.4
  1056.8 3.3 fusion.44
  1060.1 9.2 all_gather.16
  1069.6 2.5 fusion.15
  1072.0 3.7 fusion.14
  1075.7 1.0 fusion.25
  1076.8 20.8 %reduce-scatter.10.cloned.1.call-done = f32[32,128]{1,0:T(8,128)} async-done(((f32[128,128]{1,0:T(8,128)}), f32[32,128]{1,0:T(8,128)}) %reduce-scatter.10.cloned.1.call-update) | async-done | bytes 16400 | tf_op jit(solution)/shard_map/reduce_scatter | solution.py:95
  1097.5 123.3 %psum.96 = f32[32,128]{1,0:T(8,128)S(1)} all-reduce(f32[32,128]{1,0:T(8,128)} %reduce-scatter.10.cloned.1.call-done), channel_id=1, replica_groups=mesh['col'=32,'leg'=4] {'col'}, use_global_device_ids=true, to_apply=%region_13.14 | all-reduce | flops 4096 | bytes 32768 | tf_op jit(solution)/shard_map/psum | solution.py:101
  1221.4 7.7 all-reduce.1
  1230.4 3.3 fusion.45
  1234.4 7.0 psum.98
  1242.7 9.8 all_gather.17
  1252.8 4.2 fusion.13
  1257.0 3.7 fusion.12
  1261.8 24.6 %reduce-scatter.12.cloned.1.call-done = f32[32,128]{1,0:T(8,128)} async-done(((f32[128,128]{1,0:T(8,128)}), f32[32,128]{1,0:T(8,128)}) %reduce-scatter.12.cloned.1.call-update) | async-done | bytes 16400 | tf_op jit(solution)/shard_map/reduce_scatter | solution.py:95
  1286.3 123.2 %psum.99 = f32[32,128]{1,0:T(8,128)S(1)} all-reduce(f32[32,128]{1,0:T(8,128)} %reduce-scatter.12.cloned.1.call-done), channel_id=1, replica_groups=mesh['col'=32,'leg'=4] {'col'}, use_global_device_ids=true, to_apply=%region_19.20 | all-reduce | flops 4096 | bytes 32768 | tf_op jit(solution)/shard_map/psum | solution.py:101
  1410.2 7.7 psum.100
  1419.2 3.3 fusion.46
  1423.2 7.0 psum.101
  1431.5 9.3 all_gather.18
  1441.0 4.2 fusion.11
  1445.2 3.7 fusion.10
  1448.9 1.0 fusion.21
  1449.9 24.9 %reduce-scatter.14.cloned.1.call-done = f32[32,128]{1,0:T(8,128)} async-done(((f32[128,128]{1,0:T(8,128)}), f32[32,128]{1,0:T(8,128)}) %reduce-scatter.14.cloned.1.call-update) | async-done | bytes 16400 | tf_op jit(solution)/shard_map/reduce_scatter | solution.py:95
  1474.8 123.2 %psum.102 = f32[32,128]{1,0:T(8,128)S(1)} all-reduce(f32[32,128]{1,0:T(8,128)} %reduce-scatter.14.cloned.1.call-done), channel_id=1, replica_groups=mesh['col'=32,'leg'=4] {'col'}, use_global_device_ids=true, to_apply=%region_25.26 | all-reduce | flops 4096 | bytes 32768 | tf_op jit(solution)/shard_map/psum | solution.py:101
  1598.6 7.7 psum.103
  1607.6 9.0 all_gather.19
  1616.8 4.2 fusion.16
  (66 shorter events, 8.9 us)
Async XLA Ops:
  7.2 88.4 %copy-start.6 = (f32[16,128]{1,0:T(8,128)S(1)}, f32[16,128]{1,0:T(8,128)}, u32[]{:S(2)}) copy-start(f32[16,128]{1,0:T(8,128)} %param.11) | copy-start | bytes 24580
  7.2 88.4 %copy-start.7 = (f32[16,128]{1,0:T(8,128)S(1)}, f32[16,128]{1,0:T(8,128)}, u32[]{:S(2)}) copy-start(f32[16,128]{1,0:T(8,128)} %param.12) | copy-start | bytes 24580
  7.2 88.4 %copy-start.8 = (f32[16,128]{1,0:T(8,128)S(1)}, f32[16,128]{1,0:T(8,128)}, u32[]{:S(2)}) copy-start(f32[16,128]{1,0:T(8,128)} %param.13) | copy-start | bytes 24580
  7.2 194.6 %reduce-scatter.8.cloned.1.call-start = ((), (), s32[]{:S(2)}) async-start(), calls=%async_computation.6 | async-start | bytes 10485760 | tf_op jit(solution)/shard_map/reduce_scatter | solution.py:78
  91.3 4.4 copy-start
  123.8 221.7 %copy-start.9 = (f32[32,128]{1,0:T(8,128)S(1)}, f32[32,128]{1,0:T(8,128)}, u32[]{:S(2)}) copy-start(f32[32,128]{1,0:T(8,128)} %param.15) | copy-start | bytes 49156
  123.8 98.1 %reduce-scatter.6.cloned.1.call-start = ((), (), s32[]{:S(2)}) async-start(), calls=%async_computation.5 | async-start | bytes 81920 | tf_op jit(solution)/shard_map/reduce_scatter | solution.py:77
  130.7 214.8 %all-reduce.4.cloned.1.call-start = ((), (), s32[]{:S(2)}) async-start(), calls=%async_computation.7 | async-start | bytes 4194304 | tf_op jit(solution)/shard_map/psum | solution.py:75
  201.8 895.7 %reduce-scatter.10.cloned.1.call-start = ((), (), s32[]{:S(2)}) async-start(), calls=%async_computation.8 | async-start | bytes 81920 | tf_op jit(solution)/shard_map/reduce_scatter | solution.py:95
  345.5 6.2 copy-start.4
  1047.9 1.4 copy-start.5
  1052.8 16.8 %copy-start.1 = (f32[16,4,128,128]{3,2,1,0:T(8,128)S(1)}, f32[16,4,128,128]{3,2,1,0:T(8,128)}, u32[]{:S(2)}) copy-start(f32[16,4,128,128]{3,2,1,0:T(8,128)} %param.8) | copy-start | bytes 12582916
  1076.7 209.6 %reduce-scatter.12.cloned.1.call-start = ((), (), s32[]{:S(2)}) async-start(), calls=%async_computation.9 | async-start | bytes 81920 | tf_op jit(solution)/shard_map/reduce_scatter | solution.py:95
  1242.7 14.3 copy-start.2
  1261.7 213.1 %reduce-scatter.14.cloned.1.call-start = ((), (), s32[]{:S(2)}) async-start(), calls=%async_computation.10 | async-start | bytes 81920 | tf_op jit(solution)/shard_map/reduce_scatter | solution.py:95
  1431.5 13.7 copy-start.3
  1445.2 175.8 %copy-start.10 = (s32[16]{0:T(128)S(1)}, s32[16]{0:T(128)}, u32[]{:S(2)}) copy-start(s32[16]{0:T(128)} %param.10) | copy-start | bytes 196
Sparse Core Ops, SparseCore 0:
  123.9 77.8 reduce-scatter.7
  204.1 17.7 reduce-scatter.5
  225.5 109.3 all-reduce.3
  1076.8 20.6 reduce-scatter.9
  1261.8 24.4 reduce-scatter.11
  1450.0 24.6 reduce-scatter.13
where the time goes:
time: 1650 us; the launch traced here: 1630 us
  other arithmetic  705 us (43%)
  blocking collectives  647 us (39%)
  waiting for transfers between devices  161 us (10%)
  matrix products  77.4 us (5%)
  between operations  22.7 us (1%)
    another operation x4, other arithmetic, invert_one(): factor = jnp.linalg.cholesky(matrix)  376 us
    psum x3, blocking collectives, per_device(): image = lax.psum(narrow_shares, 'col') + REGULAR * direction  370 us
    another operation x3, other arithmetic, invert_one(): return jax.scipy.linalg.cho_solve((factor, True), identity)  317 us
    psum x1, blocking collectives, per_device(): lax.psum((lax.psum_scatter(rhs_part, 'leg', scatter_dimension=0, tiled=Tr...  124 us
    reduce_scatter x1, waiting for transfers between devices, per_device(): lax.psum_scatter(block_part, 'leg', scatter_dimension=0, tiled=True)  71 us
    reduce_scatter x3, waiting for transfers between devices, per_device(): lax.psum_scatter(forward_partial(scaling * transpose_apply(operate_whole)...  70.2 us
    psum x1, blocking collectives, per_device(): lax.psum((jnp.sum(valid * primal * slack), jnp.sum(valid)), ('col', 'leg'))  68.9 us
    all_gather x4, blocking collectives, widen_all(): return lax.all_gather(vector, 'leg', axis=0, tiled=True)  37.3 us
  transfers between devices with their start and end apart: 6, of which 5 were waited for; matrix products, arithmetic and copies ran while one was open for 0% of the time, Pallas kernels for 0%

commit v1 on v0

v1 whole, which is shorter than its diff:
```python
import jax
import jax.numpy as jnp
from jax import lax
from jax.experimental import pallas as pl
from jax.experimental.pallas import tpu as pltpu
from jax.sharding import Mesh, PartitionSpec as P

ITERS = 3
SIGMA = 0.3
REGULAR = 1.0
PRECISE = lax.Precision.HIGHEST

N = 128
HALF = 64
SPAN = 4
GROUPS = 16
TILES = GROUPS * SPAN
EXTRA = 8
ROWS = HALF + EXTRA

VMEM = pltpu.MemorySpace.VMEM
SMEM = pltpu.MemorySpace.SMEM
NT = (((1,), (1,)), ((), ()))


def iota(shape, axis):
    return lax.broadcasted_iota(jnp.int32, shape, axis)


def vspec():
    return pl.BlockSpec(memory_space=VMEM)


def sspec():
    return pl.BlockSpec(memory_space=SMEM)


def f32(*shape):
    return jax.ShapeDtypeStruct(shape, jnp.float32)


def params():
    return pltpu.CompilerParams(vmem_limit_bytes=48 << 20)


def gram_kernel(
    ids, counts, me, coeffs, primal, slack, own, other, small, scale_out, acc, diag, sem
):
    g = pl.program_id(0)

    @pl.when(g == 0)
    def _():
        acc[...] = jnp.zeros_like(acc)
        diag[...] = jnp.zeros_like(diag)

    valid = iota((1, N), 1) < counts[g]
    scale = jnp.where(valid, primal[pl.ds(g, 1), :] / slack[pl.ds(g, 1), :], 0.0)
    scale_out[pl.ds(g, 1), :] = scale
    row = iota((HALF, N), 0)
    lane = iota((HALF, N), 1)
    lower = jnp.logical_or(row >= lane, lane >= HALF)
    for s in range(SPAN):
        tile = coeffs[0, s]
        gram = lax.dot_general(
            tile * scale, tile, NT, precision=PRECISE, preferred_element_type=jnp.float32
        )
        top = gram[:HALF]
        rolled = pltpu.roll(gram[HALF:], HALF, 1)
        packed = jnp.where(lower, top, rolled)
        line = jnp.sum(jnp.where(row == lane, rolled, 0.0), axis=0, keepdims=True)
        block = ids[g * SPAN + s]
        place = ((block & 1) ^ me[0]) * HALF + (block >> 1)
        acc[place] += packed
        diag[place, 0:1, :] += line

    @pl.when(g == GROUPS - 1)
    def _():
        copies = [
            pltpu.make_async_copy(acc.at[pl.ds(0, HALF)], own, sem.at[0]),
            pltpu.make_async_copy(acc.at[pl.ds(HALF, HALF)], other, sem.at[1]),
            pltpu.make_async_copy(diag, small, sem.at[2]),
        ]
        for copy in copies:
            copy.start()
        for copy in copies:
            copy.wait()


def run_gram(ids, counts, me, coeffs, primal, slack):
    return pl.pallas_call(
        gram_kernel,
        out_shape=(f32(HALF, HALF, N), f32(HALF, HALF, N), f32(N, EXTRA, N), f32(GROUPS, N)),
        grid_spec=pltpu.PrefetchScalarGridSpec(
            num_scalar_prefetch=3,
            grid=(GROUPS,),
            in_specs=[
                pl.BlockSpec((1, SPAN, N, N), lambda g, *_: (g, 0, 0, 0)),
                pl.BlockSpec((GROUPS, N), lambda g, *_: (0, 0)),
                pl.BlockSpec((GROUPS, N), lambda g, *_: (0, 0)),
            ],
            out_specs=(
                pl.BlockSpec(memory_space=pl.ANY),
                pl.BlockSpec(memory_space=pl.ANY),
                pl.BlockSpec(memory_space=pl.ANY),
                pl.BlockSpec((GROUPS, N), lambda g, *_: (0, 0)),
            ),
            scratch_shapes=[
                pltpu.VMEM((N, HALF, N), jnp.float32),
                pltpu.VMEM((N, EXTRA, N), jnp.float32),
                pltpu.SemaphoreType.DMA((3,)),
            ],
        ),
        compiler_params=params(),
        cost_estimate=pl.CostEstimate(
            flops=TILES * 2 * N**3 * 6, bytes_accessed=12 << 20, transcendentals=0
        ),
        name="gram",
    )(ids, counts, me, coeffs, primal, slack)


def transpose_apply(ids, coeffs, vector, spread):
    for t in range(TILES):
        spread[pl.ds(t, 1), :] = vector[pl.ds(ids[t], 1), :]
    columns = jnp.transpose(spread[...])
    lines = []
    for g in range(GROUPS):
        total = None
        for s in range(SPAN):
            t = g * SPAN + s
            prod = coeffs[g, s] * jnp.broadcast_to(columns[:, t : t + 1], (N, N))
            part = jnp.sum(prod.reshape(N // 8, 8, N), axis=0)
            total = part if total is None else total + part
        lines.append(jnp.sum(total, axis=0, keepdims=True))
    return jnp.concatenate(lines, axis=0)


def forward_apply(coeffs, colvec):
    lane = iota((N, N), 1)
    columns = jnp.zeros((N, N), jnp.float32)
    for g in range(GROUPS):
        w = colvec[g : g + 1, :]
        for s in range(SPAN):
            t = g * SPAN + s
            total = jnp.sum(coeffs[g, s] * w, axis=1, keepdims=True)
            columns = jnp.where(lane == t, total, columns)
    return jnp.transpose(columns)[:TILES]


def place_rows(ids_line, rows, count, stride, offset):
    hot = (iota((count, TILES), 0) == stride * ids_line + offset).astype(jnp.float32)
    return jnp.dot(hot, rows, precision=PRECISE, preferred_element_type=jnp.float32)


def rhs_kernel(
    ids, counts, ids_line, coeffs, dual0, dual1, dual2, dual3, primal, slack, cost, scale, small,
    small_out, dual_res_out, spread, duals, valid_s,
):
    for k, part in enumerate((dual0, dual1, dual2, dual3)):
        duals[pl.ds(k * 32, 32), :] = part[...]
    for g in range(GROUPS):
        valid_s[pl.ds(g, 1), :] = (iota((1, N), 1) < counts[g]).astype(jnp.float32)
    valid = valid_s[...]
    dual_res = cost[...] - valid * transpose_apply(ids[0], coeffs, duals, spread) - slack[...]
    dual_res_out[...] = dual_res
    first = forward_apply(coeffs, scale[...] * dual_res)
    second = forward_apply(coeffs, valid / slack[...])
    small_out[:, 0:1, :] = small[:, 0:1, :]
    rows1 = place_rows(ids_line[...], first, N, 1, 0)
    rows2 = place_rows(ids_line[...], second, N, 1, 0)
    comp = jnp.sum(valid * primal[...] * slack[...], axis=0, keepdims=True)
    used = jnp.sum(valid, axis=0, keepdims=True)
    small_out[:, 1:2, :] = rows1.reshape(N, 1, N)
    small_out[:, 2:3, :] = rows2.reshape(N, 1, N)
    small_out[:, 3:4, :] = jnp.broadcast_to(comp.reshape(1, 1, N), (N, 1, N))
    small_out[:, 4:5, :] = jnp.broadcast_to(used.reshape(1, 1, N), (N, 1, N))
    small_out[:, 5:8, :] = jnp.zeros((N, 3, N), jnp.float32)


class Row:
    def __init__(self, ref, row):
        self.ref, self.row = ref, row

    def __getitem__(self, t):
        return self.ref[self.row, t]


def run_rhs(ids_dual, counts, ids_line, coeffs, duals, primal, slack, cost, scale, small):
    def kernel(ids_ref, *refs):
        rhs_kernel((Row(ids_ref, 0),), *refs)

    return pl.pallas_call(
        kernel,
        out_shape=(f32(N, EXTRA, N), f32(GROUPS, N)),
        in_specs=[sspec(), sspec()] + [vspec()] * 11,
        out_specs=(vspec(), vspec()),
        scratch_shapes=[
            pltpu.VMEM((TILES, N), jnp.float32),
            pltpu.VMEM((N, N), jnp.float32),
            pltpu.VMEM((GROUPS, N), jnp.float32),
        ],
        compiler_params=params(),
        cost_estimate=pl.CostEstimate(flops=1 << 27, bytes_accessed=6 << 20, transcendentals=0),
        name="rhs",
    )(ids_dual, counts, ids_line, coeffs, *duals, primal, slack, cost, scale, small)


def join_kernel(own, got, small_own, small_got, out):
    out[:, 0:HALF, :] = own[...] + got[...]
    out[:, HALF:ROWS, :] = small_own[...] + small_got[...]


def run_join(own, got, small_own, small_got):
    step = 8
    big = pl.BlockSpec((step, HALF, N), lambda i: (i, 0, 0))
    little = pl.BlockSpec((step, EXTRA, N), lambda i: (i, 0, 0))
    return pl.pallas_call(
        join_kernel,
        out_shape=f32(HALF, ROWS, N),
        grid=(HALF // step,),
        in_specs=[big, big, little, little],
        out_specs=pl.BlockSpec((step, ROWS, N), lambda i: (i, 0, 0)),
        compiler_params=params(),
        name="join",
    )(own, got, small_own, small_got)


def small_inverse(cols):
    cols = list(cols)
    sub = iota((8, N), 0)
    for m in range(8):
        rows = [jnp.broadcast_to(c[m : m + 1, :], (8, N)) for c in cols]
        inv = 1.0 / rows[m]
        factor = cols[m]
        here = sub == m
        for j in range(8):
            if j == m:
                cols[j] = jnp.where(here, inv, -factor * inv)
            else:
                scaled = rows[j] * inv
                cols[j] = jnp.where(here, scaled, cols[j] - factor * scaled)
    return cols


def invert(panels):
    panels = list(panels)
    lane = iota((8, N), 1)
    count = len(panels)
    for k in range(count):
        mine = jnp.logical_and(lane >= 8 * k, lane < 8 * k + 8)
        pivot = panels[k]
        cols = [jnp.broadcast_to(pivot[:, 8 * k + m : 8 * k + m + 1], (8, N)) for m in range(8)]
        cols = small_inverse(cols)
        total = None
        for m in range(8):
            term = cols[m] * jnp.broadcast_to(pivot[m : m + 1, :], (8, N))
            total = term if total is None else total + term
        for m in range(8):
            total = jnp.where(lane == 8 * k + m, cols[m], total)
        rows = [jnp.broadcast_to(total[m : m + 1, :], (8, N)) for m in range(8)]
        for step in range(1, count):
            i = (k + step) % count
            old = panels[i]
            new = jnp.where(mine, 0.0, old)
            for m in range(8):
                col = jnp.broadcast_to(old[:, 8 * k + m : 8 * k + m + 1], (8, N))
                new = new - col * rows[m]
            panels[i] = new
        panels[k] = total
    return panels


def pair_rows(first, second):
    return jnp.where((iota((8, N), 0) & 1) == 0, first, second)


def set_message(msg, line, scalar):
    pair = pair_rows(jnp.broadcast_to(line, (8, N)), jnp.broadcast_to(scalar, (8, N)))
    msg[...] = jnp.broadcast_to(pair[None], (N // 4, 8, N)).reshape(2 * N, N)


def first_kernel(me, got, demand, inverse_out, residual_out, mu_out, msg):
    def add(i, carry):
        return carry + got[i]

    total = lax.fori_loop(1, HALF, add, got[0], unroll=7)
    packed = total[:HALF]
    line = total[HALF : HALF + 1]
    tail = total[HALF:]
    comp = jnp.sum(tail[3:4], axis=1, keepdims=True)
    used = jnp.sum(tail[4:5], axis=1, keepdims=True)
    mu = SIGMA * (comp / used)
    mu_out[...] = jnp.broadcast_to(mu, (8, N))
    residual = demand[pl.ds(me[0], 1), :] + tail[1:2] - mu * tail[2:3]
    residual_out[...] = jnp.broadcast_to(residual, (8, N))

    row = iota((HALF, N), 0)
    lane = iota((HALF, N), 1)
    flipped = jnp.transpose(jnp.concatenate([packed, jnp.zeros((HALF, N), jnp.float32)], axis=0))
    flip_top, flip_bottom = flipped[:HALF], flipped[HALF:]
    top = jnp.where(jnp.logical_or(row >= lane, lane >= HALF), packed, flip_top)
    corner = jnp.where(row < lane, packed, flip_top)
    corner = jnp.where(row == lane, jnp.broadcast_to(line, (HALF, N)), corner)
    bottom = jnp.where(lane < HALF, flip_bottom, pltpu.roll(corner, HALF, 1))
    top = top + jnp.where(row == lane, REGULAR, 0.0)
    bottom = bottom + jnp.where(row + HALF == lane, REGULAR, 0.0)
    panels = [top[8 * i : 8 * i + 8] for i in range(8)]
    panels += [bottom[8 * i : 8 * i + 8] for i in range(8)]
    inverse = jnp.concatenate(invert(panels), axis=0)
    inverse_out[...] = inverse
    smoothed = jnp.dot(
        jnp.broadcast_to(residual, (8, N)),
        inverse,
        precision=PRECISE,
        preferred_element_type=jnp.float32,
    )[0:1]
    norm = jnp.sum(residual * smoothed, axis=1, keepdims=True)
    set_message(msg, smoothed, norm)


def run_first(me, got, demand):
    return pl.pallas_call(
        first_kernel,
        out_shape=(f32(N, N), f32(8, N), f32(8, N), f32(2 * N, N)),
        in_specs=[sspec(), vspec(), vspec()],
        out_specs=(vspec(),) * 4,
        compiler_params=params(),
        name="first",
    )(me, got, demand)


def sum_pairs(got):
    total = jnp.sum(got[...].reshape(N // 4, 8, N), axis=0)
    even = (total[0:1] + total[2:3]) + (total[4:5] + total[6:7])
    odd = (total[1:2] + total[3:4]) + (total[5:6] + total[7:8])
    return even, odd


def owner_kernel(me, got, direction, norms, residual, inverse, residual_out, msg):
    image, curve = sum_pairs(got)
    image = image + REGULAR * direction[pl.ds(me[0], 1), :]
    curve = jnp.sum(curve, axis=1, keepdims=True)
    step_len = norms[0:1, :] / (curve + norms[1:2, :])
    new = residual[0:1, :] - step_len * image
    residual_out[...] = pair_rows(jnp.broadcast_to(new, (8, N)), jnp.broadcast_to(curve, (8, N)))
    smoothed = jnp.dot(
        jnp.broadcast_to(new, (8, N)),
        inverse[...],
        precision=PRECISE,
        preferred_element_type=jnp.float32,
    )[0:1]
    set_message(msg, smoothed, jnp.sum(new * smoothed, axis=1, keepdims=True))


def run_owner(me, got, direction, norms, residual, inverse):
    return pl.pallas_call(
        owner_kernel,
        out_shape=(f32(8, N), f32(2 * N, N)),
        in_specs=[sspec()] + [vspec()] * 5,
        out_specs=(vspec(),) * 2,
        compiler_params=params(),
        name="owner",
    )(me, got, direction, norms, residual, inverse)


def tile_kernel(last, begin, ids, ids_line, coeffs, scale, got, *refs):
    if begin:
        direction_out, applied_out, norms_out, msg, spread = refs
    else:
        direction_in, norms_in, direction_out, applied_out, norms_out, msg, spread = refs
    pairs = got[...].reshape(N, 2, N)
    smoothed = pairs[:, 0, :]
    norm = jnp.sum(pairs[:, 1, :], axis=0, keepdims=True)
    if begin:
        direction = smoothed
    else:
        direction = smoothed + (norm / norms_in[0:1, :]) * direction_in[...]
    direction_out[...] = direction
    square = jnp.sum(jnp.sum(direction * direction, axis=0, keepdims=True), axis=1, keepdims=True)
    square = jnp.broadcast_to(REGULAR * square, (1, N))
    norms_out[0:1, :] = norm
    norms_out[1:2, :] = square
    applied = transpose_apply(ids, coeffs, direction_out, spread)
    applied_out[...] = applied
    weighted = scale[...] * applied
    curve = jnp.sum(weighted * applied, axis=0, keepdims=True)
    if last:
        msg[...] = jnp.broadcast_to(curve, (N, N))
    else:
        image = place_rows(ids_line[...], forward_apply(coeffs, weighted), 2 * N, 2, 0)
        odd = (iota((2 * N, N), 0) & 1) == 1
        msg[...] = jnp.where(odd, jnp.broadcast_to(curve, (2 * N, N)), image)


def run_tile(last, ids, ids_line, coeffs, scale, got, direction=None, norms=None):
    begin = direction is None
    extra = () if begin else (direction, norms)

    def kernel(*refs):
        tile_kernel(last, begin, *refs)

    return pl.pallas_call(
        kernel,
        out_shape=(f32(N, N), f32(GROUPS, N), f32(8, N), f32(N if last else 2 * N, N)),
        in_specs=[sspec()] + [vspec()] * (4 + len(extra)),
        out_specs=(vspec(),) * 4,
        scratch_shapes=[pltpu.VMEM((TILES, N), jnp.float32)],
        compiler_params=params(),
        name="tile_last" if last else "tile",
    )(ids, ids_line, coeffs, scale, got, *extra)


def final_kernel(
    leg, counts, got, curve0, curve1, d0, d1, d2, u0, u1, u2, n0, n1, n2, mu, primal, slack,
    scale, dual_res, step_dual, step_primal,
):
    curve2 = jnp.sum(jnp.sum(got[...], axis=0, keepdims=True), axis=1, keepdims=True)
    lens = []
    for curve, norms in ((curve0[1:2, :], n0), (curve1[1:2, :], n1), (curve2, n2)):
        lens.append(norms[0:1, :] / (curve + norms[1:2, :]))
    at = pl.ds(pl.multiple_of(leg[0] * 32, 32), 32)
    step_dual[...] = lens[0] * d0[at, :] + lens[1] * d1[at, :] + lens[2] * d2[at, :]
    applied = lens[0] * u0[...] + lens[1] * u1[...] + lens[2] * u2[...]
    inner = scale[...] * (applied - dual_res[...]) + (mu[0:1, :] / slack[...] - primal[...])
    for g in range(GROUPS):
        valid = iota((1, N), 1) < counts[g]
        step_primal[g : g + 1, :] = jnp.where(valid, inner[g : g + 1, :], 0.0)


def run_final(leg, counts, *args):
    return pl.pallas_call(
        final_kernel,
        out_shape=(f32(32, N), f32(GROUPS, N)),
        in_specs=[sspec(), sspec()] + [vspec()] * len(args),
        out_specs=(vspec(), vspec()),
        compiler_params=params(),
        name="final",
    )(leg, counts, *args)


ALL = ("leg", "x", "z", "core")
CHIPS = ("leg", "x", "z")


def exchange(rows, axes):
    return lax.all_to_all(rows, axes, split_axis=0, concat_axis=0, tiled=True)


def per_device(coeffs, block_ids, col_counts, primal, slack, cost, duals, demand):
    leg = lax.axis_index("leg")
    core = lax.axis_index("core")
    col = (lax.axis_index("x") * 4 + lax.axis_index("z")) * 2 + core
    ids = block_ids.reshape(TILES)
    me = (leg * 32 + col).astype(jnp.int32).reshape(1)
    core1 = core.astype(jnp.int32).reshape(1)

    parts = [duals]
    for k in (1, 2, 3):
        parts.append(lax.ppermute(duals, "leg", [(i, (i + k) % 4) for i in range(4)]))
    ids_dual = ((((leg - (ids >> 5)) & 3) << 5) | (ids & 31)).reshape(1, TILES)
    place = ((ids & 1) ^ core) * HALF + (ids >> 1)

    own, other, small, scale = run_gram(ids, col_counts, core1, coeffs, primal, slack)
    swap = [(0, 1), (1, 0)]
    got_big = lax.ppermute(other, "core", swap)
    small, dual_res = run_rhs(
        ids_dual, col_counts, place.reshape(1, TILES), coeffs, parts, primal, slack, cost, scale,
        small,
    )
    got_small = lax.ppermute(small[HALF:], "core", swap)
    joined = run_join(own, got_big, small[:HALF], got_small)
    blocks = exchange(joined, CHIPS)
    inverse, residual, mu, msg = run_first(col.astype(jnp.int32).reshape(1), blocks, demand)

    ids_line = ids.reshape(1, TILES)
    direction = norms = None
    kept = []
    curves = []
    for turn in range(ITERS):
        got = exchange(msg, ALL)
        last = turn + 1 == ITERS
        direction, applied, norms, msg = run_tile(
            last, ids, ids_line, coeffs, scale, got, direction, norms
        )
        kept.append((direction, applied, norms))
        got = exchange(msg, ALL)
        if not last:
            residual, msg = run_owner(me, got, direction, norms, residual, inverse)
            curves.append(residual)
    (d0, u0, n0), (d1, u1, n1), (d2, u2, n2) = kept
    return run_final(
        leg.astype(jnp.int32).reshape(1), col_counts, got, curves[0], curves[1], d0, d1, d2,
        u0, u1, u2, n0, n1, n2, mu, primal, slack, scale, dual_res,
    )


def solution(mesh):
    fine = Mesh(mesh.devices.reshape(4, 4, 2, 4), ("x", "z", "core", "leg"))
    every = ("x", "z", "core", "leg")
    return jax.shard_map(
        per_device,
        mesh=fine,
        in_specs=(
            P(every, None, None, None),
            P(every, None),
            P(every),
            P(every, None),
            P(every, None),
            P(every, None),
            P("leg", None),
            P("leg", None),
        ),
        out_specs=(P("leg", None), P(every, None)),
        check_vma=False,
    )
```

time: 1650 us -> 196 us (0.12); the launches traced: 1630 us -> 195 us
  other arithmetic: 705 us -> 0.01 us
  blocking collectives: 647 us -> 73 us
  waiting for transfers between devices: 161 us -> 42.8 us
  matrix products: 77.4 us -> 0 us
  Pallas kernels: 0 us -> 44.6 us
  starting transfers between devices: 0.24 us -> 24.5 us
  between operations: 22.7 us -> 0.82 us
    another operation x7 -> x0, other arithmetic: 693 us -> none  [the longest x4 376 us: invert_one(): factor = jnp.linalg.cholesky(matrix)]
    psum x10 -> x0, blocking collectives: 599 us -> none  [the longest x3 370 us: per_device(): image = lax.psum(narrow_shares, 'col') + REGULAR * direction]
    reduce_scatter x5 -> x0, waiting for transfers between devices: 161 us -> none  [the longest x1 71 us: per_device(): lax.psum_scatter(block_part, 'leg', scatter_dimension=0, tiled=True)]
    all_to_all x0 -> x5, blocking collectives: none -> 73 us  [exchange(): return lax.all_to_all(rows, axes, split_axis=0, concat_axis=0, tiled=True)]
    dot_general x23 -> x0, matrix products: 70 us -> none  [the longest x4 17 us: forward_partial(): per_tile = jnp.einsum('gsij,gj->gsi', tile_vals, colvec, precision=PRECISE)]
    all_gather x5 -> x0, blocking collectives: 47.9 us -> none  [the longest x4 37.3 us: widen_all(): return lax.all_gather(vector, 'leg', axis=0, tiled=True)]
    pallas_call x0 -> x10, Pallas kernels: none -> 44.6 us  [the longest x1 16.9 us: run_gram(): pl.pallas_call(gram_kernel, out_shape=(f32(HALF, HALF, N), f32(HALF, HALF...]
    all_to_all x0 -> x2, waiting for transfers between devices: none -> 40.6 us  [exchange(): return lax.all_to_all(rows, axes, split_axis=0, concat_axis=0, tiled=True)]
  transfers between devices with their start and end apart: 6 -> 7, of which waited for: 5 -> 4; matrix products, arithmetic and copies ran while one was open for 0% -> 0% of each run, Pallas kernels for 0% -> 2%
where the time goes in v1:
time: 196 us; the launch traced here: 195 us
  blocking collectives  73 us (37%)
  Pallas kernels  44.6 us (23%)
  waiting for transfers between devices  42.8 us (22%)
  starting transfers between devices  24.5 us (12%)
  local copies, waits for them, and re-layouts  9.59 us (5%)
    all_to_all x5, blocking collectives, exchange(): return lax.all_to_all(rows, axes, split_axis=0, concat_axis=0, tiled=True)  73 us
    all_to_all x2, waiting for transfers between devices, exchange(): return lax.all_to_all(rows, axes, split_axis=0, concat_axis=0, tiled=True)  40.6 us
    pallas_call x1, Pallas kernels, run_gram(): pl.pallas_call(gram_kernel, out_shape=(f32(HALF, HALF, N), f32(HALF, HALF...  16.9 us
    all_to_all x2, starting transfers between devices, exchange(): return lax.all_to_all(rows, axes, split_axis=0, concat_axis=0, tiled=True)  15.7 us
    pallas_call x3, Pallas kernels, run_tile(): pl.pallas_call(kernel, out_shape=(f32(N, N), f32(GROUPS, N), f32(8, N), f...  10.7 us
    unnamed x27, local copies, waits for them, and re-layouts  9.39 us
    pallas_call x1, Pallas kernels, run_join(): pl.pallas_call(join_kernel, out_shape=f32(HALF, ROWS, N), grid=(HALF // s...  5.74 us
    ppermute x3, starting transfers between devices, per_device(): lax.ppermute(duals, 'leg', [(i, (i + k) % 4) for i in range(4)])  5.68 us
  transfers between devices with their start and end apart: 7, of which 4 were waited for; matrix products, arithmetic and copies ran while one was open for 0% of the time, Pallas kernels for 2%

profile of v1, /device:TPU:1, one launch (start us, length us, event | category | flops | bytes accessed | tf_op | source)
XLA Modules:
  0.0 195.3 jit_solution(9921099975713314438)
XLA Ops:
  0.6 0.8 copy.14
  1.4 0.1 reshape.93.ids.refs_0_
  1.5 0.0 copy-start.4
  1.5 0.7 copy-done.4
  2.2 0.7 copy-done.6
  2.9 0.7 copy-done.11
  3.5 0.0 copy-start.12
  3.6 16.9 %gram.1 = (f32[64,64,128]{2,1,0:T(8,128)S(1)}, f32[64,64,128]{2,1,0:T(8,128)}, f32[128,8,128]{2,1,0:T(8,128)S(1)}, f32[16,128]{1,0:T(8,128)S(1)}) custom-call(s32[64]{0:T(128)S(1)} %reshape.93.ids.refs_0_, s32[16]{0:T(128)S(1)} %copy-done.11, s32[1]{0:T(128)} %bitcast.1.me, f32[16,4,128,128]{3,2,1,0:T(8,128)} %refs_2_.7, f32[16,128]{1,0:T(8,128)S(1)} %copy-done.4, ...), custom_call_target="tpu_custom_call" | custom-call | flops 1610612736 | bytes 12582912 | tf_op jit(solution)/shard_map/gram/pallas_call | solution.py:90
  20.5 1.5 collective-permute-start
  22.0 0.0 copy-done.8
  22.0 3.0 %collective-permute-start.2 = (f32[32,128]{1,0:T(8,128)S(1)}, f32[32,128]{1,0:T(8,128)S(1)}, u32[]{:S(2)}, u32[]{:S(2)}) collective-permute-start(f32[32,128]{1,0:T(8,128)S(1)} %copy-done.8), channel_id=1, source_target_pairs={{0,2},{1,3},{2,0},{3,1},{4,6},{5,7},{6,4},{7,5},{8,10},{9,11},{10,... | collective-permute-start | bytes 49160 | tf_op jit(solution)/shard_map/ppermute | solution.py:458
  25.0 0.4 collective-permute-start.1
  25.4 2.3 %collective-permute-start.3 = (f32[32,128]{1,0:T(8,128)S(1)}, f32[32,128]{1,0:T(8,128)S(1)}, u32[]{:S(2)}, u32[]{:S(2)}) collective-permute-start(f32[32,128]{1,0:T(8,128)S(1)} %copy-done.8), channel_id=1, source_target_pairs={{0,3},{1,0},{2,1},{3,2},{4,7},{5,4},{6,5},{7,6},{8,11},{9,8},{10,9... | collective-permute-start | bytes 49160 | tf_op jit(solution)/shard_map/ppermute | solution.py:458
  27.7 0.1 reshape_reshape.3.refs_1_
  27.8 0.0 collective-permute-done.2.refs_5_
  27.8 1.0 collective-permute-done.1.refs_4_
  28.8 0.0 collective-permute-done.3.refs_6_
  28.8 0.0 copy-done.5
  28.8 0.0 copy-done.7
  28.8 0.0 copy-done.10
  28.8 0.0 copy-done.12
  28.9 0.0 copy-start
  28.9 2.2 %copy-done = f32[16,4,128,128]{3,2,1,0:T(8,128)S(1)} copy-done((f32[16,4,128,128]{3,2,1,0:T(8,128)S(1)}, f32[16,4,128,128]{3,2,1,0:T(8,128)}, u32[]{:S(2)}) %copy-start) | copy-done | bytes 4194328
  31.0 4.9 %rhs.1 = (f32[128,8,128]{2,1,0:T(8,128)S(1)}, f32[16,128]{1,0:T(8,128)S(1)}) custom-call(s32[1,64]{1,0:T(1,128)S(1)} %get-tuple-element.57.ids_ref, s32[16]{0:T(128)S(1)} %copy-done.12, s32[1,64]{1,0:T(1,128)S(1)} %get-tuple-element.56.refs_1_, f32[16,4,128,128]{3,2,1,0:T(8,128)S(1)} %copy-done, f32[32,128]{1,0:T(8,128)S(1)} %copy-done.8, ...), custom_call_target="tpu_custom_call" | custom-call | flops 134217728 | bytes 6291456 | tf_op jit(solution)/shard_map/rhs/pallas_call | solution.py:191
  36.0 1.6 collective-permute-start.4
  37.6 1.2 collective-permute-done.4.small_got
  38.7 0.0 collective-permute-done.got
  38.7 5.7 %join.1 = f32[64,72,128]{2,1,0:T(8,128)} custom-call(f32[64,64,128]{2,1,0:T(8,128)S(1)} %get-tuple-element.29.own, f32[64,64,128]{2,1,0:T(8,128)} %collective-permute-done.got, f32[64,8,128]{2,1,0:T(8,128)S(1)} %get-tuple-element.55.small_own, f32[64,8,128]{2,1,0:T(8,128)S(1)} %collective-permute-done.4.small_got), custom_call_target="tpu_custom_call" | custom-call | tf_op jit(solution)/shard_map/join/pallas_call | solution.py:216
  44.5 11.3 %all-to-all-start = ((f32[64,72,128]{2,1,0:T(8,128)}), f32[64,72,128]{2,1,0:T(8,128)S(1)}, u32[]{:S(2)}, u32[]{:S(2)}) async-start(f32[64,72,128]{2,1,0:T(8,128)} %join.1), calls=%async_computation | async-start | bytes 4718592 | tf_op jit(solution)/shard_map/all_to_all | solution.py:445
  55.8 30.7 %all-to-all-done.got = f32[64,72,128]{2,1,0:T(8,128)S(1)} async-done(((f32[64,72,128]{2,1,0:T(8,128)}), f32[64,72,128]{2,1,0:T(8,128)S(1)}, u32[]{:S(2)}, u32[]{:S(2)}) %all-to-all-start) | async-done | bytes 2359328 | tf_op jit(solution)/shard_map/all_to_all | solution.py:445
  86.5 0.0 copy-done.9
  86.5 4.4 %first.1 = (f32[128,128]{1,0:T(8,128)S(1)}, f32[8,128]{1,0:T(8,128)S(1)}, f32[8,128]{1,0:T(8,128)S(1)}, f32[256,128]{1,0:T(8,128)S(1)}) custom-call(s32[1]{0:T(128)} %bitcast.3.me, f32[64,72,128]{2,1,0:T(8,128)S(1)} %all-to-all-done.got, f32[32,128]{1,0:T(8,128)S(1)} %copy-done.9), custom_call_target="tpu_custom_call" | custom-call | tf_op jit(solution)/shard_map/first/pallas_call | solution.py:321
  90.9 17.0 %all_to_all.71 = f32[128,2,128]{2,1,0:T(2,128)S(1)} all-to-all(f32[128,2,128]{2,1,0:T(2,128)S(1)} %bitcast.24), channel_id=1, replica_groups=mesh['x'=4,'z'=4,'core'=2,'leg'=4] {'leg','x','z','core'}, dimensions={0} | all-to-all | bytes 262144 | tf_op jit(solution)/shard_map/all_to_all | solution.py:445
  107.8 2.2 %copy-done.1 = f32[16,4,128,128]{3,2,1,0:T(8,128)S(1)} copy-done((f32[16,4,128,128]{3,2,1,0:T(8,128)S(1)}, f32[16,4,128,128]{3,2,1,0:T(8,128)}, u32[]{:S(2)}) %copy-start.1) | copy-done | bytes 4194328
  110.0 4.4 %tile.2 = (f32[128,128]{1,0:T(8,128)S(1)}, f32[16,128]{1,0:T(8,128)S(1)}, f32[8,128]{1,0:T(8,128)S(1)}, f32[256,128]{1,0:T(8,128)}) custom-call(s32[64]{0:T(128)S(1)} %reshape.93.ids.refs_0_, s32[1,64]{1,0:T(1,128)S(1)} %reshape_reshape.3.refs_1_, f32[16,4,128,128]{3,2,1,0:T(8,128)S(1)} %copy-done.1, f32[16,128]{1,0:T(8,128)S(1)} %get-tuple-element.28.refs_10_.refs_3_.scale, ...), custom_call_target="tpu_custom_call" | custom-call | tf_op jit(solution)/shard_map/tile/pallas_call | solution.py:401
  114.5 4.4 %all-to-all-start.2 = ((f32[128,2,128]{2,1,0:T(2,128)}), f32[128,2,128]{2,1,0:T(2,128)S(1)}, u32[]{:S(2)}, u32[]{:S(2)}) async-start(f32[128,2,128]{2,1,0:T(2,128)} %bitcast.6), calls=%async_computation.2 | async-start | bytes 262144 | tf_op jit(solution)/shard_map/all_to_all | solution.py:445
  118.9 9.9 %all-to-all-done.2 = f32[128,2,128]{2,1,0:T(2,128)S(1)} async-done(((f32[128,2,128]{2,1,0:T(2,128)}), f32[128,2,128]{2,1,0:T(2,128)S(1)}, u32[]{:S(2)}, u32[]{:S(2)}) %all-to-all-start.2) | async-done | bytes 131104 | tf_op jit(solution)/shard_map/all_to_all | solution.py:445
  128.8 0.4 owner.2
  129.2 14.1 %all_to_all.72 = f32[128,2,128]{2,1,0:T(2,128)S(1)} all-to-all(f32[128,2,128]{2,1,0:T(2,128)S(1)} %bitcast.27), channel_id=1, replica_groups=mesh['x'=4,'z'=4,'core'=2,'leg'=4] {'leg','x','z','core'}, dimensions={0} | all-to-all | bytes 262144 | tf_op jit(solution)/shard_map/all_to_all | solution.py:445
  143.2 2.2 %copy-done.2 = f32[16,4,128,128]{3,2,1,0:T(8,128)S(1)} copy-done((f32[16,4,128,128]{3,2,1,0:T(8,128)S(1)}, f32[16,4,128,128]{3,2,1,0:T(8,128)}, u32[]{:S(2)}) %copy-start.2) | copy-done | bytes 4194328
  145.4 3.8 %tile.3 = (f32[128,128]{1,0:T(8,128)S(1)}, f32[16,128]{1,0:T(8,128)S(1)}, f32[8,128]{1,0:T(8,128)S(1)}, f32[256,128]{1,0:T(8,128)S(1)}) custom-call(s32[64]{0:T(128)S(1)} %reshape.93.ids.refs_0_, s32[1,64]{1,0:T(1,128)S(1)} %reshape_reshape.3.refs_1_, f32[16,4,128,128]{3,2,1,0:T(8,128)S(1)} %copy-done.2, ...), custom_call_target="tpu_custom_call" | custom-call | tf_op jit(solution)/shard_map/tile/pallas_call | solution.py:401
  149.2 14.2 %all_to_all.73 = f32[128,2,128]{2,1,0:T(2,128)S(1)} all-to-all(f32[128,2,128]{2,1,0:T(2,128)S(1)} %bitcast.25), channel_id=1, replica_groups=mesh['x'=4,'z'=4,'core'=2,'leg'=4] {'leg','x','z','core'}, dimensions={0} | all-to-all | bytes 262144 | tf_op jit(solution)/shard_map/all_to_all | solution.py:445
  163.4 0.4 owner.3
  163.8 14.2 %all_to_all.74 = f32[128,2,128]{2,1,0:T(2,128)S(1)} all-to-all(f32[128,2,128]{2,1,0:T(2,128)S(1)} %bitcast.26), channel_id=1, replica_groups=mesh['x'=4,'z'=4,'core'=2,'leg'=4] {'leg','x','z','core'}, dimensions={0} | all-to-all | bytes 262144 | tf_op jit(solution)/shard_map/all_to_all | solution.py:445
  178.0 0.0 copy-done.3
  178.0 2.4 %tile_last.1 = (f32[128,128]{1,0:T(8,128)S(1)}, f32[16,128]{1,0:T(8,128)S(1)}, f32[8,128]{1,0:T(8,128)S(1)}, f32[128,128]{1,0:T(8,128)S(1)}) custom-call(s32[64]{0:T(128)S(1)} %reshape.93.ids.refs_0_, s32[1,64]{1,0:T(1,128)S(1)} %reshape_reshape.3.refs_1_, f32[16,4,128,128]{3,2,1,0:T(8,128)S(1)} %copy-done.3, ...), custom_call_target="tpu_custom_call" | custom-call | tf_op jit(solution)/shard_map/tile_last/pallas_call | solution.py:401
  180.4 13.6 %all_to_all.75 = f32[128,1,128]{2,1,0:T(1,128)S(1)} all-to-all(f32[128,1,128]{2,1,0:T(1,128)S(1)} %bitcast.28), channel_id=1, replica_groups=mesh['x'=4,'z'=4,'core'=2,'leg'=4] {'leg','x','z','core'}, dimensions={0} | all-to-all | bytes 131072 | tf_op jit(solution)/shard_map/all_to_all | solution.py:445
  194.0 1.3 final.1
  (12 shorter events, 0.1 us)
Async XLA Ops:
  1.5 0.7 copy-start.4
  2.2 0.7 copy-start.6
  2.9 0.7 copy-start.11
  3.5 18.5 %copy-start.8 = (f32[32,128]{1,0:T(8,128)S(1)}, f32[32,128]{1,0:T(8,128)}, u32[]{:S(2)}) copy-start(f32[32,128]{1,0:T(8,128)} %refs_3_.1) | copy-start | bytes 49156
  3.5 25.3 %copy-start.5 = (f32[16,128]{1,0:T(8,128)S(1)}, f32[16,128]{1,0:T(8,128)}, u32[]{:S(2)}) copy-start(f32[16,128]{1,0:T(8,128)} %primal.3) | copy-start | bytes 24580
  3.5 25.3 %copy-start.7 = (f32[16,128]{1,0:T(8,128)S(1)}, f32[16,128]{1,0:T(8,128)}, u32[]{:S(2)}) copy-start(f32[16,128]{1,0:T(8,128)} %slack.3) | copy-start | bytes 24580
  3.5 25.3 %copy-start.10 = (f32[16,128]{1,0:T(8,128)S(1)}, f32[16,128]{1,0:T(8,128)}, u32[]{:S(2)}) copy-start(f32[16,128]{1,0:T(8,128)} %refs_9_.1) | copy-start | bytes 24580
  3.5 25.3 %copy-start.12 = (s32[16]{0:T(128)S(1)}, s32[16]{0:T(128)}, u32[]{:S(2)}) copy-start(s32[16]{0:T(128)} %counts.3) | copy-start | bytes 196
  20.5 18.2 %collective-permute-start = (f32[64,64,128]{2,1,0:T(8,128)}, f32[64,64,128]{2,1,0:T(8,128)}, u32[]{:S(2)}, u32[]{:S(2)}) collective-permute-start(f32[64,64,128]{2,1,0:T(8,128)} %get-tuple-element.30), channel_id=1, source_target_pairs={{0,4},{4,0},{1,5},{5,1},{2,6},{6,2},{3,7},{7,3},{8,12},{12,8},{9,1... | collective-permute-start | bytes 6291464 | tf_op jit(solution)/shard_map/ppermute | solution.py:464
  22.0 5.8 %collective-permute-start.2 = (f32[32,128]{1,0:T(8,128)S(1)}, f32[32,128]{1,0:T(8,128)S(1)}, u32[]{:S(2)}, u32[]{:S(2)}) collective-permute-start(f32[32,128]{1,0:T(8,128)S(1)} %copy-done.8), channel_id=1, source_target_pairs={{0,2},{1,3},{2,0},{3,1},{4,6},{5,7},{6,4},{7,5},{8,10},{9,11},{10,... | collective-permute-start | bytes 49160 | tf_op jit(solution)/shard_map/ppermute | solution.py:458
  25.0 3.8 %collective-permute-start.1 = (f32[32,128]{1,0:T(8,128)S(1)}, f32[32,128]{1,0:T(8,128)S(1)}, u32[]{:S(2)}, u32[]{:S(2)}) collective-permute-start(f32[32,128]{1,0:T(8,128)S(1)} %copy-done.8), channel_id=1, source_target_pairs={{0,1},{1,2},{2,3},{3,0},{4,5},{5,6},{6,7},{7,4},{8,9},{9,10},{10,1... | collective-permute-start | bytes 49160 | tf_op jit(solution)/shard_map/ppermute | solution.py:458
  25.4 3.4 %collective-permute-start.3 = (f32[32,128]{1,0:T(8,128)S(1)}, f32[32,128]{1,0:T(8,128)S(1)}, u32[]{:S(2)}, u32[]{:S(2)}) collective-permute-start(f32[32,128]{1,0:T(8,128)S(1)} %copy-done.8), channel_id=1, source_target_pairs={{0,3},{1,0},{2,1},{3,2},{4,7},{5,4},{6,5},{7,6},{8,11},{9,8},{10,9... | collective-permute-start | bytes 49160 | tf_op jit(solution)/shard_map/ppermute | solution.py:458
  28.9 2.2 %copy-start = (f32[16,4,128,128]{3,2,1,0:T(8,128)S(1)}, f32[16,4,128,128]{3,2,1,0:T(8,128)}, u32[]{:S(2)}) copy-start(f32[16,4,128,128]{3,2,1,0:T(8,128)} %refs_2_.7) | copy-start | bytes 12582916
  36.0 2.8 %collective-permute-start.4 = (f32[64,8,128]{2,1,0:T(8,128)S(1)}, f32[64,8,128]{2,1,0:T(8,128)S(1)}, u32[]{:S(2)}, u32[]{:S(2)}) collective-permute-start(f32[64,8,128]{2,1,0:T(8,128)S(1)} %get-tuple-element.54), channel_id=1, source_target_pairs={{0,4},{4,0},{1,5},{5,1},{2,6},{6,2},{3,7},{7,3},{8,12},{12,8},{9,1... | collective-permute-start | bytes 786440 | tf_op jit(solution)/shard_map/ppermute | solution.py:469
  44.5 42.0 %copy-start.9 = (f32[32,128]{1,0:T(8,128)S(1)}, f32[32,128]{1,0:T(8,128)}, u32[]{:S(2)}) copy-start(f32[32,128]{1,0:T(8,128)} %demand.1) | copy-start | bytes 49156
  44.5 42.0 %all-to-all-start = ((f32[64,72,128]{2,1,0:T(8,128)}), f32[64,72,128]{2,1,0:T(8,128)S(1)}, u32[]{:S(2)}, u32[]{:S(2)}) async-start(f32[64,72,128]{2,1,0:T(8,128)} %join.1), calls=%async_computation | async-start | bytes 4718592 | tf_op jit(solution)/shard_map/all_to_all | solution.py:445
  107.8 2.2 %copy-start.1 = (f32[16,4,128,128]{3,2,1,0:T(8,128)S(1)}, f32[16,4,128,128]{3,2,1,0:T(8,128)}, u32[]{:S(2)}) copy-start(f32[16,4,128,128]{3,2,1,0:T(8,128)} %refs_2_.7) | copy-start | bytes 12582916
  114.5 14.3 %all-to-all-start.2 = ((f32[128,2,128]{2,1,0:T(2,128)}), f32[128,2,128]{2,1,0:T(2,128)S(1)}, u32[]{:S(2)}, u32[]{:S(2)}) async-start(f32[128,2,128]{2,1,0:T(2,128)} %bitcast.6), calls=%async_computation.2 | async-start | bytes 262144 | tf_op jit(solution)/shard_map/all_to_all | solution.py:445
  143.2 2.2 %copy-start.2 = (f32[16,4,128,128]{3,2,1,0:T(8,128)S(1)}, f32[16,4,128,128]{3,2,1,0:T(8,128)}, u32[]{:S(2)}) copy-start(f32[16,4,128,128]{3,2,1,0:T(8,128)} %refs_2_.7) | copy-start | bytes 12582916
  145.4 32.5 %copy-start.3 = (f32[16,4,128,128]{3,2,1,0:T(8,128)S(1)}, f32[16,4,128,128]{3,2,1,0:T(8,128)}, u32[]{:S(2)}) copy-start(f32[16,4,128,128]{3,2,1,0:T(8,128)} %refs_2_.7) | copy-start | bytes 12582916

commit v2 on v1

v2 whole, which is shorter than its diff:
```python
import jax
import jax.numpy as jnp
from jax import lax
from jax.experimental import pallas as pl
from jax.experimental.pallas import tpu as pltpu
from jax.sharding import Mesh, PartitionSpec as P

ITERS = 3
SIGMA = 0.3
REGULAR = 1.0
PRECISE = lax.Precision.HIGHEST

N = 128
HALF = 64
SPAN = 4
GROUPS = 16
TILES = GROUPS * SPAN
EXTRA = 8
ROWS = HALF + EXTRA

VMEM = pltpu.MemorySpace.VMEM
SMEM = pltpu.MemorySpace.SMEM
HBM = pltpu.MemorySpace.HBM
NT = (((1,), (1,)), ((), ()))


def iota(shape, axis):
    return lax.broadcasted_iota(jnp.int32, shape, axis)


def vspec():
    return pl.BlockSpec(memory_space=VMEM)


def sspec():
    return pl.BlockSpec(memory_space=SMEM)


def f32(*shape):
    return jax.ShapeDtypeStruct(shape, jnp.float32)


def device_col():
    return (lax.axis_index("x") * 4 + lax.axis_index("z")) * 2 + lax.axis_index("core")


def params():
    return pltpu.CompilerParams(vmem_limit_bytes=24 << 20)


def split(x):
    high = x.astype(jnp.bfloat16)
    return high, (x - high.astype(jnp.float32)).astype(jnp.bfloat16)


def gram_product(tile, root):
    high, low = split(tile * root)
    both = lax.dot_general(high, high, NT, preferred_element_type=jnp.float32)
    cross = lax.dot_general(
        jnp.concatenate([high, low], axis=1),
        jnp.concatenate([low, high], axis=1),
        NT,
        preferred_element_type=jnp.float32,
    )
    return both + cross


UNROLL = 4


def gram_kernel(
    coeffs_in, ids_in, counts_in, primal_in, slack_in, coeffs, acc, other, small, scale_out,
    hot_ids, hot_place, ids, counts, primal, slack, hot, hot2, sem, tile_sem,
):
    little = [
        pltpu.make_async_copy(ids_in, ids, sem.at[0]),
        pltpu.make_async_copy(counts_in, counts, sem.at[1]),
        pltpu.make_async_copy(primal_in, primal, sem.at[2]),
        pltpu.make_async_copy(slack_in, slack, sem.at[3]),
    ]
    for copy in little:
        copy.start()
    for g in range(GROUPS):
        pltpu.make_async_copy(coeffs_in.at[g], coeffs.at[g], tile_sem.at[g]).start()
    acc[...] = jnp.zeros_like(acc)
    small[...] = jnp.zeros_like(small)
    hot[...] = jnp.zeros_like(hot)
    hot2[...] = jnp.zeros_like(hot2)
    core = lax.axis_index("core")
    for copy in little:
        copy.wait()
    row = iota((HALF, N), 0)
    lane = iota((HALF, N), 1)
    line_lane = iota((1, N), 1)
    lower = jnp.logical_or(row >= lane, lane >= HALF)

    def group(g):
        pltpu.make_async_copy(coeffs_in.at[g], coeffs.at[g], tile_sem.at[g]).wait()
        valid = line_lane < counts[g]
        scale = jnp.where(valid, primal[pl.ds(g, 1), :] / slack[pl.ds(g, 1), :], 0.0)
        scale_out[pl.ds(g, 1), :] = scale
        root = jnp.sqrt(scale)
        for s in range(SPAN):
            gram = gram_product(coeffs[g, s], root)
            rolled = pltpu.roll(gram[HALF:], HALF, 1)
            packed = jnp.where(lower, gram[:HALF], rolled)
            line = jnp.sum(jnp.where(row == lane, rolled, 0.0), axis=0, keepdims=True)
            block = ids[s, g]
            place = ((block & 1) ^ core) * HALF + (block >> 1)
            acc[place] += packed
            small[place, 0:1, :] += line
            t = g * SPAN + s
            hot[pl.ds(t, 1), :] = (line_lane == block).astype(jnp.float32)
            hot2[pl.ds(t, 1), :] = (line_lane == place).astype(jnp.float32)

    @pl.loop(0, GROUPS // UNROLL)
    def _(i):
        for k in range(UNROLL):
            group(i * UNROLL + k)

    other[...] = acc[pl.ds(HALF, HALF)]
    hot_ids[...] = jnp.transpose(hot[...]).astype(jnp.bfloat16)
    hot_place[...] = jnp.transpose(hot2[...]).astype(jnp.bfloat16)


def run_gram(coeffs, ids, counts, primal, slack):
    return pl.pallas_call(
        gram_kernel,
        out_shape=(
            f32(GROUPS, SPAN, N, N),
            f32(N, HALF, N),
            f32(HALF, HALF, N),
            f32(N, EXTRA, N),
            f32(GROUPS, N),
            jax.ShapeDtypeStruct((N, N), jnp.bfloat16),
            jax.ShapeDtypeStruct((N, N), jnp.bfloat16),
        ),
        in_specs=[pl.BlockSpec(memory_space=HBM)] * 5,
        out_specs=(vspec(),) * 7,
        scratch_shapes=[
            pltpu.SMEM((SPAN, GROUPS), jnp.int32),
            pltpu.SMEM((GROUPS,), jnp.int32),
            pltpu.VMEM((GROUPS, N), jnp.float32),
            pltpu.VMEM((GROUPS, N), jnp.float32),
            pltpu.VMEM((N, N), jnp.float32),
            pltpu.VMEM((N, N), jnp.float32),
            pltpu.SemaphoreType.DMA((4,)),
            pltpu.SemaphoreType.DMA((GROUPS,)),
        ],
        compiler_params=params(),
        cost_estimate=pl.CostEstimate(
            flops=TILES * 2 * N**3 * 3, bytes_accessed=12 << 20, transcendentals=0
        ),
        name="gram",
    )(*(pltpu.with_memory_space_constraint(x, HBM) for x in (coeffs, ids, counts, primal, slack)))


def transpose_apply(ids, coeffs, vector, spread):
    for t in range(TILES):
        spread[pl.ds(t, 1), :] = vector[pl.ds(ids[t % SPAN, t // SPAN], 1), :]
    columns = jnp.transpose(spread[...])
    lines = []
    for g in range(GROUPS):
        total = None
        for s in range(SPAN):
            t = g * SPAN + s
            prod = coeffs[g, s] * jnp.broadcast_to(columns[:, t : t + 1], (N, N))
            part = jnp.sum(prod.reshape(N // 8, 8, N), axis=0)
            total = part if total is None else total + part
        lines.append(jnp.sum(total, axis=0, keepdims=True))
    return jnp.concatenate(lines, axis=0)


def forward_apply(coeffs, colvec):
    lane = iota((N, N), 1)
    columns = jnp.zeros((N, N), jnp.float32)
    for g in range(GROUPS):
        w = colvec[g : g + 1, :]
        for s in range(SPAN):
            t = g * SPAN + s
            total = jnp.sum(coeffs[g, s] * w, axis=1, keepdims=True)
            columns = jnp.where(lane == t, total, columns)
    return jnp.transpose(columns)[:TILES]


def place_rows(hot, rows):
    rows = jnp.concatenate([rows, jnp.zeros((N - TILES, N), jnp.float32)], axis=0)
    high, rest = rows.astype(jnp.bfloat16), None
    rest = rows - high.astype(jnp.float32)
    middle, low = split(rest)
    total = jnp.dot(hot, high, preferred_element_type=jnp.float32)
    total = total + jnp.dot(hot, middle, preferred_element_type=jnp.float32)
    return total + jnp.dot(hot, low, preferred_element_type=jnp.float32)


def rhs_kernel(
    ids, counts, hot_place, coeffs, dual0, dual1, dual2, dual3, primal, slack, cost, scale, small,
    own_out, other_out, dual_res_out, spread, duals, valid_s,
):
    leg = lax.axis_index("leg")
    for k, part in enumerate((dual0, dual1, dual2, dual3)):
        at = pl.multiple_of(((leg - k) & 3) * 32, 32)
        duals[pl.ds(at, 32), :] = part[...]
    for g in range(GROUPS):
        valid_s[pl.ds(g, 1), :] = (iota((1, N), 1) < counts[g]).astype(jnp.float32)
    valid = valid_s[...]
    dual_res = cost[...] - valid * transpose_apply(ids, coeffs, duals, spread) - slack[...]
    dual_res_out[...] = dual_res
    first = place_rows(hot_place[...], forward_apply(coeffs, scale[...] * dual_res))
    second = place_rows(hot_place[...], forward_apply(coeffs, valid / slack[...]))
    comp = jnp.sum(valid * primal[...] * slack[...], axis=0, keepdims=True)
    used = jnp.sum(valid, axis=0, keepdims=True)
    for k, out in enumerate((own_out, other_out)):
        half = slice(k * HALF, k * HALF + HALF)
        out[:, 0:1, :] = small[half, 0:1, :]
        out[:, 1:2, :] = first[half].reshape(HALF, 1, N)
        out[:, 2:3, :] = second[half].reshape(HALF, 1, N)
        out[:, 3:4, :] = jnp.broadcast_to(comp.reshape(1, 1, N), (HALF, 1, N))
        out[:, 4:5, :] = jnp.broadcast_to(used.reshape(1, 1, N), (HALF, 1, N))
        out[:, 5:8, :] = jnp.zeros((HALF, 3, N), jnp.float32)


def run_rhs(ids, counts, hot_place, coeffs, duals, primal, slack, cost, scale, small):
    return pl.pallas_call(
        rhs_kernel,
        out_shape=(f32(HALF, EXTRA, N), f32(HALF, EXTRA, N), f32(GROUPS, N)),
        in_specs=[sspec(), sspec()] + [vspec()] * 11,
        out_specs=(vspec(),) * 3,
        scratch_shapes=[
            pltpu.VMEM((TILES, N), jnp.float32),
            pltpu.VMEM((N, N), jnp.float32),
            pltpu.VMEM((GROUPS, N), jnp.float32),
        ],
        compiler_params=params(),
        cost_estimate=pl.CostEstimate(flops=1 << 27, bytes_accessed=6 << 20, transcendentals=0),
        name="rhs",
    )(ids, counts, hot_place, coeffs, *duals, primal, slack, cost, scale, small)


def join_kernel(acc, got, small, small_got, out):
    out[:, 0:HALF, :] = acc[pl.ds(0, HALF)] + got[...]
    out[:, HALF:ROWS, :] = small[...] + small_got[...]


def run_join(acc, got, small, small_got):
    return pl.pallas_call(
        join_kernel,
        out_shape=f32(HALF, ROWS, N),
        in_specs=[vspec()] * 4,
        out_specs=vspec(),
        compiler_params=params(),
        name="join",
    )(acc, got, small, small_got)


def small_inverse(cols):
    cols = list(cols)
    sub = iota((8, N), 0)
    for m in range(8):
        rows = [jnp.broadcast_to(c[m : m + 1, :], (8, N)) for c in cols]
        inv = 1.0 / rows[m]
        factor = cols[m]
        here = sub == m
        for j in range(8):
            if j == m:
                cols[j] = jnp.where(here, inv, -factor * inv)
            else:
                scaled = rows[j] * inv
                cols[j] = jnp.where(here, scaled, cols[j] - factor * scaled)
    return cols


def invert(panels):
    panels = list(panels)
    lane = iota((8, N), 1)
    count = len(panels)
    for k in range(count):
        mine = jnp.logical_and(lane >= 8 * k, lane < 8 * k + 8)
        pivot = panels[k]
        cols = [jnp.broadcast_to(pivot[:, 8 * k + m : 8 * k + m + 1], (8, N)) for m in range(8)]
        cols = small_inverse(cols)
        total = None
        for m in range(8):
            term = cols[m] * jnp.broadcast_to(pivot[m : m + 1, :], (8, N))
            total = term if total is None else total + term
        for m in range(8):
            total = jnp.where(lane == 8 * k + m, cols[m], total)
        rows = [jnp.broadcast_to(total[m : m + 1, :], (8, N)) for m in range(8)]
        for step in range(1, count):
            i = (k + step) % count
            old = panels[i]
            new = jnp.where(mine, 0.0, old)
            for m in range(8):
                col = jnp.broadcast_to(old[:, 8 * k + m : 8 * k + m + 1], (8, N))
                new = new - col * rows[m]
            panels[i] = new
        panels[k] = total
    return panels


def pair_rows(first, second):
    return jnp.where((iota((8, N), 0) & 1) == 0, first, second)


def set_message(msg, line, scalar):
    pair = pair_rows(jnp.broadcast_to(line, (8, N)), jnp.broadcast_to(scalar, (8, N)))
    msg[...] = jnp.broadcast_to(pair[None], (N // 4, 8, N)).reshape(2 * N, N)


def first_kernel(got, demand, inverse_out, residual_out, mu_out, msg):
    def add(i, carry):
        return carry + got[i]

    total = lax.fori_loop(1, HALF, add, got[0], unroll=7)
    packed = total[:HALF]
    line = total[HALF : HALF + 1]
    tail = total[HALF:]
    comp = jnp.sum(tail[3:4], axis=1, keepdims=True)
    used = jnp.sum(tail[4:5], axis=1, keepdims=True)
    mu = SIGMA * (comp / used)
    mu_out[...] = jnp.broadcast_to(mu, (8, N))
    residual = demand[pl.ds(device_col(), 1), :] + tail[1:2] - mu * tail[2:3]
    residual_out[...] = jnp.broadcast_to(residual, (8, N))

    row = iota((HALF, N), 0)
    lane = iota((HALF, N), 1)
    flipped = jnp.transpose(jnp.concatenate([packed, jnp.zeros((HALF, N), jnp.float32)], axis=0))
    flip_top, flip_bottom = flipped[:HALF], flipped[HALF:]
    top = jnp.where(jnp.logical_or(row >= lane, lane >= HALF), packed, flip_top)
    corner = jnp.where(row < lane, packed, flip_top)
    corner = jnp.where(row == lane, jnp.broadcast_to(line, (HALF, N)), corner)
    bottom = jnp.where(lane < HALF, flip_bottom, pltpu.roll(corner, HALF, 1))
    top = top + jnp.where(row == lane, REGULAR, 0.0)
    bottom = bottom + jnp.where(row + HALF == lane, REGULAR, 0.0)
    panels = [top[8 * i : 8 * i + 8] for i in range(8)]
    panels += [bottom[8 * i : 8 * i + 8] for i in range(8)]
    inverse = jnp.concatenate(invert(panels), axis=0)
    inverse_out[...] = inverse
    smoothed = jnp.dot(
        jnp.broadcast_to(residual, (8, N)),
        inverse,
        precision=PRECISE,
        preferred_element_type=jnp.float32,
    )[0:1]
    norm = jnp.sum(residual * smoothed, axis=1, keepdims=True)
    set_message(msg, smoothed, norm)


def run_first(got, demand):
    return pl.pallas_call(
        first_kernel,
        out_shape=(f32(N, N), f32(8, N), f32(8, N), f32(2 * N, N)),
        in_specs=[vspec(), vspec()],
        out_specs=(vspec(),) * 4,
        compiler_params=params(),
        name="first",
    )(got, demand)


def sum_pairs(got):
    total = jnp.sum(got[...].reshape(N // 4, 8, N), axis=0)
    even = (total[0:1] + total[2:3]) + (total[4:5] + total[6:7])
    odd = (total[1:2] + total[3:4]) + (total[5:6] + total[7:8])
    return even, odd


def owner_kernel(got, direction, norms, residual, inverse, residual_out, msg):
    image, curve = sum_pairs(got)
    image = image + REGULAR * direction[pl.ds(lax.axis_index("leg") * 32 + device_col(), 1), :]
    curve = jnp.sum(curve, axis=1, keepdims=True)
    step_len = norms[0:1, :] / (curve + norms[1:2, :])
    new = residual[0:1, :] - step_len * image
    residual_out[...] = pair_rows(jnp.broadcast_to(new, (8, N)), jnp.broadcast_to(curve, (8, N)))
    smoothed = jnp.dot(
        jnp.broadcast_to(new, (8, N)),
        inverse[...],
        precision=PRECISE,
        preferred_element_type=jnp.float32,
    )[0:1]
    set_message(msg, smoothed, jnp.sum(new * smoothed, axis=1, keepdims=True))


def run_owner(got, direction, norms, residual, inverse):
    return pl.pallas_call(
        owner_kernel,
        out_shape=(f32(8, N), f32(2 * N, N)),
        in_specs=[vspec()] * 5,
        out_specs=(vspec(),) * 2,
        compiler_params=params(),
        name="owner",
    )(got, direction, norms, residual, inverse)


def tile_kernel(last, begin, ids, hot, coeffs, scale, got, *refs):
    if begin:
        direction_out, applied_out, norms_out, msg, spread = refs
    else:
        direction_in, norms_in, direction_out, applied_out, norms_out, msg, spread = refs
    smoothed = got[pl.ds(0, N, stride=2), :]
    norm = jnp.sum(got[pl.ds(1, N, stride=2), :], axis=0, keepdims=True)
    if begin:
        direction = smoothed
    else:
        direction = smoothed + (norm / norms_in[0:1, :]) * direction_in[...]
    direction_out[...] = direction
    square = jnp.sum(jnp.sum(direction * direction, axis=0, keepdims=True), axis=1, keepdims=True)
    square = jnp.broadcast_to(REGULAR * square, (1, N))
    norms_out[0:1, :] = norm
    norms_out[1:2, :] = square
    applied = transpose_apply(ids, coeffs, direction_out, spread)
    applied_out[...] = applied
    weighted = scale[...] * applied
    curve = jnp.sum(weighted * applied, axis=0, keepdims=True)
    if last:
        msg[...] = jnp.broadcast_to(curve, (N, N))
    else:
        image = place_rows(hot[...], forward_apply(coeffs, weighted))
        msg[pl.ds(0, N, stride=2), :] = image
        msg[pl.ds(1, N, stride=2), :] = jnp.broadcast_to(curve, (N, N))


def run_tile(last, ids, hot, coeffs, scale, got, direction=None, norms=None):
    begin = direction is None
    extra = () if begin else (direction, norms)

    def kernel(*refs):
        tile_kernel(last, begin, *refs)

    return pl.pallas_call(
        kernel,
        out_shape=(f32(N, N), f32(GROUPS, N), f32(8, N), f32(N if last else 2 * N, N)),
        in_specs=[sspec()] + [vspec()] * (4 + len(extra)),
        out_specs=(vspec(),) * 4,
        scratch_shapes=[pltpu.VMEM((TILES, N), jnp.float32)],
        compiler_params=params(),
        name="tile_last" if last else "tile",
    )(ids, hot, coeffs, scale, got, *extra)


def final_kernel(
    counts, got, curve0, curve1, d0, d1, d2, u0, u1, u2, n0, n1, n2, mu, primal, slack,
    scale, dual_res, step_dual, step_primal,
):
    curve2 = jnp.sum(jnp.sum(got[...], axis=0, keepdims=True), axis=1, keepdims=True)
    lens = []
    for curve, norms in ((curve0[1:2, :], n0), (curve1[1:2, :], n1), (curve2, n2)):
        lens.append(norms[0:1, :] / (curve + norms[1:2, :]))
    at = pl.ds(pl.multiple_of(lax.axis_index("leg") * 32, 32), 32)
    step_dual[...] = lens[0] * d0[at, :] + lens[1] * d1[at, :] + lens[2] * d2[at, :]
    applied = lens[0] * u0[...] + lens[1] * u1[...] + lens[2] * u2[...]
    inner = scale[...] * (applied - dual_res[...]) + (mu[0:1, :] / slack[...] - primal[...])
    for g in range(GROUPS):
        valid = iota((1, N), 1) < counts[g]
        step_primal[g : g + 1, :] = jnp.where(valid, inner[g : g + 1, :], 0.0)


def run_final(counts, *args):
    return pl.pallas_call(
        final_kernel,
        out_shape=(f32(32, N), f32(GROUPS, N)),
        in_specs=[sspec()] + [vspec()] * len(args),
        out_specs=(vspec(), vspec()),
        compiler_params=params(),
        name="final",
    )(counts, *args)


ALL = ("leg", "x", "z", "core")
CHIPS = ("leg", "x", "z")


def exchange(rows, axes):
    return lax.all_to_all(rows, axes, split_axis=0, concat_axis=0, tiled=True)


def per_device(coeffs, block_ids, col_counts, primal, slack, cost, duals, demand):
    ids = block_ids.T
    parts = [duals]
    for k in (1, 2, 3):
        parts.append(lax.ppermute(duals, "leg", [(i, (i + k) % 4) for i in range(4)]))

    tiles, acc, other, small, scale, hot, hot_place = run_gram(
        coeffs, ids, col_counts, primal, slack
    )
    swap = [(0, 1), (1, 0)]
    got_big = lax.ppermute(other, "core", swap)
    small, small_other, dual_res = run_rhs(
        ids, col_counts, hot_place, tiles, parts, primal, slack, cost, scale, small
    )
    got_small = lax.ppermute(small_other, "core", swap)
    joined = run_join(acc, got_big, small, got_small)
    blocks = exchange(joined, CHIPS)
    inverse, residual, mu, msg = run_first(blocks, demand)

    direction = norms = None
    kept = []
    curves = []
    for turn in range(ITERS):
        got = exchange(msg, ALL)
        last = turn + 1 == ITERS
        direction, applied, norms, msg = run_tile(
            last, ids, hot, tiles, scale, got, direction, norms
        )
        kept.append((direction, applied, norms))
        got = exchange(msg, ALL)
        if not last:
            residual, msg = run_owner(got, direction, norms, residual, inverse)
            curves.append(residual)
    (d0, u0, n0), (d1, u1, n1), (d2, u2, n2) = kept
    return run_final(
        col_counts, got, curves[0], curves[1], d0, d1, d2, u0, u1, u2, n0, n1, n2, mu, primal,
        slack, scale, dual_res,
    )


def solution(mesh):
    fine = Mesh(mesh.devices.reshape(4, 4, 2, 4), ("x", "z", "core", "leg"))
    every = ("x", "z", "core", "leg")
    return jax.shard_map(
        per_device,
        mesh=fine,
        in_specs=(
            P(every, None, None, None),
            P(every, None),
            P(every),
            P(every, None),
            P(every, None),
            P(every, None),
            P("leg", None),
            P("leg", None),
        ),
        out_specs=(P("leg", None), P(every, None)),
        check_vma=False,
    )
```

time: 196 us -> 171 us (0.87)
  blocking collectives: 73 us -> 129 us
  waiting for transfers between devices: 42.8 us -> 2.29 us
  starting transfers between devices: 24.5 us -> 8.78 us
  Pallas kernels: 44.6 us -> 29.7 us
  local copies, waits for them, and re-layouts: 9.59 us -> 0.03 us
    all_to_all x5 -> x7, blocking collectives: 73 us -> 129 us  [exchange(): return lax.all_to_all(rows, axes, split_axis=0, concat_axis=0, tiled=True)]
    all_to_all x2 -> x0, waiting for transfers between devices: 40.6 us -> none  [exchange(): return lax.all_to_all(rows, axes, split_axis=0, concat_axis=0, tiled=True)]
    all_to_all x2 -> x0, starting transfers between devices: 15.7 us -> none  [exchange(): return lax.all_to_all(rows, axes, split_axis=0, concat_axis=0, tiled=True)]
    pallas_call x3, Pallas kernels: 27.5 us -> 13.8 us  [the longest x1 8.74 us: run_gram(): pl.pallas_call(gram_kernel, out_shape=(f32(GROUPS, SPAN, N, N), f32(N, HA...]
    unnamed x27 -> x14, local copies, waits for them, and re-layouts: 9.39 us -> 0.03 us
  transfers between devices with their start and end apart: 7 -> 5, of which waited for: 4 -> 2; matrix products, arithmetic and copies ran while one was open for 0% -> 0% of each run, Pallas kernels for 2% -> 3%
where the time goes in v2:
time: 171 us; the launch traced here: 170 us
  blocking collectives  129 us (75%)
  Pallas kernels  29.7 us (17%)
  starting transfers between devices  8.78 us (5%)
  waiting for transfers between devices  2.29 us (1%)
    all_to_all x7, blocking collectives, exchange(): return lax.all_to_all(rows, axes, split_axis=0, concat_axis=0, tiled=True)  129 us
    pallas_call x3, Pallas kernels, run_tile(): pl.pallas_call(kernel, out_shape=(f32(N, N), f32(GROUPS, N), f32(8, N), f...  9.57 us
    pallas_call x1, Pallas kernels, run_gram(): pl.pallas_call(gram_kernel, out_shape=(f32(GROUPS, SPAN, N, N), f32(N, HA...  8.74 us
    ppermute x3, starting transfers between devices, per_device(): lax.ppermute(duals, 'leg', [(i, (i + k) % 4) for i in range(4)])  5.69 us
    pallas_call x1, Pallas kernels, run_rhs(): pl.pallas_call(rhs_kernel, out_shape=(f32(HALF, EXTRA, N), f32(HALF, EXTR...  4.83 us
    pallas_call x1, Pallas kernels, run_first(): pl.pallas_call(first_kernel, out_shape=(f32(N, N), f32(8, N), f32(8, N),...  4.38 us
  transfers between devices with their start and end apart: 5, of which 2 were waited for; matrix products, arithmetic and copies ran while one was open for 0% of the time, Pallas kernels for 3%

profile of v2, /device:TPU:1, one launch (start us, length us, event | category | flops | bytes accessed | tf_op | source)
XLA Modules:
  0.0 170.5 jit_solution(4550530200853825512)
XLA Ops:
  0.6 0.0 copy-start.1
  0.6 0.0 copy-start
  0.7 0.0 copy-start.6
  0.7 0.0 copy-start.2
  0.7 0.0 copy-start.3
  0.7 0.0 copy-start.5
  0.7 8.7 %gram.1 = (f32[16,4,128,128]{3,2,1,0:T(8,128)S(1)}, f32[128,64,128]{2,1,0:T(8,128)S(1)}, f32[64,64,128]{2,1,0:T(8,128)S(1)}, f32[128,8,128]{2,1,0:T(8,128)S(1)},...) custom-call(f32[16,4,128,128]{3,2,1,0:T(8,128)} %coeffs_in.1, ...), custom_call_target="tpu_custom_call" | custom-call | flops 805306368 | bytes 12582912 | tf_op jit(solution)/shard_map/gram/pallas_call | solution.py:127
  9.4 1.5 collective-permute-start
  10.9 0.0 copy-done.3
  10.9 3.0 %collective-permute-start.2 = (f32[32,128]{1,0:T(8,128)S(1)}, f32[32,128]{1,0:T(8,128)S(1)}, u32[]{:S(2)}, u32[]{:S(2)}) collective-permute-start(f32[32,128]{1,0:T(8,128)S(1)} %copy-done.3), channel_id=1, source_target_pairs={{0,2},{1,3},{2,0},{3,1},{4,6},{5,7},{6,4},{7,5},{8,10},{9,11},{10,... | collective-permute-start | bytes 49160 | tf_op jit(solution)/shard_map/ppermute | solution.py:480
  14.0 0.4 collective-permute-start.1
  14.4 2.3 %collective-permute-start.3 = (f32[32,128]{1,0:T(8,128)S(1)}, f32[32,128]{1,0:T(8,128)S(1)}, u32[]{:S(2)}, u32[]{:S(2)}) collective-permute-start(f32[32,128]{1,0:T(8,128)S(1)} %copy-done.3), channel_id=1, source_target_pairs={{0,3},{1,0},{2,1},{3,2},{4,7},{5,4},{6,5},{7,6},{8,11},{9,8},{10,9... | collective-permute-start | bytes 49160 | tf_op jit(solution)/shard_map/ppermute | solution.py:480
  16.6 0.0 collective-permute-done.2.dual2
  16.6 1.1 collective-permute-done.1.dual1
  17.8 0.0 collective-permute-done.3.dual3
  17.8 0.0 copy-done.1
  17.8 0.0 copy-done
  17.8 0.0 copy-done.6
  17.8 0.0 copy-done.2
  17.8 0.0 copy-done.5
  17.8 4.8 %rhs.1 = (f32[64,8,128]{2,1,0:T(8,128)S(1)}, f32[64,8,128]{2,1,0:T(8,128)S(1)}, f32[16,128]{1,0:T(8,128)S(1)}) custom-call(s32[4,16]{1,0:T(4,128)S(1)} %bitcast.28, s32[16]{0:T(128)S(1)} %copy-done.6, bf16[128,128]{1,0:T(8,128)(2,1)S(1)} %get-tuple-element.37.hot_place, f32[16,4,128,128]{3,2,1,0:T(8,128)S(1)} %get-tuple-element.33.coeffs.refs_2_, ...), custom_call_target="tpu_custom_call" | custom-call | flops 134217728 | bytes 6291456 | tf_op jit(solution)/shard_map/rhs/pallas_call | solution.py:224
  22.6 1.6 collective-permute-start.4
  24.2 1.2 collective-permute-done.4.small_got
  25.4 0.0 collective-permute-done.got
  25.4 0.2 join.1
  25.6 0.0 copy-start.4
  25.7 43.3 %all_to_all.71.got = f32[64,72,128]{2,1,0:T(8,128)S(1)} all-to-all(f32[64,72,128]{2,1,0:T(8,128)S(1)} %join.1), channel_id=1, replica_groups=mesh['x'=4,'z'=4,'core'=2,'leg'=4] {'leg','x','z'}, dimensions={0} | all-to-all | bytes 4718592 | tf_op jit(solution)/shard_map/all_to_all | solution.py:473
  69.0 0.0 copy-done.4
  69.0 4.4 %first.1 = (f32[128,128]{1,0:T(8,128)S(1)}, f32[8,128]{1,0:T(8,128)S(1)}, f32[8,128]{1,0:T(8,128)S(1)}, f32[256,128]{1,0:T(8,128)S(1)}) custom-call(f32[64,72,128]{2,1,0:T(8,128)S(1)} %all_to_all.71.got, f32[32,128]{1,0:T(8,128)S(1)} %copy-done.4), custom_call_target="tpu_custom_call" | custom-call | tf_op jit(solution)/shard_map/first/pallas_call | solution.py:350
  73.4 15.2 %all_to_all.72 = f32[128,2,128]{2,1,0:T(2,128)S(1)} all-to-all(f32[128,2,128]{2,1,0:T(2,128)S(1)} %bitcast.21), channel_id=1, replica_groups=mesh['x'=4,'z'=4,'core'=2,'leg'=4] {'leg','x','z','core'}, dimensions={0} | all-to-all | bytes 262144 | tf_op jit(solution)/shard_map/all_to_all | solution.py:473
  88.6 3.6 %tile.2 = (f32[128,128]{1,0:T(8,128)S(1)}, f32[16,128]{1,0:T(8,128)S(1)}, f32[8,128]{1,0:T(8,128)S(1)}, f32[256,128]{1,0:T(8,128)S(1)}) custom-call(s32[4,16]{1,0:T(4,128)S(1)} %bitcast.29, bf16[128,128]{1,0:T(8,128)(2,1)S(1)} %get-tuple-element.32.refs_1_, f32[16,4,128,128]{3,2,1,0:T(8,128)S(1)} %get-tuple-element.33.coeffs.refs_2_, ...), custom_call_target="tpu_custom_call" | custom-call | tf_op jit(solution)/shard_map/tile/pallas_call | solution.py:429
  92.2 14.2 %all_to_all.73 = f32[128,2,128]{2,1,0:T(2,128)S(1)} all-to-all(f32[128,2,128]{2,1,0:T(2,128)S(1)} %bitcast.22), channel_id=1, replica_groups=mesh['x'=4,'z'=4,'core'=2,'leg'=4] {'leg','x','z','core'}, dimensions={0} | all-to-all | bytes 262144 | tf_op jit(solution)/shard_map/all_to_all | solution.py:473
  106.4 0.4 owner.2
  106.7 14.2 %all_to_all.74 = f32[128,2,128]{2,1,0:T(2,128)S(1)} all-to-all(f32[128,2,128]{2,1,0:T(2,128)S(1)} %bitcast.24), channel_id=1, replica_groups=mesh['x'=4,'z'=4,'core'=2,'leg'=4] {'leg','x','z','core'}, dimensions={0} | all-to-all | bytes 262144 | tf_op jit(solution)/shard_map/all_to_all | solution.py:473
  120.9 3.6 %tile.3 = (f32[128,128]{1,0:T(8,128)S(1)}, f32[16,128]{1,0:T(8,128)S(1)}, f32[8,128]{1,0:T(8,128)S(1)}, f32[256,128]{1,0:T(8,128)S(1)}) custom-call(s32[4,16]{1,0:T(4,128)S(1)} %bitcast.30, bf16[128,128]{1,0:T(8,128)(2,1)S(1)} %get-tuple-element.32.refs_1_, f32[16,4,128,128]{3,2,1,0:T(8,128)S(1)} %get-tuple-element.33.coeffs.refs_2_, ...), custom_call_target="tpu_custom_call" | custom-call | tf_op jit(solution)/shard_map/tile/pallas_call | solution.py:429
  124.6 14.2 %all_to_all.75 = f32[128,2,128]{2,1,0:T(2,128)S(1)} all-to-all(f32[128,2,128]{2,1,0:T(2,128)S(1)} %bitcast.23), channel_id=1, replica_groups=mesh['x'=4,'z'=4,'core'=2,'leg'=4] {'leg','x','z','core'}, dimensions={0} | all-to-all | bytes 262144 | tf_op jit(solution)/shard_map/all_to_all | solution.py:473
  138.7 0.4 owner.3
  139.1 14.2 %all_to_all.76 = f32[128,2,128]{2,1,0:T(2,128)S(1)} all-to-all(f32[128,2,128]{2,1,0:T(2,128)S(1)} %bitcast.25), channel_id=1, replica_groups=mesh['x'=4,'z'=4,'core'=2,'leg'=4] {'leg','x','z','core'}, dimensions={0} | all-to-all | bytes 262144 | tf_op jit(solution)/shard_map/all_to_all | solution.py:473
  153.3 2.3 %tile_last.1 = (f32[128,128]{1,0:T(8,128)S(1)}, f32[16,128]{1,0:T(8,128)S(1)}, f32[8,128]{1,0:T(8,128)S(1)}, f32[128,128]{1,0:T(8,128)S(1)}) custom-call(s32[4,16]{1,0:T(4,128)S(1)} %bitcast.31, bf16[128,128]{1,0:T(8,128)(2,1)S(1)} %get-tuple-element.32.refs_1_, f32[16,4,128,128]{3,2,1,0:T(8,128)S(1)} %get-tuple-element.33.coeffs.refs_2_, ...), custom_call_target="tpu_custom_call" | custom-call | tf_op jit(solution)/shard_map/tile_last/pallas_call | solution.py:429
  155.6 13.6 %all_to_all.77 = f32[128,1,128]{2,1,0:T(1,128)S(1)} all-to-all(f32[128,1,128]{2,1,0:T(1,128)S(1)} %bitcast.26), channel_id=1, replica_groups=mesh['x'=4,'z'=4,'core'=2,'leg'=4] {'leg','x','z','core'}, dimensions={0} | all-to-all | bytes 131072 | tf_op jit(solution)/shard_map/all_to_all | solution.py:473
  169.2 1.3 final.1
Async XLA Ops:
  0.6 17.1 %copy-start.1 = (f32[16,128]{1,0:T(8,128)S(1)}, f32[16,128]{1,0:T(8,128)}, u32[]{:S(2)}) copy-start(f32[16,128]{1,0:T(8,128)} %slack.3) | copy-start | bytes 24580
  0.6 17.1 %copy-start = (f32[16,128]{1,0:T(8,128)S(1)}, f32[16,128]{1,0:T(8,128)}, u32[]{:S(2)}) copy-start(f32[16,128]{1,0:T(8,128)} %primal.3) | copy-start | bytes 24580
  0.7 17.1 %copy-start.6 = (s32[16]{0:T(128)S(1)}, s32[16]{0:T(128)}, u32[]{:S(2)}) copy-start(s32[16]{0:T(128)} %counts.3) | copy-start | bytes 196
  0.7 17.1 %copy-start.2 = (s32[16,4]{0,1:T(4,128)S(1)}, s32[16,4]{0,1:T(4,128)}, u32[]{:S(2)}) copy-start(s32[16,4]{0,1:T(4,128)} %param.9) | copy-start | bytes 772
  0.7 10.3 %copy-start.3 = (f32[32,128]{1,0:T(8,128)S(1)}, f32[32,128]{1,0:T(8,128)}, u32[]{:S(2)}) copy-start(f32[32,128]{1,0:T(8,128)} %dual0.1) | copy-start | bytes 49156
  0.7 17.1 %copy-start.5 = (f32[16,128]{1,0:T(8,128)S(1)}, f32[16,128]{1,0:T(8,128)}, u32[]{:S(2)}) copy-start(f32[16,128]{1,0:T(8,128)} %cost.1) | copy-start | bytes 24580
  9.4 16.0 %collective-permute-start = (f32[64,64,128]{2,1,0:T(8,128)S(1)}, f32[64,64,128]{2,1,0:T(8,128)S(1)}, u32[]{:S(2)}, u32[]{:S(2)}) collective-permute-start(f32[64,64,128]{2,1,0:T(8,128)S(1)} %get-tuple-element.36), channel_id=1, source_target_pairs={{0,4},{4,0},{1,5},{5,1},{2,6},{6,2},{3,7},{7,3},{8,12},{12,8},{9,1... | collective-permute-start | bytes 6291464 | tf_op jit(solution)/shard_map/ppermute | solution.py:486
  10.9 5.7 %collective-permute-start.2 = (f32[32,128]{1,0:T(8,128)S(1)}, f32[32,128]{1,0:T(8,128)S(1)}, u32[]{:S(2)}, u32[]{:S(2)}) collective-permute-start(f32[32,128]{1,0:T(8,128)S(1)} %copy-done.3), channel_id=1, source_target_pairs={{0,2},{1,3},{2,0},{3,1},{4,6},{5,7},{6,4},{7,5},{8,10},{9,11},{10,... | collective-permute-start | bytes 49160 | tf_op jit(solution)/shard_map/ppermute | solution.py:480
  14.0 3.8 %collective-permute-start.1 = (f32[32,128]{1,0:T(8,128)S(1)}, f32[32,128]{1,0:T(8,128)S(1)}, u32[]{:S(2)}, u32[]{:S(2)}) collective-permute-start(f32[32,128]{1,0:T(8,128)S(1)} %copy-done.3), channel_id=1, source_target_pairs={{0,1},{1,2},{2,3},{3,0},{4,5},{5,6},{6,7},{7,4},{8,9},{9,10},{10,1... | collective-permute-start | bytes 49160 | tf_op jit(solution)/shard_map/ppermute | solution.py:480
  14.4 3.4 %collective-permute-start.3 = (f32[32,128]{1,0:T(8,128)S(1)}, f32[32,128]{1,0:T(8,128)S(1)}, u32[]{:S(2)}, u32[]{:S(2)}) collective-permute-start(f32[32,128]{1,0:T(8,128)S(1)} %copy-done.3), channel_id=1, source_target_pairs={{0,3},{1,0},{2,1},{3,2},{4,7},{5,4},{6,5},{7,6},{8,11},{9,8},{10,9... | collective-permute-start | bytes 49160 | tf_op jit(solution)/shard_map/ppermute | solution.py:480
  22.6 2.8 %collective-permute-start.4 = (f32[64,8,128]{2,1,0:T(8,128)S(1)}, f32[64,8,128]{2,1,0:T(8,128)S(1)}, u32[]{:S(2)}, u32[]{:S(2)}) collective-permute-start(f32[64,8,128]{2,1,0:T(8,128)S(1)} %get-tuple-element.40), channel_id=1, source_target_pairs={{0,4},{4,0},{1,5},{5,1},{2,6},{6,2},{3,7},{7,3},{8,12},{12,8},{9,1... | collective-permute-start | bytes 786440 | tf_op jit(solution)/shard_map/ppermute | solution.py:490
  25.6 43.4 %copy-start.4 = (f32[32,128]{1,0:T(8,128)S(1)}, f32[32,128]{1,0:T(8,128)}, u32[]{:S(2)}) copy-start(f32[32,128]{1,0:T(8,128)} %demand.1) | copy-start | bytes 49156

commit v3 on v2

--- a/solution.py
+++ b/solution.py
@@ -15,7 +15,7 @@
 SPAN = 4
 GROUPS = 16
 TILES = GROUPS * SPAN
-EXTRA = 8
+EXTRA = 4
 ROWS = HALF + EXTRA
 
 VMEM = pltpu.MemorySpace.VMEM
@@ -41,7 +41,7 @@
 
 
 def device_col():
-    return (lax.axis_index("x") * 4 + lax.axis_index("z")) * 2 + lax.axis_index("core")
+    return (lax.axis_index("x") * 2 + lax.axis_index("core")) * 4 + lax.axis_index("z")
 
 
 def params():
@@ -53,24 +53,15 @@
     return high, (x - high.astype(jnp.float32)).astype(jnp.bfloat16)
 
 
-def gram_product(tile, root):
-    high, low = split(tile * root)
-    both = lax.dot_general(high, high, NT, preferred_element_type=jnp.float32)
-    cross = lax.dot_general(
-        jnp.concatenate([high, low], axis=1),
-        jnp.concatenate([low, high], axis=1),
-        NT,
-        preferred_element_type=jnp.float32,
-    )
-    return both + cross
-
-
-UNROLL = 4
+def gram_product(high, low):
+    both = jnp.concatenate([high, low], axis=0)
+    full = lax.dot_general(both, both, NT, preferred_element_type=jnp.float32)
+    return (full[:N, :N] + full[N:, N:]) + (full[:N, N:] + full[N:, :N])
 
 
 def gram_kernel(
-    coeffs_in, ids_in, counts_in, primal_in, slack_in, coeffs, acc, other, small, scale_out,
-    hot_ids, hot_place, ids, counts, primal, slack, hot, hot2, sem, tile_sem,
+    coeffs_in, ids_in, counts_in, primal_in, slack_in, tiles, acc, other, small, root_out,
+    hot_ids, hot_place, coeffs, ids, counts, primal, slack, hot, hot2, sem, tile_sem,
 ):
     little = [
         pltpu.make_async_copy(ids_in, ids, sem.at[0]),
@@ -78,10 +69,9 @@
         pltpu.make_async_copy(primal_in, primal, sem.at[2]),
         pltpu.make_async_copy(slack_in, slack, sem.at[3]),
     ]
-    for copy in little:
+    big = [pltpu.make_async_copy(coeffs_in.at[g], coeffs.at[g], tile_sem.at[g]) for g in range(GROUPS)]
+    for copy in little + big:
         copy.start()
-    for g in range(GROUPS):
-        pltpu.make_async_copy(coeffs_in.at[g], coeffs.at[g], tile_sem.at[g]).start()
     acc[...] = jnp.zeros_like(acc)
     small[...] = jnp.zeros_like(small)
     hot[...] = jnp.zeros_like(hot)
@@ -93,31 +83,27 @@
     lane = iota((HALF, N), 1)
     line_lane = iota((1, N), 1)
     lower = jnp.logical_or(row >= lane, lane >= HALF)
-
-    def group(g):
-        pltpu.make_async_copy(coeffs_in.at[g], coeffs.at[g], tile_sem.at[g]).wait()
-        valid = line_lane < counts[g]
-        scale = jnp.where(valid, primal[pl.ds(g, 1), :] / slack[pl.ds(g, 1), :], 0.0)
-        scale_out[pl.ds(g, 1), :] = scale
-        root = jnp.sqrt(scale)
+    for g in range(GROUPS):
+        scale = jnp.where(line_lane < counts[g], primal[g : g + 1, :] / slack[g : g + 1, :], 0.0)
+        root_out[g : g + 1, :] = jnp.sqrt(scale)
+    for g in range(GROUPS):
+        big[g].wait()
+        root = root_out[g : g + 1, :]
         for s in range(SPAN):
-            gram = gram_product(coeffs[g, s], root)
+            high, low = split(coeffs[g, s] * root)
+            tiles[g, s * N : (s + 1) * N, :] = jnp.concatenate([high, low], axis=1)
+            gram = gram_product(high, low)
             rolled = pltpu.roll(gram[HALF:], HALF, 1)
             packed = jnp.where(lower, gram[:HALF], rolled)
             line = jnp.sum(jnp.where(row == lane, rolled, 0.0), axis=0, keepdims=True)
             block = ids[s, g]
-            place = ((block & 1) ^ core) * HALF + (block >> 1)
+            chip = ((block >> 3) << 2) | (block & 3)
+            place = (((block >> 2) & 1) ^ core) * HALF + chip
             acc[place] += packed
-            small[place, 0:1, :] += line
+            small[pl.ds(place * EXTRA, 1), :] += line
             t = g * SPAN + s
-            hot[pl.ds(t, 1), :] = (line_lane == block).astype(jnp.float32)
-            hot2[pl.ds(t, 1), :] = (line_lane == place).astype(jnp.float32)
-
-    @pl.loop(0, GROUPS // UNROLL)
-    def _(i):
-        for k in range(UNROLL):
-            group(i * UNROLL + k)
-
+            hot[t : t + 1, :] = (line_lane == block).astype(jnp.float32)
+            hot2[t : t + 1, :] = (line_lane == place).astype(jnp.float32)
     other[...] = acc[pl.ds(HALF, HALF)]
     hot_ids[...] = jnp.transpose(hot[...]).astype(jnp.bfloat16)
     hot_place[...] = jnp.transpose(hot2[...]).astype(jnp.bfloat16)
@@ -127,10 +113,10 @@
     return pl.pallas_call(
         gram_kernel,
         out_shape=(
-            f32(GROUPS, SPAN, N, N),
+            jax.ShapeDtypeStruct((GROUPS, SPAN * N, 2 * N), jnp.bfloat16),
             f32(N, HALF, N),
             f32(HALF, HALF, N),
-            f32(N, EXTRA, N),
+            f32(N * EXTRA, N),
             f32(GROUPS, N),
             jax.ShapeDtypeStruct((N, N), jnp.bfloat16),
             jax.ShapeDtypeStruct((N, N), jnp.bfloat16),
@@ -138,6 +124,7 @@
         in_specs=[pl.BlockSpec(memory_space=HBM)] * 5,
         out_specs=(vspec(),) * 7,
         scratch_shapes=[
+            pltpu.VMEM((GROUPS, SPAN, N, N), jnp.float32),
             pltpu.SMEM((SPAN, GROUPS), jnp.int32),
             pltpu.SMEM((GROUPS,), jnp.int32),
             pltpu.VMEM((GROUPS, N), jnp.float32),
@@ -149,103 +136,117 @@
         ],
         compiler_params=params(),
         cost_estimate=pl.CostEstimate(
-            flops=TILES * 2 * N**3 * 3, bytes_accessed=12 << 20, transcendentals=0
+            flops=TILES * 2 * N**3 * 4, bytes_accessed=12 << 20, transcendentals=0
         ),
         name="gram",
     )(*(pltpu.with_memory_space_constraint(x, HBM) for x in (coeffs, ids, counts, primal, slack)))
 
 
-def transpose_apply(ids, coeffs, vector, spread):
+def transpose_apply(ids, tiles, vector, spread, out):
     for t in range(TILES):
-        spread[pl.ds(t, 1), :] = vector[pl.ds(ids[t % SPAN, t // SPAN], 1), :]
-    columns = jnp.transpose(spread[...])
+        spread[t : t + 1, :] = vector[pl.ds(ids[t % SPAN, t // SPAN], 1), :]
+    high, low = split(spread[...])
+    for g in range(GROUPS):
+        parts = []
+        for rows in (high, low):
+            own = [rows[g * SPAN + s : g * SPAN + s + 1] for s in range(SPAN)]
+            parts.append(jnp.concatenate(own, axis=1))
+        both = jnp.concatenate(parts, axis=0)
+        full = jnp.dot(both, tiles[g], preferred_element_type=jnp.float32)
+        out[g : g + 1, :] = (full[0:1, :N] + full[1:2, N:]) + (full[0:1, N:] + full[1:2, :N])
+
+
+def forward_apply(tiles, colvecs, outs):
     lines = []
+    for w in colvecs:
+        high, low = split(w)
+        lines.append(jnp.concatenate([high, high], axis=1))
+        lines.append(jnp.concatenate([low, jnp.zeros_like(low)], axis=1))
     for g in range(GROUPS):
-        total = None
-        for s in range(SPAN):
-            t = g * SPAN + s
-            prod = coeffs[g, s] * jnp.broadcast_to(columns[:, t : t + 1], (N, N))
-            part = jnp.sum(prod.reshape(N // 8, 8, N), axis=0)
-            total = part if total is None else total + part
-        lines.append(jnp.sum(total, axis=0, keepdims=True))
-    return jnp.concatenate(lines, axis=0)
-
-
-def forward_apply(coeffs, colvec):
-    lane = iota((N, N), 1)
-    columns = jnp.zeros((N, N), jnp.float32)
-    for g in range(GROUPS):
-        w = colvec[g : g + 1, :]
-        for s in range(SPAN):
-            t = g * SPAN + s
-            total = jnp.sum(coeffs[g, s] * w, axis=1, keepdims=True)
-            columns = jnp.where(lane == t, total, columns)
-    return jnp.transpose(columns)[:TILES]
+        both = jnp.concatenate([line[g : g + 1] for line in lines], axis=0)
+        full = lax.dot_general(both, tiles[g], NT, preferred_element_type=jnp.float32)
+        for k, out in enumerate(outs):
+            total = full[2 * k : 2 * k + 1] + full[2 * k + 1 : 2 * k + 2]
+            for s in range(SPAN):
+                t = g * SPAN + s
+                out[t : t + 1, :] = total[:, s * N : (s + 1) * N]
 
 
 def place_rows(hot, rows):
     rows = jnp.concatenate([rows, jnp.zeros((N - TILES, N), jnp.float32)], axis=0)
-    high, rest = rows.astype(jnp.bfloat16), None
-    rest = rows - high.astype(jnp.float32)
-    middle, low = split(rest)
+    high = rows.astype(jnp.bfloat16)
+    middle, low = split(rows - high.astype(jnp.float32))
     total = jnp.dot(hot, high, preferred_element_type=jnp.float32)
     total = total + jnp.dot(hot, middle, preferred_element_type=jnp.float32)
     return total + jnp.dot(hot, low, preferred_element_type=jnp.float32)
 
 
 def rhs_kernel(
-    ids, counts, hot_place, coeffs, dual0, dual1, dual2, dual3, primal, slack, cost, scale, small,
-    own_out, other_out, dual_res_out, spread, duals, valid_s,
+    ids, counts, hot_place, tiles, dual0, dual1, dual2, dual3, primal, slack, cost, root, small,
+    own_out, other_out, base_out, scale_out, spread, spread2, duals, valid_s, applied,
 ):
     leg = lax.axis_index("leg")
     for k, part in enumerate((dual0, dual1, dual2, dual3)):
         at = pl.multiple_of(((leg - k) & 3) * 32, 32)
         duals[pl.ds(at, 32), :] = part[...]
     for g in range(GROUPS):
-        valid_s[pl.ds(g, 1), :] = (iota((1, N), 1) < counts[g]).astype(jnp.float32)
+        valid_s[g : g + 1, :] = (iota((1, N), 1) < counts[g]).astype(jnp.float32)
     valid = valid_s[...]
-    dual_res = cost[...] - valid * transpose_apply(ids, coeffs, duals, spread) - slack[...]
-    dual_res_out[...] = dual_res
-    first = place_rows(hot_place[...], forward_apply(coeffs, scale[...] * dual_res))
-    second = place_rows(hot_place[...], forward_apply(coeffs, valid / slack[...]))
-    comp = jnp.sum(valid * primal[...] * slack[...], axis=0, keepdims=True)
-    used = jnp.sum(valid, axis=0, keepdims=True)
+    used = valid > 0.0
+    transpose_apply(ids, tiles, duals, spread, applied)
+    dual_res = cost[...] - applied[...] / jnp.where(used, root[...], 1.0) - slack[...]
+    weighted = root[...] * dual_res
+    ratio = valid / slack[...]
+    base_out[...] = -(root[...] * weighted) - valid * primal[...]
+    scale_out[...] = ratio
+    product = primal[...] * slack[...]
+    forward_apply(tiles, (weighted, valid / jnp.sqrt(product)), (spread, spread2))
+    first = place_rows(hot_place[...], spread[...])
+    second = place_rows(hot_place[...], spread2[...])
+    comp = jnp.sum(valid * product, axis=0, keepdims=True)
+    count = jnp.sum(jnp.sum(valid, axis=0, keepdims=True), axis=1, keepdims=True)
     for k, out in enumerate((own_out, other_out)):
         half = slice(k * HALF, k * HALF + HALF)
-        out[:, 0:1, :] = small[half, 0:1, :]
-        out[:, 1:2, :] = first[half].reshape(HALF, 1, N)
-        out[:, 2:3, :] = second[half].reshape(HALF, 1, N)
-        out[:, 3:4, :] = jnp.broadcast_to(comp.reshape(1, 1, N), (HALF, 1, N))
-        out[:, 4:5, :] = jnp.broadcast_to(used.reshape(1, 1, N), (HALF, 1, N))
-        out[:, 5:8, :] = jnp.zeros((HALF, 3, N), jnp.float32)
-
-
-def run_rhs(ids, counts, hot_place, coeffs, duals, primal, slack, cost, scale, small):
+        diag = small[pl.ds(k * HALF * EXTRA, HALF, stride=EXTRA), :]
+        diag = jnp.where(iota((HALF, N), 1) < HALF, diag, jnp.broadcast_to(count, (HALF, N)))
+        out[pl.ds(0, HALF, stride=EXTRA), :] = diag
+        out[pl.ds(1, HALF, stride=EXTRA), :] = first[half]
+        out[pl.ds(2, HALF, stride=EXTRA), :] = second[half]
+        out[pl.ds(3, HALF, stride=EXTRA), :] = jnp.broadcast_to(comp, (HALF, N))
+
+
+def run_rhs(ids, counts, hot_place, tiles, duals, primal, slack, cost, root, small):
     return pl.pallas_call(
         rhs_kernel,
-        out_shape=(f32(HALF, EXTRA, N), f32(HALF, EXTRA, N), f32(GROUPS, N)),
+        out_shape=(f32(HALF * EXTRA, N), f32(HALF * EXTRA, N), f32(GROUPS, N), f32(GROUPS, N)),
         in_specs=[sspec(), sspec()] + [vspec()] * 11,
-        out_specs=(vspec(),) * 3,
+        out_specs=(vspec(),) * 4,
         scratch_shapes=[
+            pltpu.VMEM((TILES, N), jnp.float32),
             pltpu.VMEM((TILES, N), jnp.float32),
             pltpu.VMEM((N, N), jnp.float32),
             pltpu.VMEM((GROUPS, N), jnp.float32),
+            pltpu.VMEM((GROUPS, N), jnp.float32),
         ],
         compiler_params=params(),
         cost_estimate=pl.CostEstimate(flops=1 << 27, bytes_accessed=6 << 20, transcendentals=0),
         name="rhs",
-    )(ids, counts, hot_place, coeffs, *duals, primal, slack, cost, scale, small)
+    )(ids, counts, hot_place, tiles, *duals, primal, slack, cost, root, small)
 
 
 def join_kernel(acc, got, small, small_got, out):
-    out[:, 0:HALF, :] = acc[pl.ds(0, HALF)] + got[...]
-    out[:, HALF:ROWS, :] = small[...] + small_got[...]
+    for p in range(HALF // 2):
+        at = 2 * ROWS * p
+        out[at : at + HALF, :] = acc[2 * p] + got[2 * p]
+        extra = slice(2 * EXTRA * p, 2 * EXTRA * (p + 1))
+        out[at + HALF : at + HALF + 2 * EXTRA, :] = small[extra, :] + small_got[extra, :]
+        out[at + HALF + 2 * EXTRA : at + 2 * ROWS, :] = acc[2 * p + 1] + got[2 * p + 1]
 
 
 def run_join(acc, got, small, small_got):
     return pl.pallas_call(
         join_kernel,
-        out_shape=f32(HALF, ROWS, N),
+        out_shape=f32(HALF * ROWS, N),
         in_specs=[vspec()] * 4,
         out_specs=vspec(),
         compiler_params=params(),
@@ -309,14 +310,16 @@
 
 def first_kernel(got, demand, inverse_out, residual_out, mu_out, msg):
     def add(i, carry):
-        return carry + got[i]
-
-    total = lax.fori_loop(1, HALF, add, got[0], unroll=7)
-    packed = total[:HALF]
-    line = total[HALF : HALF + 1]
-    tail = total[HALF:]
+        return carry + got[pl.ds(pl.multiple_of(i * 2 * ROWS, 8), 2 * ROWS), :]
+
+    total = lax.fori_loop(1, HALF // 2, add, got[0 : 2 * ROWS, :], unroll=True)
+    total = total[:ROWS] + total[ROWS:]
+    odd = (lax.axis_index("z") & 1) == 1
+    packed = jnp.where(odd, total[EXTRA:], total[:HALF])
+    tail = jnp.where(odd, total[:EXTRA], total[HALF:])
+    line = tail[0:1]
     comp = jnp.sum(tail[3:4], axis=1, keepdims=True)
-    used = jnp.sum(tail[4:5], axis=1, keepdims=True)
+    used = line[:, HALF : HALF + 1]
     mu = SIGMA * (comp / used)
     mu_out[...] = jnp.broadcast_to(mu, (8, N))
     residual = demand[pl.ds(device_col(), 1), :] + tail[1:2] - mu * tail[2:3]
@@ -391,7 +394,7 @@
     )(got, direction, norms, residual, inverse)
 
 
-def tile_kernel(last, begin, ids, hot, coeffs, scale, got, *refs):
+def tile_kernel(last, begin, ids, hot, tiles, got, *refs):
     if begin:
         direction_out, applied_out, norms_out, msg, spread = refs
     else:
@@ -403,23 +406,21 @@
     else:
         direction = smoothed + (norm / norms_in[0:1, :]) * direction_in[...]
     direction_out[...] = direction
+    transpose_apply(ids, tiles, direction_out, spread, applied_out)
     square = jnp.sum(jnp.sum(direction * direction, axis=0, keepdims=True), axis=1, keepdims=True)
-    square = jnp.broadcast_to(REGULAR * square, (1, N))
     norms_out[0:1, :] = norm
-    norms_out[1:2, :] = square
-    applied = transpose_apply(ids, coeffs, direction_out, spread)
-    applied_out[...] = applied
-    weighted = scale[...] * applied
-    curve = jnp.sum(weighted * applied, axis=0, keepdims=True)
+    norms_out[1:2, :] = jnp.broadcast_to(REGULAR * square, (1, N))
+    applied = applied_out[...]
+    curve = jnp.sum(applied * applied, axis=0, keepdims=True)
     if last:
         msg[...] = jnp.broadcast_to(curve, (N, N))
     else:
-        image = place_rows(hot[...], forward_apply(coeffs, weighted))
-        msg[pl.ds(0, N, stride=2), :] = image
+        forward_apply(tiles, (applied,), (spread,))
+        msg[pl.ds(0, N, stride=2), :] = place_rows(hot[...], spread[...])
         msg[pl.ds(1, N, stride=2), :] = jnp.broadcast_to(curve, (N, N))
 
 
-def run_tile(last, ids, hot, coeffs, scale, got, direction=None, norms=None):
+def run_tile(last, ids, hot, tiles, got, direction=None, norms=None):
     begin = direction is None
     extra = () if begin else (direction, norms)
 
@@ -429,17 +430,17 @@
     return pl.pallas_call(
         kernel,
         out_shape=(f32(N, N), f32(GROUPS, N), f32(8, N), f32(N if last else 2 * N, N)),
-        in_specs=[sspec()] + [vspec()] * (4 + len(extra)),
+        in_specs=[sspec()] + [vspec()] * (3 + len(extra)),
         out_specs=(vspec(),) * 4,
         scratch_shapes=[pltpu.VMEM((TILES, N), jnp.float32)],
         compiler_params=params(),
         name="tile_last" if last else "tile",
-    )(ids, hot, coeffs, scale, got, *extra)
+    )(ids, hot, tiles, got, *extra)
 
 
 def final_kernel(
-    counts, got, curve0, curve1, d0, d1, d2, u0, u1, u2, n0, n1, n2, mu, primal, slack,
-    scale, dual_res, step_dual, step_primal,
+    got, curve0, curve1, d0, d1, d2, u0, u1, u2, n0, n1, n2, mu, root, base, ratio, step_dual,
+    step_primal,
 ):
     curve2 = jnp.sum(jnp.sum(got[...], axis=0, keepdims=True), axis=1, keepdims=True)
     lens = []
@@ -448,24 +449,21 @@
     at = pl.ds(pl.multiple_of(lax.axis_index("leg") * 32, 32), 32)
     step_dual[...] = lens[0] * d0[at, :] + lens[1] * d1[at, :] + lens[2] * d2[at, :]
     applied = lens[0] * u0[...] + lens[1] * u1[...] + lens[2] * u2[...]
-    inner = scale[...] * (applied - dual_res[...]) + (mu[0:1, :] / slack[...] - primal[...])
-    for g in range(GROUPS):
-        valid = iota((1, N), 1) < counts[g]
-        step_primal[g : g + 1, :] = jnp.where(valid, inner[g : g + 1, :], 0.0)
-
-
-def run_final(counts, *args):
+    step_primal[...] = root[...] * applied + (mu[0:1, :] * ratio[...] + base[...])
+
+
+def run_final(*args):
     return pl.pallas_call(
         final_kernel,
         out_shape=(f32(32, N), f32(GROUPS, N)),
-        in_specs=[sspec()] + [vspec()] * len(args),
+        in_specs=[vspec()] * len(args),
         out_specs=(vspec(), vspec()),
         compiler_params=params(),
         name="final",
-    )(counts, *args)
-
-
-ALL = ("leg", "x", "z", "core")
+    )(*args)
+
+
+ALL = ("leg", "x", "core", "z")
 CHIPS = ("leg", "x", "z")
 
 
@@ -479,17 +477,18 @@
     for k in (1, 2, 3):
         parts.append(lax.ppermute(duals, "leg", [(i, (i + k) % 4) for i in range(4)]))
 
-    tiles, acc, other, small, scale, hot, hot_place = run_gram(
+    tiles, acc, other, small, root, hot, hot_place = run_gram(
         coeffs, ids, col_counts, primal, slack
     )
     swap = [(0, 1), (1, 0)]
+    other, *parts = lax.optimization_barrier((other, *parts))
     got_big = lax.ppermute(other, "core", swap)
-    small, small_other, dual_res = run_rhs(
-        ids, col_counts, hot_place, tiles, parts, primal, slack, cost, scale, small
+    small, small_other, base, ratio = run_rhs(
+        ids, col_counts, hot_place, tiles, parts, primal, slack, cost, root, small
     )
     got_small = lax.ppermute(small_other, "core", swap)
     joined = run_join(acc, got_big, small, got_small)
-    blocks = exchange(joined, CHIPS)
+    blocks = exchange(joined.reshape(HALF * ROWS // 4, 4, N), CHIPS).reshape(HALF * ROWS, N)
     inverse, residual, mu, msg = run_first(blocks, demand)
 
     direction = norms = None
@@ -498,9 +497,7 @@
     for turn in range(ITERS):
         got = exchange(msg, ALL)
         last = turn + 1 == ITERS
-        direction, applied, norms, msg = run_tile(
-            last, ids, hot, tiles, scale, got, direction, norms
-        )
+        direction, applied, norms, msg = run_tile(last, ids, hot, tiles, got, direction, norms)
         kept.append((direction, applied, norms))
         got = exchange(msg, ALL)
         if not last:
@@ -508,8 +505,7 @@
             curves.append(residual)
     (d0, u0, n0), (d1, u1, n1), (d2, u2, n2) = kept
     return run_final(
-        col_counts, got, curves[0], curves[1], d0, d1, d2, u0, u1, u2, n0, n1, n2, mu, primal,
-        slack, scale, dual_res,
+        got, curves[0], curves[1], d0, d1, d2, u0, u1, u2, n0, n1, n2, mu, root, base, ratio
     )
 
 

time: 171 us -> 159 us (0.930)
  Pallas kernels: 29.7 us -> 23.6 us
  blocking collectives: 129 us -> 125 us
    all_to_all x7, blocking collectives: 129 us -> 125 us  [exchange(): return lax.all_to_all(rows, axes, split_axis=0, concat_axis=0, tiled=True)]
    pallas_call x3, Pallas kernels: 9.57 us -> 6.53 us  [run_tile(): pl.pallas_call(kernel, out_shape=(f32(N, N), f32(GROUPS, N), f32(8, N), f...]
    pallas_call x3, Pallas kernels: 13.8 us -> 11.3 us  [the longest x1 8.47 us: run_gram(): pl.pallas_call(gram_kernel, out_shape=(jax.ShapeDtypeStruct((GROUPS, SPAN...]
  transfers between devices with their start and end apart: 5 -> 5, of which waited for: 2 -> 1; matrix products, arithmetic and copies ran while one was open for 0% -> 0% of each run, Pallas kernels for 3% -> 7%
where the time goes in v3:
time: 159 us
  blocking collectives  125 us (79%)
  Pallas kernels  23.6 us (15%)
  starting transfers between devices  8.21 us (5%)
    all_to_all x7, blocking collectives, exchange(): return lax.all_to_all(rows, axes, split_axis=0, concat_axis=0, tiled=True)  125 us
    pallas_call x1, Pallas kernels, run_gram(): pl.pallas_call(gram_kernel, out_shape=(jax.ShapeDtypeStruct((GROUPS, SPAN...  8.47 us
    pallas_call x3, Pallas kernels, run_tile(): pl.pallas_call(kernel, out_shape=(f32(N, N), f32(GROUPS, N), f32(8, N), f...  6.53 us
    ppermute x3, starting transfers between devices, per_device(): lax.ppermute(duals, 'leg', [(i, (i + k) % 4) for i in range(4)])  6.5 us
    pallas_call x1, Pallas kernels, run_first(): pl.pallas_call(first_kernel, out_shape=(f32(N, N), f32(8, N), f32(8, N),...  4.35 us
  transfers between devices with their start and end apart: 5, of which 1 were waited for; matrix products, arithmetic and copies ran while one was open for 0% of the time, Pallas kernels for 7%

profile of v3, /device:TPU:1, one launch (start us, length us, event | category | flops | bytes accessed | tf_op | source)
XLA Modules:
  0.0 158.8 jit_solution(8732235526601229775)
XLA Ops:
  0.6 0.0 copy-start.3
  0.6 0.0 copy-start.2
  0.7 0.0 copy-start.1
  0.7 0.0 copy-start.6
  0.7 0.0 copy-start
  0.7 0.0 copy-start.5
  0.7 3.8 %collective-permute-start.1 = (f32[32,128]{1,0:T(8,128)}, f32[32,128]{1,0:T(8,128)S(1)}, u32[]{:S(2)}, u32[]{:S(2)}) collective-permute-start(f32[32,128]{1,0:T(8,128)} %dual0), channel_id=1, source_target_pairs={{0,2},{1,3},{2,0},{3,1},{4,6},{5,7},{6,4},{7,5},{8,10},{9,11},{10,... | collective-permute-start | bytes 49160 | tf_op jit(solution)/shard_map/ppermute | solution.py:478
  4.5 0.4 collective-permute-start
  4.9 2.3 %collective-permute-start.2 = (f32[32,128]{1,0:T(8,128)}, f32[32,128]{1,0:T(8,128)S(1)}, u32[]{:S(2)}, u32[]{:S(2)}) collective-permute-start(f32[32,128]{1,0:T(8,128)} %dual0), channel_id=1, source_target_pairs={{0,3},{1,0},{2,1},{3,2},{4,7},{5,4},{6,5},{7,6},{8,11},{9,8},{10,9... | collective-permute-start | bytes 49160 | tf_op jit(solution)/shard_map/ppermute | solution.py:478
  7.2 8.5 %gram.1 = (bf16[16,512,256]{2,1,0:T(8,128)(2,1)S(1)}, f32[128,64,128]{2,1,0:T(8,128)S(1)}, f32[64,64,128]{2,1,0:T(8,128)S(1)}, f32[512,128]{1,0:T(8,128)S(1)}, f...) custom-call(f32[16,4,128,128]{3,2,1,0:T(8,128)} %coeffs_in.1, s32[4,16]{1,0:T(4,128)} %bitcast.31, ...), custom_call_target="tpu_custom_call" | custom-call | flops 1073741824 | bytes 12582912 | tf_op jit(solution)/shard_map/gram/pallas_call | solution.py:113
  15.7 0.0 collective-permute-done.1.dual2
  15.7 0.0 collective-permute-done.dual1
  15.7 0.0 collective-permute-done.2.dual3
  15.7 1.6 %collective-permute-start.3 = (f32[64,64,128]{2,1,0:T(8,128)S(1)}, f32[64,64,128]{2,1,0:T(8,128)S(1)}, u32[]{:S(2)}, u32[]{:S(2)}) collective-permute-start(f32[64,64,128]{2,1,0:T(8,128)S(1)} %get-tuple-element.42), channel_id=1, source_target_pairs={{0,4},{4,0},{1,5},{5,1},{2,6},{6,2},{3,7},{7,3},{8,12},{12,8},{9,1... | collective-permute-start | bytes 6291464 | tf_op jit(solution)/shard_map/ppermute | solution.py:485
  17.3 0.0 copy-done.3
  17.3 0.0 copy-done.2
  17.3 0.0 copy-done.1
  17.3 0.0 copy-done.6
  17.3 0.0 copy-done
  17.3 0.0 copy-done.5
  17.3 2.6 %rhs.1 = (f32[256,128]{1,0:T(8,128)S(1)}, f32[256,128]{1,0:T(8,128)S(1)}, f32[16,128]{1,0:T(8,128)S(1)}, f32[16,128]{1,0:T(8,128)S(1)}) custom-call(s32[4,16]{1,0:T(4,128)S(1)} %bitcast.32, s32[16]{0:T(128)S(1)} %copy-done.6, bf16[128,128]{1,0:T(8,128)(2,1)S(1)} %get-tuple-element.43.hot_place, bf16[16,512,256]{2,1,0:T(8,128)(2,1)S(1)} %get-tuple-element.39.tiles.refs_2_, ...), custom_call_target="tpu_custom_call" | custom-call | flops 134217728 | bytes 6291456 | tf_op jit(solution)/shard_map/rhs/pallas_call | solution.py:219
  20.0 0.1 collective-permute-start.4
  20.1 1.3 collective-permute-done.4.small_got
  21.4 0.0 collective-permute-done.3.got
  21.4 0.2 join.1
  21.6 0.0 copy-start.4
  21.6 39.2 %all_to_all.71 = f32[1088,4,128]{2,1,0:T(4,128)S(1)} all-to-all(f32[1088,4,128]{2,1,0:T(4,128)S(1)} %bitcast.18), channel_id=1, replica_groups=mesh['x'=4,'z'=4,'core'=2,'leg'=4] {'leg','x','z'}, dimensions={0} | all-to-all | bytes 4456448 | tf_op jit(solution)/shard_map/all_to_all | solution.py:471
  60.8 0.0 copy-done.4
  60.8 4.3 %first.1 = (f32[128,128]{1,0:T(8,128)S(1)}, f32[8,128]{1,0:T(8,128)S(1)}, f32[8,128]{1,0:T(8,128)S(1)}, f32[256,128]{1,0:T(8,128)S(1)}) custom-call(f32[4352,128]{1,0:T(8,128)S(1)} %bitcast.17, f32[32,128]{1,0:T(8,128)S(1)} %copy-done.4), custom_call_target="tpu_custom_call" | custom-call | tf_op jit(solution)/shard_map/first/pallas_call | solution.py:353
  65.2 15.6 %all_to_all.72 = f32[128,2,128]{2,1,0:T(2,128)S(1)} all-to-all(f32[128,2,128]{2,1,0:T(2,128)S(1)} %bitcast.25), channel_id=1, replica_groups=mesh['x'=4,'z'=4,'core'=2,'leg'=4] {'leg','x','core','z'}, dimensions={0} | all-to-all | bytes 262144 | tf_op jit(solution)/shard_map/all_to_all | solution.py:471
  80.8 2.6 %tile.2 = (f32[128,128]{1,0:T(8,128)S(1)}, f32[16,128]{1,0:T(8,128)S(1)}, f32[8,128]{1,0:T(8,128)S(1)}, f32[256,128]{1,0:T(8,128)S(1)}) custom-call(s32[4,16]{1,0:T(4,128)S(1)} %bitcast.33, bf16[128,128]{1,0:T(8,128)(2,1)S(1)} %get-tuple-element.38.refs_1_, bf16[16,512,256]{2,1,0:T(8,128)(2,1)S(1)} %get-tuple-element.39.tiles.refs_2_, f32[256,128]{1,0:T(8,128)S(1)} %bitcast.20), custom_call_target="tpu_custom_call" | custom-call | tf_op jit(solution)/shard_map/tile/pallas_call | solution.py:430
  83.4 14.1 %all_to_all.73 = f32[128,2,128]{2,1,0:T(2,128)S(1)} all-to-all(f32[128,2,128]{2,1,0:T(2,128)S(1)} %bitcast.26), channel_id=1, replica_groups=mesh['x'=4,'z'=4,'core'=2,'leg'=4] {'leg','x','core','z'}, dimensions={0} | all-to-all | bytes 262144 | tf_op jit(solution)/shard_map/all_to_all | solution.py:471
  97.5 0.4 owner.2
  97.9 14.1 %all_to_all.74 = f32[128,2,128]{2,1,0:T(2,128)S(1)} all-to-all(f32[128,2,128]{2,1,0:T(2,128)S(1)} %bitcast.28), channel_id=1, replica_groups=mesh['x'=4,'z'=4,'core'=2,'leg'=4] {'leg','x','core','z'}, dimensions={0} | all-to-all | bytes 262144 | tf_op jit(solution)/shard_map/all_to_all | solution.py:471
  112.0 2.6 %tile.3 = (f32[128,128]{1,0:T(8,128)S(1)}, f32[16,128]{1,0:T(8,128)S(1)}, f32[8,128]{1,0:T(8,128)S(1)}, f32[256,128]{1,0:T(8,128)S(1)}) custom-call(s32[4,16]{1,0:T(4,128)S(1)} %bitcast.34, bf16[128,128]{1,0:T(8,128)(2,1)S(1)} %get-tuple-element.38.refs_1_, bf16[16,512,256]{2,1,0:T(8,128)(2,1)S(1)} %get-tuple-element.39.tiles.refs_2_, ...), custom_call_target="tpu_custom_call" | custom-call | tf_op jit(solution)/shard_map/tile/pallas_call | solution.py:430
  114.6 14.1 %all_to_all.75 = f32[128,2,128]{2,1,0:T(2,128)S(1)} all-to-all(f32[128,2,128]{2,1,0:T(2,128)S(1)} %bitcast.27), channel_id=1, replica_groups=mesh['x'=4,'z'=4,'core'=2,'leg'=4] {'leg','x','core','z'}, dimensions={0} | all-to-all | bytes 262144 | tf_op jit(solution)/shard_map/all_to_all | solution.py:471
  128.7 0.4 owner.3
  129.1 14.1 %all_to_all.76 = f32[128,2,128]{2,1,0:T(2,128)S(1)} all-to-all(f32[128,2,128]{2,1,0:T(2,128)S(1)} %bitcast.29), channel_id=1, replica_groups=mesh['x'=4,'z'=4,'core'=2,'leg'=4] {'leg','x','core','z'}, dimensions={0} | all-to-all | bytes 262144 | tf_op jit(solution)/shard_map/all_to_all | solution.py:471
  143.2 1.3 tile_last.1
  144.5 13.6 %all_to_all.77 = f32[128,1,128]{2,1,0:T(1,128)S(1)} all-to-all(f32[128,1,128]{2,1,0:T(1,128)S(1)} %bitcast.30), channel_id=1, replica_groups=mesh['x'=4,'z'=4,'core'=2,'leg'=4] {'leg','x','core','z'}, dimensions={0} | all-to-all | bytes 131072 | tf_op jit(solution)/shard_map/all_to_all | solution.py:471
  158.1 0.7 final.1
Async XLA Ops:
  0.6 16.7 %copy-start.3 = (f32[32,128]{1,0:T(8,128)S(1)}, f32[32,128]{1,0:T(8,128)}, u32[]{:S(2)}) copy-start(f32[32,128]{1,0:T(8,128)} %dual0) | copy-start | bytes 49156
  0.6 16.7 %copy-start.2 = (f32[16,128]{1,0:T(8,128)S(1)}, f32[16,128]{1,0:T(8,128)}, u32[]{:S(2)}) copy-start(f32[16,128]{1,0:T(8,128)} %slack.1) | copy-start | bytes 24580
  0.7 16.7 %copy-start.1 = (f32[16,128]{1,0:T(8,128)S(1)}, f32[16,128]{1,0:T(8,128)}, u32[]{:S(2)}) copy-start(f32[16,128]{1,0:T(8,128)} %primal.1) | copy-start | bytes 24580
  0.7 16.6 %copy-start.6 = (s32[16]{0:T(128)S(1)}, s32[16]{0:T(128)}, u32[]{:S(2)}) copy-start(s32[16]{0:T(128)} %counts.1) | copy-start | bytes 196
  0.7 16.6 %copy-start = (s32[16,4]{0,1:T(4,128)S(1)}, s32[16,4]{0,1:T(4,128)}, u32[]{:S(2)}) copy-start(s32[16,4]{0,1:T(4,128)} %param.9) | copy-start | bytes 772
  0.7 16.6 %copy-start.5 = (f32[16,128]{1,0:T(8,128)S(1)}, f32[16,128]{1,0:T(8,128)}, u32[]{:S(2)}) copy-start(f32[16,128]{1,0:T(8,128)} %cost.1) | copy-start | bytes 24580
  0.7 15.0 %collective-permute-start.1 = (f32[32,128]{1,0:T(8,128)}, f32[32,128]{1,0:T(8,128)S(1)}, u32[]{:S(2)}, u32[]{:S(2)}) collective-permute-start(f32[32,128]{1,0:T(8,128)} %dual0), channel_id=1, source_target_pairs={{0,2},{1,3},{2,0},{3,1},{4,6},{5,7},{6,4},{7,5},{8,10},{9,11},{10,... | collective-permute-start | bytes 49160 | tf_op jit(solution)/shard_map/ppermute | solution.py:478
  4.5 11.2 %collective-permute-start = (f32[32,128]{1,0:T(8,128)}, f32[32,128]{1,0:T(8,128)S(1)}, u32[]{:S(2)}, u32[]{:S(2)}) collective-permute-start(f32[32,128]{1,0:T(8,128)} %dual0), channel_id=1, source_target_pairs={{0,1},{1,2},{2,3},{3,0},{4,5},{5,6},{6,7},{7,4},{8,9},{9,10},{10,1... | collective-permute-start | bytes 49160 | tf_op jit(solution)/shard_map/ppermute | solution.py:478
  4.9 10.8 %collective-permute-start.2 = (f32[32,128]{1,0:T(8,128)}, f32[32,128]{1,0:T(8,128)S(1)}, u32[]{:S(2)}, u32[]{:S(2)}) collective-permute-start(f32[32,128]{1,0:T(8,128)} %dual0), channel_id=1, source_target_pairs={{0,3},{1,0},{2,1},{3,2},{4,7},{5,4},{6,5},{7,6},{8,11},{9,8},{10,9... | collective-permute-start | bytes 49160 | tf_op jit(solution)/shard_map/ppermute | solution.py:478
  15.7 5.7 %collective-permute-start.3 = (f32[64,64,128]{2,1,0:T(8,128)S(1)}, f32[64,64,128]{2,1,0:T(8,128)S(1)}, u32[]{:S(2)}, u32[]{:S(2)}) collective-permute-start(f32[64,64,128]{2,1,0:T(8,128)S(1)} %get-tuple-element.42), channel_id=1, source_target_pairs={{0,4},{4,0},{1,5},{5,1},{2,6},{6,2},{3,7},{7,3},{8,12},{12,8},{9,1... | collective-permute-start | bytes 6291464 | tf_op jit(solution)/shard_map/ppermute | solution.py:485
  20.0 1.4 collective-permute-start.4
  21.6 39.2 %copy-start.4 = (f32[32,128]{1,0:T(8,128)S(1)}, f32[32,128]{1,0:T(8,128)}, u32[]{:S(2)}) copy-start(f32[32,128]{1,0:T(8,128)} %demand.1) | copy-start | bytes 49156

commit v4 on v3

--- a/solution.py
+++ b/solution.py
@@ -57,6 +57,9 @@
     both = jnp.concatenate([high, low], axis=0)
     full = lax.dot_general(both, both, NT, preferred_element_type=jnp.float32)
     return (full[:N, :N] + full[N:, N:]) + (full[:N, N:] + full[N:, :N])
+
+
+CHUNKS = (0, 2, 6)
 
 
 def gram_kernel(
@@ -69,8 +72,11 @@
         pltpu.make_async_copy(primal_in, primal, sem.at[2]),
         pltpu.make_async_copy(slack_in, slack, sem.at[3]),
     ]
-    big = [pltpu.make_async_copy(coeffs_in.at[g], coeffs.at[g], tile_sem.at[g]) for g in range(GROUPS)]
-    for copy in little + big:
+    big = {}
+    for k, g in enumerate(CHUNKS):
+        part = pl.ds(g, (CHUNKS + (GROUPS,))[k + 1] - g)
+        big[g] = pltpu.make_async_copy(coeffs_in.at[part], coeffs.at[part], tile_sem.at[k])
+    for copy in little + list(big.values()):
         copy.start()
     acc[...] = jnp.zeros_like(acc)
     small[...] = jnp.zeros_like(small)
@@ -87,7 +93,8 @@
         scale = jnp.where(line_lane < counts[g], primal[g : g + 1, :] / slack[g : g + 1, :], 0.0)
         root_out[g : g + 1, :] = jnp.sqrt(scale)
     for g in range(GROUPS):
-        big[g].wait()
+        if g in big:
+            big[g].wait()
         root = root_out[g : g + 1, :]
         for s in range(SPAN):
             high, low = split(coeffs[g, s] * root)
@@ -97,7 +104,7 @@
             packed = jnp.where(lower, gram[:HALF], rolled)
             line = jnp.sum(jnp.where(row == lane, rolled, 0.0), axis=0, keepdims=True)
             block = ids[s, g]
-            chip = ((block >> 3) << 2) | (block & 3)
+            chip = (((block >> 3) & 3) << 4) | ((block & 3) << 2) | (block >> 5)
             place = (((block >> 2) & 1) ^ core) * HALF + chip
             acc[place] += packed
             small[pl.ds(place * EXTRA, 1), :] += line
@@ -314,7 +321,7 @@
 
     total = lax.fori_loop(1, HALF // 2, add, got[0 : 2 * ROWS, :], unroll=True)
     total = total[:ROWS] + total[ROWS:]
-    odd = (lax.axis_index("z") & 1) == 1
+    odd = (lax.axis_index("leg") & 1) == 1
     packed = jnp.where(odd, total[EXTRA:], total[:HALF])
     tail = jnp.where(odd, total[:EXTRA], total[HALF:])
     line = tail[0:1]
@@ -464,7 +471,7 @@
 
 
 ALL = ("leg", "x", "core", "z")
-CHIPS = ("leg", "x", "z")
+CHIPS = ("x", "z", "leg")
 
 
 def exchange(rows, axes):

time: 159 us -> 155 us (0.975)
  Pallas kernels: 23.6 us -> 19.7 us
    pallas_call x1, Pallas kernels: 8.47 us -> 4.57 us  [run_gram(): pl.pallas_call(gram_kernel, out_shape=(jax.ShapeDtypeStruct((GROUPS, SPAN...]
  transfers between devices with their start and end apart: 5 -> 5, of which waited for: 1 -> 1; matrix products, arithmetic and copies ran while one was open for 0% -> 0% of each run, Pallas kernels for 7% -> 5%
where the time goes in v4:
time: 155 us
  blocking collectives  125 us (81%)
  Pallas kernels  19.7 us (13%)
  starting transfers between devices  8.21 us (5%)
    all_to_all x7, blocking collectives, exchange(): return lax.all_to_all(rows, axes, split_axis=0, concat_axis=0, tiled=True)  125 us
    pallas_call x3, Pallas kernels, run_tile(): pl.pallas_call(kernel, out_shape=(f32(N, N), f32(GROUPS, N), f32(8, N), f...  6.53 us
    ppermute x3, starting transfers between devices, per_device(): lax.ppermute(duals, 'leg', [(i, (i + k) % 4) for i in range(4)])  6.5 us
    pallas_call x1, Pallas kernels, run_gram(): pl.pallas_call(gram_kernel, out_shape=(jax.ShapeDtypeStruct((GROUPS, SPAN...  4.57 us
    pallas_call x1, Pallas kernels, run_first(): pl.pallas_call(first_kernel, out_shape=(f32(N, N), f32(8, N), f32(8, N),...  4.35 us
  transfers between devices with their start and end apart: 5, of which 1 were waited for; matrix products, arithmetic and copies ran while one was open for 0% of the time, Pallas kernels for 5%

profile of v4, /device:TPU:1, one launch (start us, length us, event | category | flops | bytes accessed | tf_op | source)
XLA Modules:
  0.0 154.8 jit_solution(4154385492138859693)
XLA Ops:
  0.6 0.0 copy-start.3
  0.6 0.0 copy-start.2
  0.7 0.0 copy-start.1
  0.7 0.0 copy-start.6
  0.7 0.0 copy-start
  0.7 0.0 copy-start.5
  0.7 3.8 %collective-permute-start.1 = (f32[32,128]{1,0:T(8,128)}, f32[32,128]{1,0:T(8,128)S(1)}, u32[]{:S(2)}, u32[]{:S(2)}) collective-permute-start(f32[32,128]{1,0:T(8,128)} %dual0), channel_id=1, source_target_pairs={{0,2},{1,3},{2,0},{3,1},{4,6},{5,7},{6,4},{7,5},{8,10},{9,11},{10,... | collective-permute-start | bytes 49160 | tf_op jit(solution)/shard_map/ppermute | solution.py:485
  4.5 0.4 collective-permute-start
  4.9 2.3 %collective-permute-start.2 = (f32[32,128]{1,0:T(8,128)}, f32[32,128]{1,0:T(8,128)S(1)}, u32[]{:S(2)}, u32[]{:S(2)}) collective-permute-start(f32[32,128]{1,0:T(8,128)} %dual0), channel_id=1, source_target_pairs={{0,3},{1,0},{2,1},{3,2},{4,7},{5,4},{6,5},{7,6},{8,11},{9,8},{10,9... | collective-permute-start | bytes 49160 | tf_op jit(solution)/shard_map/ppermute | solution.py:485
  7.2 4.6 %gram.1 = (bf16[16,512,256]{2,1,0:T(8,128)(2,1)S(1)}, f32[128,64,128]{2,1,0:T(8,128)S(1)}, f32[64,64,128]{2,1,0:T(8,128)S(1)}, f32[512,128]{1,0:T(8,128)S(1)}, f...) custom-call(f32[16,4,128,128]{3,2,1,0:T(8,128)} %coeffs_in.1, s32[4,16]{1,0:T(4,128)} %bitcast.31, ...), custom_call_target="tpu_custom_call" | custom-call | flops 1073741824 | bytes 12582912 | tf_op jit(solution)/shard_map/gram/pallas_call | solution.py:120
  11.8 0.0 collective-permute-done.1.dual2
  11.8 0.0 collective-permute-done.dual1
  11.8 0.0 collective-permute-done.2.dual3
  11.8 1.6 %collective-permute-start.3 = (f32[64,64,128]{2,1,0:T(8,128)S(1)}, f32[64,64,128]{2,1,0:T(8,128)S(1)}, u32[]{:S(2)}, u32[]{:S(2)}) collective-permute-start(f32[64,64,128]{2,1,0:T(8,128)S(1)} %get-tuple-element.42), channel_id=1, source_target_pairs={{0,4},{4,0},{1,5},{5,1},{2,6},{6,2},{3,7},{7,3},{8,12},{12,8},{9,1... | collective-permute-start | bytes 6291464 | tf_op jit(solution)/shard_map/ppermute | solution.py:492
  13.4 0.0 copy-done.3
  13.4 0.0 copy-done.2
  13.4 0.0 copy-done.1
  13.4 0.0 copy-done.6
  13.4 0.0 copy-done
  13.4 0.0 copy-done.5
  13.4 2.6 %rhs.1 = (f32[256,128]{1,0:T(8,128)S(1)}, f32[256,128]{1,0:T(8,128)S(1)}, f32[16,128]{1,0:T(8,128)S(1)}, f32[16,128]{1,0:T(8,128)S(1)}) custom-call(s32[4,16]{1,0:T(4,128)S(1)} %bitcast.32, s32[16]{0:T(128)S(1)} %copy-done.6, bf16[128,128]{1,0:T(8,128)(2,1)S(1)} %get-tuple-element.43.hot_place, bf16[16,512,256]{2,1,0:T(8,128)(2,1)S(1)} %get-tuple-element.39.tiles.refs_2_, ...), custom_call_target="tpu_custom_call" | custom-call | flops 134217728 | bytes 6291456 | tf_op jit(solution)/shard_map/rhs/pallas_call | solution.py:226
  16.1 0.1 collective-permute-start.4
  16.2 1.3 collective-permute-done.4.small_got
  17.5 0.0 collective-permute-done.3.got
  17.5 0.2 join.1
  17.7 0.0 copy-start.4
  17.7 39.0 %all_to_all.71 = f32[1088,4,128]{2,1,0:T(4,128)S(1)} all-to-all(f32[1088,4,128]{2,1,0:T(4,128)S(1)} %bitcast.18), channel_id=1, replica_groups=mesh['x'=4,'z'=4,'core'=2,'leg'=4] {'x','z','leg'}, dimensions={0} | all-to-all | bytes 4456448 | tf_op jit(solution)/shard_map/all_to_all | solution.py:478
  56.7 0.0 copy-done.4
  56.7 4.4 %first.1 = (f32[128,128]{1,0:T(8,128)S(1)}, f32[8,128]{1,0:T(8,128)S(1)}, f32[8,128]{1,0:T(8,128)S(1)}, f32[256,128]{1,0:T(8,128)S(1)}) custom-call(f32[4352,128]{1,0:T(8,128)S(1)} %bitcast.17, f32[32,128]{1,0:T(8,128)S(1)} %copy-done.4), custom_call_target="tpu_custom_call" | custom-call | tf_op jit(solution)/shard_map/first/pallas_call | solution.py:360
  61.1 15.8 %all_to_all.72 = f32[128,2,128]{2,1,0:T(2,128)S(1)} all-to-all(f32[128,2,128]{2,1,0:T(2,128)S(1)} %bitcast.25), channel_id=1, replica_groups=mesh['x'=4,'z'=4,'core'=2,'leg'=4] {'leg','x','core','z'}, dimensions={0} | all-to-all | bytes 262144 | tf_op jit(solution)/shard_map/all_to_all | solution.py:478
  76.8 2.6 %tile.2 = (f32[128,128]{1,0:T(8,128)S(1)}, f32[16,128]{1,0:T(8,128)S(1)}, f32[8,128]{1,0:T(8,128)S(1)}, f32[256,128]{1,0:T(8,128)S(1)}) custom-call(s32[4,16]{1,0:T(4,128)S(1)} %bitcast.33, bf16[128,128]{1,0:T(8,128)(2,1)S(1)} %get-tuple-element.38.refs_1_, bf16[16,512,256]{2,1,0:T(8,128)(2,1)S(1)} %get-tuple-element.39.tiles.refs_2_, f32[256,128]{1,0:T(8,128)S(1)} %bitcast.20), custom_call_target="tpu_custom_call" | custom-call | tf_op jit(solution)/shard_map/tile/pallas_call | solution.py:437
  79.5 14.1 %all_to_all.73 = f32[128,2,128]{2,1,0:T(2,128)S(1)} all-to-all(f32[128,2,128]{2,1,0:T(2,128)S(1)} %bitcast.26), channel_id=1, replica_groups=mesh['x'=4,'z'=4,'core'=2,'leg'=4] {'leg','x','core','z'}, dimensions={0} | all-to-all | bytes 262144 | tf_op jit(solution)/shard_map/all_to_all | solution.py:478
  93.6 0.4 owner.2
  93.9 14.1 %all_to_all.74 = f32[128,2,128]{2,1,0:T(2,128)S(1)} all-to-all(f32[128,2,128]{2,1,0:T(2,128)S(1)} %bitcast.28), channel_id=1, replica_groups=mesh['x'=4,'z'=4,'core'=2,'leg'=4] {'leg','x','core','z'}, dimensions={0} | all-to-all | bytes 262144 | tf_op jit(solution)/shard_map/all_to_all | solution.py:478
  108.0 2.6 %tile.3 = (f32[128,128]{1,0:T(8,128)S(1)}, f32[16,128]{1,0:T(8,128)S(1)}, f32[8,128]{1,0:T(8,128)S(1)}, f32[256,128]{1,0:T(8,128)S(1)}) custom-call(s32[4,16]{1,0:T(4,128)S(1)} %bitcast.34, bf16[128,128]{1,0:T(8,128)(2,1)S(1)} %get-tuple-element.38.refs_1_, bf16[16,512,256]{2,1,0:T(8,128)(2,1)S(1)} %get-tuple-element.39.tiles.refs_2_, ...), custom_call_target="tpu_custom_call" | custom-call | tf_op jit(solution)/shard_map/tile/pallas_call | solution.py:437
  110.7 14.1 %all_to_all.75 = f32[128,2,128]{2,1,0:T(2,128)S(1)} all-to-all(f32[128,2,128]{2,1,0:T(2,128)S(1)} %bitcast.27), channel_id=1, replica_groups=mesh['x'=4,'z'=4,'core'=2,'leg'=4] {'leg','x','core','z'}, dimensions={0} | all-to-all | bytes 262144 | tf_op jit(solution)/shard_map/all_to_all | solution.py:478
  124.8 0.4 owner.3
  125.1 14.1 %all_to_all.76 = f32[128,2,128]{2,1,0:T(2,128)S(1)} all-to-all(f32[128,2,128]{2,1,0:T(2,128)S(1)} %bitcast.29), channel_id=1, replica_groups=mesh['x'=4,'z'=4,'core'=2,'leg'=4] {'leg','x','core','z'}, dimensions={0} | all-to-all | bytes 262144 | tf_op jit(solution)/shard_map/all_to_all | solution.py:478
  139.2 1.3 tile_last.1
  140.5 13.6 %all_to_all.77 = f32[128,1,128]{2,1,0:T(1,128)S(1)} all-to-all(f32[128,1,128]{2,1,0:T(1,128)S(1)} %bitcast.30), channel_id=1, replica_groups=mesh['x'=4,'z'=4,'core'=2,'leg'=4] {'leg','x','core','z'}, dimensions={0} | all-to-all | bytes 131072 | tf_op jit(solution)/shard_map/all_to_all | solution.py:478
  154.1 0.7 final.1
Async XLA Ops:
  0.6 12.8 %copy-start.3 = (f32[32,128]{1,0:T(8,128)S(1)}, f32[32,128]{1,0:T(8,128)}, u32[]{:S(2)}) copy-start(f32[32,128]{1,0:T(8,128)} %dual0) | copy-start | bytes 49156
  0.6 12.8 %copy-start.2 = (f32[16,128]{1,0:T(8,128)S(1)}, f32[16,128]{1,0:T(8,128)}, u32[]{:S(2)}) copy-start(f32[16,128]{1,0:T(8,128)} %slack.1) | copy-start | bytes 24580
  0.7 12.8 %copy-start.1 = (f32[16,128]{1,0:T(8,128)S(1)}, f32[16,128]{1,0:T(8,128)}, u32[]{:S(2)}) copy-start(f32[16,128]{1,0:T(8,128)} %primal.1) | copy-start | bytes 24580
  0.7 12.7 %copy-start.6 = (s32[16]{0:T(128)S(1)}, s32[16]{0:T(128)}, u32[]{:S(2)}) copy-start(s32[16]{0:T(128)} %counts.1) | copy-start | bytes 196
  0.7 12.7 %copy-start = (s32[16,4]{0,1:T(4,128)S(1)}, s32[16,4]{0,1:T(4,128)}, u32[]{:S(2)}) copy-start(s32[16,4]{0,1:T(4,128)} %param.9) | copy-start | bytes 772
  0.7 12.7 %copy-start.5 = (f32[16,128]{1,0:T(8,128)S(1)}, f32[16,128]{1,0:T(8,128)}, u32[]{:S(2)}) copy-start(f32[16,128]{1,0:T(8,128)} %cost.1) | copy-start | bytes 24580
  0.7 11.1 %collective-permute-start.1 = (f32[32,128]{1,0:T(8,128)}, f32[32,128]{1,0:T(8,128)S(1)}, u32[]{:S(2)}, u32[]{:S(2)}) collective-permute-start(f32[32,128]{1,0:T(8,128)} %dual0), channel_id=1, source_target_pairs={{0,2},{1,3},{2,0},{3,1},{4,6},{5,7},{6,4},{7,5},{8,10},{9,11},{10,... | collective-permute-start | bytes 49160 | tf_op jit(solution)/shard_map/ppermute | solution.py:485
  4.5 7.3 %collective-permute-start = (f32[32,128]{1,0:T(8,128)}, f32[32,128]{1,0:T(8,128)S(1)}, u32[]{:S(2)}, u32[]{:S(2)}) collective-permute-start(f32[32,128]{1,0:T(8,128)} %dual0), channel_id=1, source_target_pairs={{0,1},{1,2},{2,3},{3,0},{4,5},{5,6},{6,7},{7,4},{8,9},{9,10},{10,1... | collective-permute-start | bytes 49160 | tf_op jit(solution)/shard_map/ppermute | solution.py:485
  4.9 6.9 %collective-permute-start.2 = (f32[32,128]{1,0:T(8,128)}, f32[32,128]{1,0:T(8,128)S(1)}, u32[]{:S(2)}, u32[]{:S(2)}) collective-permute-start(f32[32,128]{1,0:T(8,128)} %dual0), channel_id=1, source_target_pairs={{0,3},{1,0},{2,1},{3,2},{4,7},{5,4},{6,5},{7,6},{8,11},{9,8},{10,9... | collective-permute-start | bytes 49160 | tf_op jit(solution)/shard_map/ppermute | solution.py:485
  11.8 5.7 %collective-permute-start.3 = (f32[64,64,128]{2,1,0:T(8,128)S(1)}, f32[64,64,128]{2,1,0:T(8,128)S(1)}, u32[]{:S(2)}, u32[]{:S(2)}) collective-permute-start(f32[64,64,128]{2,1,0:T(8,128)S(1)} %get-tuple-element.42), channel_id=1, source_target_pairs={{0,4},{4,0},{1,5},{5,1},{2,6},{6,2},{3,7},{7,3},{8,12},{12,8},{9,1... | collective-permute-start | bytes 6291464 | tf_op jit(solution)/shard_map/ppermute | solution.py:492
  16.1 1.4 collective-permute-start.4
  17.7 39.0 %copy-start.4 = (f32[32,128]{1,0:T(8,128)S(1)}, f32[32,128]{1,0:T(8,128)}, u32[]{:S(2)}) copy-start(f32[32,128]{1,0:T(8,128)} %demand.1) | copy-start | bytes 49156

commit v5 on v4

--- a/solution.py
+++ b/solution.py
@@ -169,7 +169,17 @@
         high, low = split(w)
         lines.append(jnp.concatenate([high, high], axis=1))
         lines.append(jnp.concatenate([low, jnp.zeros_like(low)], axis=1))
+    every = len(colvecs) + 1
     for g in range(GROUPS):
+        if g % every == every - 1:
+            for s in range(SPAN):
+                t = g * SPAN + s
+                pair = tiles[g, s * N : (s + 1) * N, :].astype(jnp.float32)
+                tile = pair[:, :N] + pair[:, N:]
+                for w, out in zip(colvecs, outs):
+                    turned = jnp.transpose(tile * w[g : g + 1])
+                    out[t : t + 1, :] = jnp.sum(turned, axis=0, keepdims=True)
+            continue
         both = jnp.concatenate([line[g : g + 1] for line in lines], axis=0)
         full = lax.dot_general(both, tiles[g], NT, preferred_element_type=jnp.float32)
         for k, out in enumerate(outs):

time: 155 us -> 154 us (level)
  transfers between devices with their start and end apart: 5 -> 5, of which waited for: 1 -> 1; matrix products, arithmetic and copies ran while one was open for 0% -> 0% of each run, Pallas kernels for 5% -> 4%
where the time goes in v5:
time: 154 us; the launch traced here: 153 us
  blocking collectives  124 us (81%)
  Pallas kernels  18.3 us (12%)
  starting transfers between devices  8.21 us (5%)
    all_to_all x7, blocking collectives, exchange(): return lax.all_to_all(rows, axes, split_axis=0, concat_axis=0, tiled=True)  124 us
    ppermute x3, starting transfers between devices, per_device(): lax.ppermute(duals, 'leg', [(i, (i + k) % 4) for i in range(4)])  6.5 us
    pallas_call x3, Pallas kernels, run_tile(): pl.pallas_call(kernel, out_shape=(f32(N, N), f32(GROUPS, N), f32(8, N), f...  5.44 us
    pallas_call x1, Pallas kernels, run_gram(): pl.pallas_call(gram_kernel, out_shape=(jax.ShapeDtypeStruct((GROUPS, SPAN...  4.56 us
    pallas_call x1, Pallas kernels, run_first(): pl.pallas_call(first_kernel, out_shape=(f32(N, N), f32(8, N), f32(8, N),...  4.35 us
  transfers between devices with their start and end apart: 5, of which 1 were waited for; matrix products, arithmetic and copies ran while one was open for 0% of the time, Pallas kernels for 4%

profile of v5, /device:TPU:1, one launch (start us, length us, event | category | flops | bytes accessed | tf_op | source)
XLA Modules:
  0.0 153.3 jit_solution(14834245396077284210)
XLA Ops:
  0.6 0.0 copy-start.3
  0.6 0.0 copy-start.2
  0.7 0.0 copy-start.1
  0.7 0.0 copy-start.6
  0.7 0.0 copy-start
  0.7 0.0 copy-start.5
  0.7 3.8 %collective-permute-start.1 = (f32[32,128]{1,0:T(8,128)}, f32[32,128]{1,0:T(8,128)S(1)}, u32[]{:S(2)}, u32[]{:S(2)}) collective-permute-start(f32[32,128]{1,0:T(8,128)} %dual0), channel_id=1, source_target_pairs={{0,2},{1,3},{2,0},{3,1},{4,6},{5,7},{6,4},{7,5},{8,10},{9,11},{10,... | collective-permute-start | bytes 49160 | tf_op jit(solution)/shard_map/ppermute | solution.py:495
  4.5 0.4 collective-permute-start
  4.9 2.3 %collective-permute-start.2 = (f32[32,128]{1,0:T(8,128)}, f32[32,128]{1,0:T(8,128)S(1)}, u32[]{:S(2)}, u32[]{:S(2)}) collective-permute-start(f32[32,128]{1,0:T(8,128)} %dual0), channel_id=1, source_target_pairs={{0,3},{1,0},{2,1},{3,2},{4,7},{5,4},{6,5},{7,6},{8,11},{9,8},{10,9... | collective-permute-start | bytes 49160 | tf_op jit(solution)/shard_map/ppermute | solution.py:495
  7.2 4.6 %gram.1 = (bf16[16,512,256]{2,1,0:T(8,128)(2,1)S(1)}, f32[128,64,128]{2,1,0:T(8,128)S(1)}, f32[64,64,128]{2,1,0:T(8,128)S(1)}, f32[512,128]{1,0:T(8,128)S(1)}, f...) custom-call(f32[16,4,128,128]{3,2,1,0:T(8,128)} %coeffs_in.1, s32[4,16]{1,0:T(4,128)} %bitcast.31, ...), custom_call_target="tpu_custom_call" | custom-call | flops 1073741824 | bytes 12582912 | tf_op jit(solution)/shard_map/gram/pallas_call | solution.py:120
  11.8 0.0 collective-permute-done.1.dual2
  11.8 0.0 collective-permute-done.dual1
  11.8 0.0 collective-permute-done.2.dual3
  11.8 1.6 %collective-permute-start.3 = (f32[64,64,128]{2,1,0:T(8,128)S(1)}, f32[64,64,128]{2,1,0:T(8,128)S(1)}, u32[]{:S(2)}, u32[]{:S(2)}) collective-permute-start(f32[64,64,128]{2,1,0:T(8,128)S(1)} %get-tuple-element.42), channel_id=1, source_target_pairs={{0,4},{4,0},{1,5},{5,1},{2,6},{6,2},{3,7},{7,3},{8,12},{12,8},{9,1... | collective-permute-start | bytes 6291464 | tf_op jit(solution)/shard_map/ppermute | solution.py:502
  13.4 0.0 copy-done.3
  13.4 0.0 copy-done.2
  13.4 0.0 copy-done.1
  13.4 0.0 copy-done.6
  13.4 0.0 copy-done
  13.4 0.0 copy-done.5
  13.4 2.3 %rhs.1 = (f32[256,128]{1,0:T(8,128)S(1)}, f32[256,128]{1,0:T(8,128)S(1)}, f32[16,128]{1,0:T(8,128)S(1)}, f32[16,128]{1,0:T(8,128)S(1)}) custom-call(s32[4,16]{1,0:T(4,128)S(1)} %bitcast.32, s32[16]{0:T(128)S(1)} %copy-done.6, bf16[128,128]{1,0:T(8,128)(2,1)S(1)} %get-tuple-element.43.hot_place, bf16[16,512,256]{2,1,0:T(8,128)(2,1)S(1)} %get-tuple-element.39.tiles.refs_2_, ...), custom_call_target="tpu_custom_call" | custom-call | flops 134217728 | bytes 6291456 | tf_op jit(solution)/shard_map/rhs/pallas_call | solution.py:236
  15.7 0.1 collective-permute-start.4
  15.8 1.5 collective-permute-done.4.small_got
  17.4 0.0 collective-permute-done.3.got
  17.4 0.2 join.1
  17.6 0.0 copy-start.4
  17.6 39.0 %all_to_all.71 = f32[1088,4,128]{2,1,0:T(4,128)S(1)} all-to-all(f32[1088,4,128]{2,1,0:T(4,128)S(1)} %bitcast.18), channel_id=1, replica_groups=mesh['x'=4,'z'=4,'core'=2,'leg'=4] {'x','z','leg'}, dimensions={0} | all-to-all | bytes 4456448 | tf_op jit(solution)/shard_map/all_to_all | solution.py:488
  56.6 0.0 copy-done.4
  56.6 4.4 %first.1 = (f32[128,128]{1,0:T(8,128)S(1)}, f32[8,128]{1,0:T(8,128)S(1)}, f32[8,128]{1,0:T(8,128)S(1)}, f32[256,128]{1,0:T(8,128)S(1)}) custom-call(f32[4352,128]{1,0:T(8,128)S(1)} %bitcast.17, f32[32,128]{1,0:T(8,128)S(1)} %copy-done.4), custom_call_target="tpu_custom_call" | custom-call | tf_op jit(solution)/shard_map/first/pallas_call | solution.py:370
  61.0 15.5 %all_to_all.72 = f32[128,2,128]{2,1,0:T(2,128)S(1)} all-to-all(f32[128,2,128]{2,1,0:T(2,128)S(1)} %bitcast.25), channel_id=1, replica_groups=mesh['x'=4,'z'=4,'core'=2,'leg'=4] {'leg','x','core','z'}, dimensions={0} | all-to-all | bytes 262144 | tf_op jit(solution)/shard_map/all_to_all | solution.py:488
  76.5 2.1 %tile.2 = (f32[128,128]{1,0:T(8,128)S(1)}, f32[16,128]{1,0:T(8,128)S(1)}, f32[8,128]{1,0:T(8,128)S(1)}, f32[256,128]{1,0:T(8,128)S(1)}) custom-call(s32[4,16]{1,0:T(4,128)S(1)} %bitcast.33, bf16[128,128]{1,0:T(8,128)(2,1)S(1)} %get-tuple-element.38.refs_1_, bf16[16,512,256]{2,1,0:T(8,128)(2,1)S(1)} %get-tuple-element.39.tiles.refs_2_, f32[256,128]{1,0:T(8,128)S(1)} %bitcast.20), custom_call_target="tpu_custom_call" | custom-call | tf_op jit(solution)/shard_map/tile/pallas_call | solution.py:447
  78.5 14.1 %all_to_all.73 = f32[128,2,128]{2,1,0:T(2,128)S(1)} all-to-all(f32[128,2,128]{2,1,0:T(2,128)S(1)} %bitcast.26), channel_id=1, replica_groups=mesh['x'=4,'z'=4,'core'=2,'leg'=4] {'leg','x','core','z'}, dimensions={0} | all-to-all | bytes 262144 | tf_op jit(solution)/shard_map/all_to_all | solution.py:488
  92.6 0.4 owner.2
  93.0 14.1 %all_to_all.74 = f32[128,2,128]{2,1,0:T(2,128)S(1)} all-to-all(f32[128,2,128]{2,1,0:T(2,128)S(1)} %bitcast.28), channel_id=1, replica_groups=mesh['x'=4,'z'=4,'core'=2,'leg'=4] {'leg','x','core','z'}, dimensions={0} | all-to-all | bytes 262144 | tf_op jit(solution)/shard_map/all_to_all | solution.py:488
  107.1 2.1 %tile.3 = (f32[128,128]{1,0:T(8,128)S(1)}, f32[16,128]{1,0:T(8,128)S(1)}, f32[8,128]{1,0:T(8,128)S(1)}, f32[256,128]{1,0:T(8,128)S(1)}) custom-call(s32[4,16]{1,0:T(4,128)S(1)} %bitcast.34, bf16[128,128]{1,0:T(8,128)(2,1)S(1)} %get-tuple-element.38.refs_1_, bf16[16,512,256]{2,1,0:T(8,128)(2,1)S(1)} %get-tuple-element.39.tiles.refs_2_, ...), custom_call_target="tpu_custom_call" | custom-call | tf_op jit(solution)/shard_map/tile/pallas_call | solution.py:447
  109.2 14.1 %all_to_all.75 = f32[128,2,128]{2,1,0:T(2,128)S(1)} all-to-all(f32[128,2,128]{2,1,0:T(2,128)S(1)} %bitcast.27), channel_id=1, replica_groups=mesh['x'=4,'z'=4,'core'=2,'leg'=4] {'leg','x','core','z'}, dimensions={0} | all-to-all | bytes 262144 | tf_op jit(solution)/shard_map/all_to_all | solution.py:488
  123.3 0.4 owner.3
  123.6 14.1 %all_to_all.76 = f32[128,2,128]{2,1,0:T(2,128)S(1)} all-to-all(f32[128,2,128]{2,1,0:T(2,128)S(1)} %bitcast.29), channel_id=1, replica_groups=mesh['x'=4,'z'=4,'core'=2,'leg'=4] {'leg','x','core','z'}, dimensions={0} | all-to-all | bytes 262144 | tf_op jit(solution)/shard_map/all_to_all | solution.py:488
  137.7 1.3 tile_last.1
  139.0 13.6 %all_to_all.77 = f32[128,1,128]{2,1,0:T(1,128)S(1)} all-to-all(f32[128,1,128]{2,1,0:T(1,128)S(1)} %bitcast.30), channel_id=1, replica_groups=mesh['x'=4,'z'=4,'core'=2,'leg'=4] {'leg','x','core','z'}, dimensions={0} | all-to-all | bytes 131072 | tf_op jit(solution)/shard_map/all_to_all | solution.py:488
  152.6 0.7 final.1
Async XLA Ops:
  0.6 12.8 %copy-start.3 = (f32[32,128]{1,0:T(8,128)S(1)}, f32[32,128]{1,0:T(8,128)}, u32[]{:S(2)}) copy-start(f32[32,128]{1,0:T(8,128)} %dual0) | copy-start | bytes 49156
  0.6 12.8 %copy-start.2 = (f32[16,128]{1,0:T(8,128)S(1)}, f32[16,128]{1,0:T(8,128)}, u32[]{:S(2)}) copy-start(f32[16,128]{1,0:T(8,128)} %slack.1) | copy-start | bytes 24580
  0.7 12.7 %copy-start.1 = (f32[16,128]{1,0:T(8,128)S(1)}, f32[16,128]{1,0:T(8,128)}, u32[]{:S(2)}) copy-start(f32[16,128]{1,0:T(8,128)} %primal.1) | copy-start | bytes 24580
  0.7 12.7 %copy-start.6 = (s32[16]{0:T(128)S(1)}, s32[16]{0:T(128)}, u32[]{:S(2)}) copy-start(s32[16]{0:T(128)} %counts.1) | copy-start | bytes 196
  0.7 12.7 %copy-start = (s32[16,4]{0,1:T(4,128)S(1)}, s32[16,4]{0,1:T(4,128)}, u32[]{:S(2)}) copy-start(s32[16,4]{0,1:T(4,128)} %param.9) | copy-start | bytes 772
  0.7 12.7 %copy-start.5 = (f32[16,128]{1,0:T(8,128)S(1)}, f32[16,128]{1,0:T(8,128)}, u32[]{:S(2)}) copy-start(f32[16,128]{1,0:T(8,128)} %cost.1) | copy-start | bytes 24580
  0.7 11.1 %collective-permute-start.1 = (f32[32,128]{1,0:T(8,128)}, f32[32,128]{1,0:T(8,128)S(1)}, u32[]{:S(2)}, u32[]{:S(2)}) collective-permute-start(f32[32,128]{1,0:T(8,128)} %dual0), channel_id=1, source_target_pairs={{0,2},{1,3},{2,0},{3,1},{4,6},{5,7},{6,4},{7,5},{8,10},{9,11},{10,... | collective-permute-start | bytes 49160 | tf_op jit(solution)/shard_map/ppermute | solution.py:495
  4.5 7.3 %collective-permute-start = (f32[32,128]{1,0:T(8,128)}, f32[32,128]{1,0:T(8,128)S(1)}, u32[]{:S(2)}, u32[]{:S(2)}) collective-permute-start(f32[32,128]{1,0:T(8,128)} %dual0), channel_id=1, source_target_pairs={{0,1},{1,2},{2,3},{3,0},{4,5},{5,6},{6,7},{7,4},{8,9},{9,10},{10,1... | collective-permute-start | bytes 49160 | tf_op jit(solution)/shard_map/ppermute | solution.py:495
  4.9 6.9 %collective-permute-start.2 = (f32[32,128]{1,0:T(8,128)}, f32[32,128]{1,0:T(8,128)S(1)}, u32[]{:S(2)}, u32[]{:S(2)}) collective-permute-start(f32[32,128]{1,0:T(8,128)} %dual0), channel_id=1, source_target_pairs={{0,3},{1,0},{2,1},{3,2},{4,7},{5,4},{6,5},{7,6},{8,11},{9,8},{10,9... | collective-permute-start | bytes 49160 | tf_op jit(solution)/shard_map/ppermute | solution.py:495
  11.8 5.6 %collective-permute-start.3 = (f32[64,64,128]{2,1,0:T(8,128)S(1)}, f32[64,64,128]{2,1,0:T(8,128)S(1)}, u32[]{:S(2)}, u32[]{:S(2)}) collective-permute-start(f32[64,64,128]{2,1,0:T(8,128)S(1)} %get-tuple-element.42), channel_id=1, source_target_pairs={{0,4},{4,0},{1,5},{5,1},{2,6},{6,2},{3,7},{7,3},{8,12},{12,8},{9,1... | collective-permute-start | bytes 6291464 | tf_op jit(solution)/shard_map/ppermute | solution.py:502
  15.7 1.6 %collective-permute-start.4 = (f32[256,128]{1,0:T(8,128)S(1)}, f32[256,128]{1,0:T(8,128)S(1)}, u32[]{:S(2)}, u32[]{:S(2)}) collective-permute-start(f32[256,128]{1,0:T(8,128)S(1)} %get-tuple-element.51), channel_id=1, source_target_pairs={{0,4},{4,0},{1,5},{5,1},{2,6},{6,2},{3,7},{7,3},{8,12},{12,8},{9,1... | collective-permute-start | bytes 393224 | tf_op jit(solution)/shard_map/ppermute | solution.py:506
  17.6 39.0 %copy-start.4 = (f32[32,128]{1,0:T(8,128)S(1)}, f32[32,128]{1,0:T(8,128)}, u32[]{:S(2)}) copy-start(f32[32,128]{1,0:T(8,128)} %demand.1) | copy-start | bytes 49156

commit v6 on v5

--- a/solution.py
+++ b/solution.py
@@ -5,7 +5,6 @@
 from jax.experimental.pallas import tpu as pltpu
 from jax.sharding import Mesh, PartitionSpec as P
 
-ITERS = 3
 SIGMA = 0.3
 REGULAR = 1.0
 PRECISE = lax.Precision.HIGHEST
@@ -316,16 +315,24 @@
     return panels
 
 
-def pair_rows(first, second):
-    return jnp.where((iota((8, N), 0) & 1) == 0, first, second)
-
-
-def set_message(msg, line, scalar):
-    pair = pair_rows(jnp.broadcast_to(line, (8, N)), jnp.broadcast_to(scalar, (8, N)))
-    msg[...] = jnp.broadcast_to(pair[None], (N // 4, 8, N)).reshape(2 * N, N)
-
-
-def first_kernel(got, demand, inverse_out, residual_out, mu_out, msg):
+RESIDUAL, SMOOTHED, DIRECTION, IMAGE, PART, NORM, CURVE, STEP, BETA = range(9)
+KEPT = 16
+
+
+def total_of(line):
+    return jnp.sum(line, axis=1, keepdims=True)
+
+
+def smooth(residual, inverse):
+    return jnp.dot(
+        jnp.broadcast_to(residual, (8, N)),
+        inverse,
+        precision=PRECISE,
+        preferred_element_type=jnp.float32,
+    )[0:1]
+
+
+def first_kernel(got, demand, inverse_out, kept, mu_out, msg):
     def add(i, carry):
         return carry + got[pl.ds(pl.multiple_of(i * 2 * ROWS, 8), 2 * ROWS), :]
 
@@ -340,7 +347,6 @@
     mu = SIGMA * (comp / used)
     mu_out[...] = jnp.broadcast_to(mu, (8, N))
     residual = demand[pl.ds(device_col(), 1), :] + tail[1:2] - mu * tail[2:3]
-    residual_out[...] = jnp.broadcast_to(residual, (8, N))
 
     row = iota((HALF, N), 0)
     lane = iota((HALF, N), 1)
@@ -356,20 +362,21 @@
     panels += [bottom[8 * i : 8 * i + 8] for i in range(8)]
     inverse = jnp.concatenate(invert(panels), axis=0)
     inverse_out[...] = inverse
-    smoothed = jnp.dot(
-        jnp.broadcast_to(residual, (8, N)),
-        inverse,
-        precision=PRECISE,
-        preferred_element_type=jnp.float32,
-    )[0:1]
-    norm = jnp.sum(residual * smoothed, axis=1, keepdims=True)
-    set_message(msg, smoothed, norm)
+    smoothed = smooth(residual, inverse)
+    part = total_of(residual * smoothed)
+    zero = jnp.zeros((1, N), jnp.float32)
+    kept[RESIDUAL : RESIDUAL + 1, :] = residual
+    kept[SMOOTHED : SMOOTHED + 1, :] = smoothed
+    kept[PART : PART + 1, :] = jnp.broadcast_to(part, (1, N))
+    for at in (DIRECTION, IMAGE):
+        kept[at : at + 1, :] = zero
+    msg[...] = jnp.broadcast_to(smoothed, (N, N))
 
 
 def run_first(got, demand):
     return pl.pallas_call(
         first_kernel,
-        out_shape=(f32(N, N), f32(8, N), f32(8, N), f32(2 * N, N)),
+        out_shape=(f32(N, N), f32(KEPT, N), f32(8, N), f32(N, N)),
         in_specs=[vspec(), vspec()],
         out_specs=(vspec(),) * 4,
         compiler_params=params(),
@@ -384,88 +391,121 @@
     return even, odd
 
 
-def owner_kernel(got, direction, norms, residual, inverse, residual_out, msg):
-    image, curve = sum_pairs(got)
-    image = image + REGULAR * direction[pl.ds(lax.axis_index("leg") * 32 + device_col(), 1), :]
-    curve = jnp.sum(curve, axis=1, keepdims=True)
-    step_len = norms[0:1, :] / (curve + norms[1:2, :])
-    new = residual[0:1, :] - step_len * image
-    residual_out[...] = pair_rows(jnp.broadcast_to(new, (8, N)), jnp.broadcast_to(curve, (8, N)))
-    smoothed = jnp.dot(
-        jnp.broadcast_to(new, (8, N)),
-        inverse[...],
-        precision=PRECISE,
-        preferred_element_type=jnp.float32,
-    )[0:1]
-    set_message(msg, smoothed, jnp.sum(new * smoothed, axis=1, keepdims=True))
-
-
-def run_owner(got, direction, norms, residual, inverse):
-    return pl.pallas_call(
-        owner_kernel,
-        out_shape=(f32(8, N), f32(2 * N, N)),
-        in_specs=[vspec()] * 5,
+def combine(line, before, begin):
+    curve, cross, norm = line[:, 0:1], line[:, 1:2], line[:, 2:3]
+    if begin:
+        return norm, jnp.zeros_like(norm), curve
+    beta = norm / before[NORM : NORM + 1, 0:1]
+    old = before[CURVE : CURVE + 1, 0:1]
+    return norm, beta, curve + beta * (2.0 * cross + beta * old)
+
+
+def owner_kernel(begin, got, before, inverse, kept, msg):
+    image, line = sum_pairs(got)
+    smoothed = before[SMOOTHED : SMOOTHED + 1, :]
+    image = image + REGULAR * smoothed
+    norm, beta, curve = combine(line, before, begin)
+    direction = smoothed
+    if not begin:
+        image = image + beta * before[IMAGE : IMAGE + 1, :]
+        direction = smoothed + beta * before[DIRECTION : DIRECTION + 1, :]
+    step_len = norm / curve
+    residual = before[RESIDUAL : RESIDUAL + 1, :] - step_len * image
+    smoothed = smooth(residual, inverse[...])
+    rows = (
+        (RESIDUAL, residual),
+        (SMOOTHED, smoothed),
+        (DIRECTION, direction),
+        (IMAGE, image),
+        (PART, total_of(residual * smoothed)),
+        (NORM, norm),
+        (CURVE, curve),
+        (STEP, step_len),
+        (BETA, beta),
+    )
+    for at, row in rows:
+        kept[at : at + 1, :] = jnp.broadcast_to(row, (1, N))
+    msg[...] = jnp.broadcast_to(smoothed, (N, N))
+
+
+def run_owner(begin, got, before, inverse):
+    def kernel(*refs):
+        owner_kernel(begin, *refs)
+
+    return pl.pallas_call(
+        kernel,
+        out_shape=(f32(KEPT, N), f32(N, N)),
+        in_specs=[vspec()] * 3,
         out_specs=(vspec(),) * 2,
         compiler_params=params(),
         name="owner",
-    )(got, direction, norms, residual, inverse)
-
-
-def tile_kernel(last, begin, ids, hot, tiles, got, *refs):
-    if begin:
-        direction_out, applied_out, norms_out, msg, spread = refs
+    )(got, before, inverse)
+
+
+def sum_pairs(got):
+    total = jnp.sum(got[...].reshape(N // 4, 8, N), axis=0)
+    even = (total[0:1] + total[2:3]) + (total[4:5] + total[6:7])
+    odd = (total[1:2] + total[3:4]) + (total[5:6] + total[7:8])
+    return even, odd
+
+
+def tile_kernel(turn, ids, hot, tiles, got, kept, *refs):
+    spread = refs[-1]
+    msg, applied_out = refs[-2], refs[-3]
+    transpose_apply(ids, tiles, got, spread, applied_out)
+    applied = applied_out[...]
+    smoothed = kept[SMOOTHED : SMOOTHED + 1, :]
+    curve = jnp.sum(applied * applied, axis=0, keepdims=True) + REGULAR * smoothed * smoothed
+    if turn == 0:
+        cross = jnp.zeros((1, 1), jnp.float32)
     else:
-        direction_in, norms_in, direction_out, applied_out, norms_out, msg, spread = refs
-    smoothed = got[pl.ds(0, N, stride=2), :]
-    norm = jnp.sum(got[pl.ds(1, N, stride=2), :], axis=0, keepdims=True)
-    if begin:
-        direction = smoothed
+        before = refs[0][...]
+        if turn == 2:
+            before = before + kept[BETA : BETA + 1, :] * refs[1][...]
+        cross = jnp.sum(applied * before, axis=0, keepdims=True)
+        cross = total_of(cross + REGULAR * smoothed * kept[DIRECTION : DIRECTION + 1, :])
+    lane = iota((1, N), 1)
+    line = jnp.where(lane == 0, total_of(curve), jnp.where(lane == 1, cross, 0.0))
+    line = jnp.where(lane == 2, kept[PART : PART + 1, :], line)
+    if turn == 2:
+        msg[...] = jnp.broadcast_to(line, (N, N))
     else:
-        direction = smoothed + (norm / norms_in[0:1, :]) * direction_in[...]
-    direction_out[...] = direction
-    transpose_apply(ids, tiles, direction_out, spread, applied_out)
-    square = jnp.sum(jnp.sum(direction * direction, axis=0, keepdims=True), axis=1, keepdims=True)
-    norms_out[0:1, :] = norm
-    norms_out[1:2, :] = jnp.broadcast_to(REGULAR * square, (1, N))
-    applied = applied_out[...]
-    curve = jnp.sum(applied * applied, axis=0, keepdims=True)
-    if last:
-        msg[...] = jnp.broadcast_to(curve, (N, N))
-    else:
+        msg[pl.ds(1, N, stride=2), :] = jnp.broadcast_to(line, (N, N))
         forward_apply(tiles, (applied,), (spread,))
         msg[pl.ds(0, N, stride=2), :] = place_rows(hot[...], spread[...])
-        msg[pl.ds(1, N, stride=2), :] = jnp.broadcast_to(curve, (N, N))
-
-
-def run_tile(last, ids, hot, tiles, got, direction=None, norms=None):
-    begin = direction is None
-    extra = () if begin else (direction, norms)
-
+
+
+def run_tile(turn, ids, hot, tiles, got, kept, *before):
     def kernel(*refs):
-        tile_kernel(last, begin, *refs)
+        tile_kernel(turn, *refs)
 
     return pl.pallas_call(
         kernel,
-        out_shape=(f32(N, N), f32(GROUPS, N), f32(8, N), f32(N if last else 2 * N, N)),
-        in_specs=[sspec()] + [vspec()] * (3 + len(extra)),
-        out_specs=(vspec(),) * 4,
+        out_shape=(f32(GROUPS, N), f32(N if turn == 2 else 2 * N, N)),
+        in_specs=[sspec()] + [vspec()] * (4 + len(before)),
+        out_specs=(vspec(),) * 2,
         scratch_shapes=[pltpu.VMEM((TILES, N), jnp.float32)],
         compiler_params=params(),
-        name="tile_last" if last else "tile",
-    )(ids, hot, tiles, got, *extra)
+        name="tile_last" if turn == 2 else "tile",
+    )(ids, hot, tiles, got, kept, *before)
 
 
 def final_kernel(
-    got, curve0, curve1, d0, d1, d2, u0, u1, u2, n0, n1, n2, mu, root, base, ratio, step_dual,
-    step_primal,
+    got, kept1, kept2, z0, z1, z2, a0, a1, a2, mu, root, base, ratio, step_dual, step_primal
 ):
-    curve2 = jnp.sum(jnp.sum(got[...], axis=0, keepdims=True), axis=1, keepdims=True)
-    lens = []
-    for curve, norms in ((curve0[1:2, :], n0), (curve1[1:2, :], n1), (curve2, n2)):
-        lens.append(norms[0:1, :] / (curve + norms[1:2, :]))
+    line = jnp.sum(got[...], axis=0, keepdims=True)
+    norm, beta2, curve = combine(line, kept2, False)
+    len2 = norm / curve
+    len0, len1 = kept1[STEP : STEP + 1, :], kept2[STEP : STEP + 1, :]
+    beta1 = kept2[BETA : BETA + 1, :]
     at = pl.ds(pl.multiple_of(lax.axis_index("leg") * 32, 32), 32)
-    step_dual[...] = lens[0] * d0[at, :] + lens[1] * d1[at, :] + lens[2] * d2[at, :]
-    applied = lens[0] * u0[...] + lens[1] * u1[...] + lens[2] * u2[...]
+
+    def step(v0, v1, v2):
+        second = v1 + beta1 * v0
+        return len0 * v0 + len1 * second + len2 * (v2 + beta2 * second)
+
+    step_dual[...] = step(z0[at, :], z1[at, :], z2[at, :])
+    applied = step(a0[...], a1[...], a2[...])
     step_primal[...] = root[...] * applied + (mu[0:1, :] * ratio[...] + base[...])
 
 
@@ -506,24 +546,18 @@
     got_small = lax.ppermute(small_other, "core", swap)
     joined = run_join(acc, got_big, small, got_small)
     blocks = exchange(joined.reshape(HALF * ROWS // 4, 4, N), CHIPS).reshape(HALF * ROWS, N)
-    inverse, residual, mu, msg = run_first(blocks, demand)
-
-    direction = norms = None
-    kept = []
-    curves = []
-    for turn in range(ITERS):
-        got = exchange(msg, ALL)
-        last = turn + 1 == ITERS
-        direction, applied, norms, msg = run_tile(last, ids, hot, tiles, got, direction, norms)
-        kept.append((direction, applied, norms))
-        got = exchange(msg, ALL)
-        if not last:
-            residual, msg = run_owner(got, direction, norms, residual, inverse)
-            curves.append(residual)
-    (d0, u0, n0), (d1, u1, n1), (d2, u2, n2) = kept
-    return run_final(
-        got, curves[0], curves[1], d0, d1, d2, u0, u1, u2, n0, n1, n2, mu, root, base, ratio
-    )
+    inverse, kept0, mu, msg = run_first(blocks, demand)
+
+    z0 = exchange(msg, ALL)
+    a0, msg = run_tile(0, ids, hot, tiles, z0, kept0)
+    kept1, msg = run_owner(True, exchange(msg, ALL), kept0, inverse)
+    z1 = exchange(msg, ALL)
+    a1, msg = run_tile(1, ids, hot, tiles, z1, kept1, a0)
+    kept2, msg = run_owner(False, exchange(msg, ALL), kept1, inverse)
+    z2 = exchange(msg, ALL)
+    a2, msg = run_tile(2, ids, hot, tiles, z2, kept2, a1, a0)
+    got = exchange(msg, ALL)
+    return run_final(got, kept1, kept2, z0, z1, z2, a0, a1, a2, mu, root, base, ratio)
 
 
 def solution(mesh):

time: 154 us -> 153 us (level)
  no operation moved by 1% of the time
where the time goes in v6:
time: 153 us
  blocking collectives  123 us (80%)
  Pallas kernels  19 us (12%)
  starting transfers between devices  8.2 us (5%)
  waiting for transfers between devices  1.53 us (1%)
    all_to_all x7, blocking collectives, exchange(): return lax.all_to_all(rows, axes, split_axis=0, concat_axis=0, tiled=True)  123 us
    ppermute x3, starting transfers between devices, per_device(): lax.ppermute(duals, 'leg', [(i, (i + k) % 4) for i in range(4)])  6.5 us
    pallas_call x3, Pallas kernels, run_tile(): pl.pallas_call(kernel, out_shape=(f32(GROUPS, N), f32(N if turn == 2 else...  5.45 us
    pallas_call x1, Pallas kernels, run_gram(): pl.pallas_call(gram_kernel, out_shape=(jax.ShapeDtypeStruct((GROUPS, SPAN...  4.57 us
    pallas_call x1, Pallas kernels, run_first(): pl.pallas_call(first_kernel, out_shape=(f32(N, N), f32(KEPT, N), f32(8, N...  4.34 us
  transfers between devices with their start and end apart: 5, of which 1 were waited for; matrix products, arithmetic and copies ran while one was open for 0% of the time, Pallas kernels for 4%

profile of v6, /device:TPU:1, one launch (start us, length us, event | category | flops | bytes accessed | tf_op | source)
XLA Modules:
  0.0 153.0 jit_solution(14355845734670353901)
XLA Ops:
  0.6 0.0 copy-start.3
  0.6 0.0 copy-start.2
  0.7 0.0 copy-start.1
  0.7 0.0 copy-start.6
  0.7 0.0 copy-start
  0.7 0.0 copy-start.5
  0.7 3.8 %collective-permute-start.1 = (f32[32,128]{1,0:T(8,128)}, f32[32,128]{1,0:T(8,128)S(1)}, u32[]{:S(2)}, u32[]{:S(2)}) collective-permute-start(f32[32,128]{1,0:T(8,128)} %dual0), channel_id=1, source_target_pairs={{0,2},{1,3},{2,0},{3,1},{4,6},{5,7},{6,4},{7,5},{8,10},{9,11},{10,... | collective-permute-start | bytes 49160 | tf_op jit(solution)/shard_map/ppermute | solution.py:535
  4.5 0.4 collective-permute-start
  4.9 2.3 %collective-permute-start.2 = (f32[32,128]{1,0:T(8,128)}, f32[32,128]{1,0:T(8,128)S(1)}, u32[]{:S(2)}, u32[]{:S(2)}) collective-permute-start(f32[32,128]{1,0:T(8,128)} %dual0), channel_id=1, source_target_pairs={{0,3},{1,0},{2,1},{3,2},{4,7},{5,4},{6,5},{7,6},{8,11},{9,8},{10,9... | collective-permute-start | bytes 49160 | tf_op jit(solution)/shard_map/ppermute | solution.py:535
  7.2 4.6 %gram.1 = (bf16[16,512,256]{2,1,0:T(8,128)(2,1)S(1)}, f32[128,64,128]{2,1,0:T(8,128)S(1)}, f32[64,64,128]{2,1,0:T(8,128)S(1)}, f32[512,128]{1,0:T(8,128)S(1)}, f...) custom-call(f32[16,4,128,128]{3,2,1,0:T(8,128)} %coeffs_in.1, s32[4,16]{1,0:T(4,128)} %bitcast.40, ...), custom_call_target="tpu_custom_call" | custom-call | flops 1073741824 | bytes 12582912 | tf_op jit(solution)/shard_map/gram/pallas_call | solution.py:119
  11.8 0.0 collective-permute-done.1.dual2
  11.8 0.0 collective-permute-done.dual1
  11.8 0.0 collective-permute-done.2.dual3
  11.8 1.6 %collective-permute-start.3 = (f32[64,64,128]{2,1,0:T(8,128)S(1)}, f32[64,64,128]{2,1,0:T(8,128)S(1)}, u32[]{:S(2)}, u32[]{:S(2)}) collective-permute-start(f32[64,64,128]{2,1,0:T(8,128)S(1)} %get-tuple-element.36), channel_id=1, source_target_pairs={{0,4},{4,0},{1,5},{5,1},{2,6},{6,2},{3,7},{7,3},{8,12},{12,8},{9,1... | collective-permute-start | bytes 6291464 | tf_op jit(solution)/shard_map/ppermute | solution.py:542
  13.4 0.0 copy-done.3
  13.4 0.0 copy-done.2
  13.4 0.0 copy-done.1
  13.4 0.0 copy-done.6
  13.4 0.0 copy-done
  13.4 0.0 copy-done.5
  13.4 2.3 %rhs.1 = (f32[256,128]{1,0:T(8,128)S(1)}, f32[256,128]{1,0:T(8,128)S(1)}, f32[16,128]{1,0:T(8,128)S(1)}, f32[16,128]{1,0:T(8,128)S(1)}) custom-call(s32[4,16]{1,0:T(4,128)S(1)} %bitcast.41, s32[16]{0:T(128)S(1)} %copy-done.6, bf16[128,128]{1,0:T(8,128)(2,1)S(1)} %get-tuple-element.37.hot_place, bf16[16,512,256]{2,1,0:T(8,128)(2,1)S(1)} %get-tuple-element.33.tiles.refs_2_, ...), custom_call_target="tpu_custom_call" | custom-call | flops 134217728 | bytes 6291456 | tf_op jit(solution)/shard_map/rhs/pallas_call | solution.py:235
  15.7 0.1 collective-permute-start.4
  15.8 1.5 collective-permute-done.4.small_got
  17.4 0.0 collective-permute-done.3.got
  17.4 0.2 join.1
  17.6 0.0 copy-start.4
  17.6 39.0 %all_to_all.71 = f32[1088,4,128]{2,1,0:T(4,128)S(1)} all-to-all(f32[1088,4,128]{2,1,0:T(4,128)S(1)} %bitcast.24), channel_id=1, replica_groups=mesh['x'=4,'z'=4,'core'=2,'leg'=4] {'x','z','leg'}, dimensions={0} | all-to-all | bytes 4456448 | tf_op jit(solution)/shard_map/all_to_all | solution.py:528
  56.6 0.0 copy-done.4
  56.6 4.3 %first.1 = (f32[128,128]{1,0:T(8,128)S(1)}, f32[16,128]{1,0:T(8,128)S(1)}, f32[8,128]{1,0:T(8,128)S(1)}, f32[128,128]{1,0:T(8,128)S(1)}) custom-call(f32[4352,128]{1,0:T(8,128)S(1)} %bitcast.23, f32[32,128]{1,0:T(8,128)S(1)} %copy-done.4), custom_call_target="tpu_custom_call" | custom-call | tf_op jit(solution)/shard_map/first/pallas_call | solution.py:377
  61.0 15.0 %all_to_all.72 = f32[128,1,128]{2,1,0:T(1,128)S(1)} all-to-all(f32[128,1,128]{2,1,0:T(1,128)S(1)} %bitcast.36), channel_id=1, replica_groups=mesh['x'=4,'z'=4,'core'=2,'leg'=4] {'leg','x','core','z'}, dimensions={0} | all-to-all | bytes 131072 | tf_op jit(solution)/shard_map/all_to_all | solution.py:528
  76.0 2.1 %tile.2 = (f32[16,128]{1,0:T(8,128)S(1)}, f32[256,128]{1,0:T(8,128)S(1)}) custom-call(s32[4,16]{1,0:T(4,128)S(1)} %bitcast.42, bf16[128,128]{1,0:T(8,128)(2,1)S(1)} %get-tuple-element.32.refs_1_, bf16[16,512,256]{2,1,0:T(8,128)(2,1)S(1)} %get-tuple-element.33.tiles.refs_2_, f32[128,128]{1,0:T(8,128)S(1)} %bitcast.25, ...), custom_call_target="tpu_custom_call" | custom-call | tf_op jit(solution)/shard_map/tile/pallas_call | solution.py:482
  78.0 14.2 %all_to_all.73 = f32[128,2,128]{2,1,0:T(2,128)S(1)} all-to-all(f32[128,2,128]{2,1,0:T(2,128)S(1)} %bitcast.34), channel_id=1, replica_groups=mesh['x'=4,'z'=4,'core'=2,'leg'=4] {'leg','x','core','z'}, dimensions={0} | all-to-all | bytes 262144 | tf_op jit(solution)/shard_map/all_to_all | solution.py:528
  92.3 0.4 owner.2
  92.6 13.6 %all_to_all.74 = f32[128,1,128]{2,1,0:T(1,128)S(1)} all-to-all(f32[128,1,128]{2,1,0:T(1,128)S(1)} %bitcast.37), channel_id=1, replica_groups=mesh['x'=4,'z'=4,'core'=2,'leg'=4] {'leg','x','core','z'}, dimensions={0} | all-to-all | bytes 131072 | tf_op jit(solution)/shard_map/all_to_all | solution.py:528
  106.3 2.1 %tile.3 = (f32[16,128]{1,0:T(8,128)S(1)}, f32[256,128]{1,0:T(8,128)S(1)}) custom-call(s32[4,16]{1,0:T(4,128)S(1)} %bitcast.43, bf16[128,128]{1,0:T(8,128)(2,1)S(1)} %get-tuple-element.32.refs_1_, bf16[16,512,256]{2,1,0:T(8,128)(2,1)S(1)} %get-tuple-element.33.tiles.refs_2_, f32[128,128]{1,0:T(8,128)S(1)} %bitcast.27, ...), custom_call_target="tpu_custom_call" | custom-call | tf_op jit(solution)/shard_map/tile/pallas_call | solution.py:482
  108.4 14.2 %all_to_all.75 = f32[128,2,128]{2,1,0:T(2,128)S(1)} all-to-all(f32[128,2,128]{2,1,0:T(2,128)S(1)} %bitcast.35), channel_id=1, replica_groups=mesh['x'=4,'z'=4,'core'=2,'leg'=4] {'leg','x','core','z'}, dimensions={0} | all-to-all | bytes 262144 | tf_op jit(solution)/shard_map/all_to_all | solution.py:528
  122.6 0.6 owner.3
  123.2 13.6 %all_to_all.76 = f32[128,1,128]{2,1,0:T(1,128)S(1)} all-to-all(f32[128,1,128]{2,1,0:T(1,128)S(1)} %bitcast.38), channel_id=1, replica_groups=mesh['x'=4,'z'=4,'core'=2,'leg'=4] {'leg','x','core','z'}, dimensions={0} | all-to-all | bytes 131072 | tf_op jit(solution)/shard_map/all_to_all | solution.py:528
  136.8 1.3 tile_last.1
  138.2 13.8 %all_to_all.77 = f32[128,1,128]{2,1,0:T(1,128)S(1)} all-to-all(f32[128,1,128]{2,1,0:T(1,128)S(1)} %bitcast.39), channel_id=1, replica_groups=mesh['x'=4,'z'=4,'core'=2,'leg'=4] {'leg','x','core','z'}, dimensions={0} | all-to-all | bytes 131072 | tf_op jit(solution)/shard_map/all_to_all | solution.py:528
  151.9 1.1 final.1
Async XLA Ops:
  0.6 12.8 %copy-start.3 = (f32[32,128]{1,0:T(8,128)S(1)}, f32[32,128]{1,0:T(8,128)}, u32[]{:S(2)}) copy-start(f32[32,128]{1,0:T(8,128)} %dual0) | copy-start | bytes 49156
  0.6 12.8 %copy-start.2 = (f32[16,128]{1,0:T(8,128)S(1)}, f32[16,128]{1,0:T(8,128)}, u32[]{:S(2)}) copy-start(f32[16,128]{1,0:T(8,128)} %slack.1) | copy-start | bytes 24580
  0.7 12.7 %copy-start.1 = (f32[16,128]{1,0:T(8,128)S(1)}, f32[16,128]{1,0:T(8,128)}, u32[]{:S(2)}) copy-start(f32[16,128]{1,0:T(8,128)} %primal.1) | copy-start | bytes 24580
  0.7 12.7 %copy-start.6 = (s32[16]{0:T(128)S(1)}, s32[16]{0:T(128)}, u32[]{:S(2)}) copy-start(s32[16]{0:T(128)} %counts.1) | copy-start | bytes 196
  0.7 12.7 %copy-start = (s32[16,4]{0,1:T(4,128)S(1)}, s32[16,4]{0,1:T(4,128)}, u32[]{:S(2)}) copy-start(s32[16,4]{0,1:T(4,128)} %param.9) | copy-start | bytes 772
  0.7 12.7 %copy-start.5 = (f32[16,128]{1,0:T(8,128)S(1)}, f32[16,128]{1,0:T(8,128)}, u32[]{:S(2)}) copy-start(f32[16,128]{1,0:T(8,128)} %cost.1) | copy-start | bytes 24580
  0.7 11.1 %collective-permute-start.1 = (f32[32,128]{1,0:T(8,128)}, f32[32,128]{1,0:T(8,128)S(1)}, u32[]{:S(2)}, u32[]{:S(2)}) collective-permute-start(f32[32,128]{1,0:T(8,128)} %dual0), channel_id=1, source_target_pairs={{0,2},{1,3},{2,0},{3,1},{4,6},{5,7},{6,4},{7,5},{8,10},{9,11},{10,... | collective-permute-start | bytes 49160 | tf_op jit(solution)/shard_map/ppermute | solution.py:535
  4.5 7.3 %collective-permute-start = (f32[32,128]{1,0:T(8,128)}, f32[32,128]{1,0:T(8,128)S(1)}, u32[]{:S(2)}, u32[]{:S(2)}) collective-permute-start(f32[32,128]{1,0:T(8,128)} %dual0), channel_id=1, source_target_pairs={{0,1},{1,2},{2,3},{3,0},{4,5},{5,6},{6,7},{7,4},{8,9},{9,10},{10,1... | collective-permute-start | bytes 49160 | tf_op jit(solution)/shard_map/ppermute | solution.py:535
  4.9 6.9 %collective-permute-start.2 = (f32[32,128]{1,0:T(8,128)}, f32[32,128]{1,0:T(8,128)S(1)}, u32[]{:S(2)}, u32[]{:S(2)}) collective-permute-start(f32[32,128]{1,0:T(8,128)} %dual0), channel_id=1, source_target_pairs={{0,3},{1,0},{2,1},{3,2},{4,7},{5,4},{6,5},{7,6},{8,11},{9,8},{10,9... | collective-permute-start | bytes 49160 | tf_op jit(solution)/shard_map/ppermute | solution.py:535
  11.8 5.6 %collective-permute-start.3 = (f32[64,64,128]{2,1,0:T(8,128)S(1)}, f32[64,64,128]{2,1,0:T(8,128)S(1)}, u32[]{:S(2)}, u32[]{:S(2)}) collective-permute-start(f32[64,64,128]{2,1,0:T(8,128)S(1)} %get-tuple-element.36), channel_id=1, source_target_pairs={{0,4},{4,0},{1,5},{5,1},{2,6},{6,2},{3,7},{7,3},{8,12},{12,8},{9,1... | collective-permute-start | bytes 6291464 | tf_op jit(solution)/shard_map/ppermute | solution.py:542
  15.7 1.6 %collective-permute-start.4 = (f32[256,128]{1,0:T(8,128)S(1)}, f32[256,128]{1,0:T(8,128)S(1)}, u32[]{:S(2)}, u32[]{:S(2)}) collective-permute-start(f32[256,128]{1,0:T(8,128)S(1)} %get-tuple-element.45), channel_id=1, source_target_pairs={{0,4},{4,0},{1,5},{5,1},{2,6},{6,2},{3,7},{7,3},{8,12},{12,8},{9,1... | collective-permute-start | bytes 393224 | tf_op jit(solution)/shard_map/ppermute | solution.py:546
  17.6 39.0 %copy-start.4 = (f32[32,128]{1,0:T(8,128)S(1)}, f32[32,128]{1,0:T(8,128)}, u32[]{:S(2)}) copy-start(f32[32,128]{1,0:T(8,128)} %demand.1) | copy-start | bytes 49156

commit v7 on v6

--- a/solution.py
+++ b/solution.py
@@ -63,7 +63,7 @@
 
 def gram_kernel(
     coeffs_in, ids_in, counts_in, primal_in, slack_in, tiles, acc, other, small, root_out,
-    hot_ids, hot_place, coeffs, ids, counts, primal, slack, hot, hot2, sem, tile_sem,
+    hot_rows, hot_ids, hot_place, coeffs, ids, counts, primal, slack, hot, hot2, sem, tile_sem,
 ):
     little = [
         pltpu.make_async_copy(ids_in, ids, sem.at[0]),
@@ -111,6 +111,7 @@
             hot[t : t + 1, :] = (line_lane == block).astype(jnp.float32)
             hot2[t : t + 1, :] = (line_lane == place).astype(jnp.float32)
     other[...] = acc[pl.ds(HALF, HALF)]
+    hot_rows[...] = hot[:TILES, :].astype(jnp.bfloat16)
     hot_ids[...] = jnp.transpose(hot[...]).astype(jnp.bfloat16)
     hot_place[...] = jnp.transpose(hot2[...]).astype(jnp.bfloat16)
 
@@ -124,11 +125,12 @@
             f32(HALF, HALF, N),
             f32(N * EXTRA, N),
             f32(GROUPS, N),
+            jax.ShapeDtypeStruct((TILES, N), jnp.bfloat16),
             jax.ShapeDtypeStruct((N, N), jnp.bfloat16),
             jax.ShapeDtypeStruct((N, N), jnp.bfloat16),
         ),
         in_specs=[pl.BlockSpec(memory_space=HBM)] * 5,
-        out_specs=(vspec(),) * 7,
+        out_specs=(vspec(),) * 8,
         scratch_shapes=[
             pltpu.VMEM((GROUPS, SPAN, N, N), jnp.float32),
             pltpu.SMEM((SPAN, GROUPS), jnp.int32),
@@ -148,11 +150,25 @@
     )(*(pltpu.with_memory_space_constraint(x, HBM) for x in (coeffs, ids, counts, primal, slack)))
 
 
-def transpose_apply(ids, tiles, vector, spread, out):
-    for t in range(TILES):
-        spread[t : t + 1, :] = vector[pl.ds(ids[t % SPAN, t // SPAN], 1), :]
-    high, low = split(spread[...])
+def transpose_apply(hot, tiles, vector, out):
+    high, low = split(vector[...])
+    high = jnp.dot(hot, high, preferred_element_type=jnp.float32)
+    low = jnp.dot(hot, low, preferred_element_type=jnp.float32)
+    whole = high + low
+    high, low = high.astype(jnp.bfloat16), low.astype(jnp.bfloat16)
+    turned = jnp.transpose(whole)
     for g in range(GROUPS):
+        if g % 5 == 4:
+            total = None
+            for s in range(SPAN):
+                t = g * SPAN + s
+                pair = tiles[g, s * N : (s + 1) * N, :].astype(jnp.float32)
+                tile = pair[:, :N] + pair[:, N:]
+                part = tile * jnp.broadcast_to(turned[:, t : t + 1], (N, N))
+                part = jnp.sum(part.reshape(N // 8, 8, N), axis=0)
+                total = part if total is None else total + part
+            out[g : g + 1, :] = jnp.sum(total, axis=0, keepdims=True)
+            continue
         parts = []
         for rows in (high, low):
             own = [rows[g * SPAN + s : g * SPAN + s + 1] for s in range(SPAN)]
@@ -198,18 +214,16 @@
 
 
 def rhs_kernel(
-    ids, counts, hot_place, tiles, dual0, dual1, dual2, dual3, primal, slack, cost, root, small,
-    own_out, other_out, base_out, scale_out, spread, spread2, duals, valid_s, applied,
+    hot_rows, hot_place, tiles, dual0, dual1, dual2, dual3, primal, slack, cost, root, small,
+    own_out, other_out, base_out, scale_out, spread, spread2, duals, applied,
 ):
     leg = lax.axis_index("leg")
     for k, part in enumerate((dual0, dual1, dual2, dual3)):
         at = pl.multiple_of(((leg - k) & 3) * 32, 32)
         duals[pl.ds(at, 32), :] = part[...]
-    for g in range(GROUPS):
-        valid_s[g : g + 1, :] = (iota((1, N), 1) < counts[g]).astype(jnp.float32)
-    valid = valid_s[...]
-    used = valid > 0.0
-    transpose_apply(ids, tiles, duals, spread, applied)
+    used = root[...] > 0.0
+    valid = used.astype(jnp.float32)
+    transpose_apply(hot_rows[...], tiles, duals, applied)
     dual_res = cost[...] - applied[...] / jnp.where(used, root[...], 1.0) - slack[...]
     weighted = root[...] * dual_res
     ratio = valid / slack[...]
@@ -231,23 +245,22 @@
         out[pl.ds(3, HALF, stride=EXTRA), :] = jnp.broadcast_to(comp, (HALF, N))
 
 
-def run_rhs(ids, counts, hot_place, tiles, duals, primal, slack, cost, root, small):
+def run_rhs(hot_rows, hot_place, tiles, duals, primal, slack, cost, root, small):
     return pl.pallas_call(
         rhs_kernel,
         out_shape=(f32(HALF * EXTRA, N), f32(HALF * EXTRA, N), f32(GROUPS, N), f32(GROUPS, N)),
-        in_specs=[sspec(), sspec()] + [vspec()] * 11,
+        in_specs=[vspec()] * 12,
         out_specs=(vspec(),) * 4,
         scratch_shapes=[
             pltpu.VMEM((TILES, N), jnp.float32),
             pltpu.VMEM((TILES, N), jnp.float32),
             pltpu.VMEM((N, N), jnp.float32),
             pltpu.VMEM((GROUPS, N), jnp.float32),
-            pltpu.VMEM((GROUPS, N), jnp.float32),
         ],
         compiler_params=params(),
         cost_estimate=pl.CostEstimate(flops=1 << 27, bytes_accessed=6 << 20, transcendentals=0),
         name="rhs",
-    )(ids, counts, hot_place, tiles, *duals, primal, slack, cost, root, small)
+    )(hot_rows, hot_place, tiles, *duals, primal, slack, cost, root, small)
 
 
 def join_kernel(acc, got, small, small_got, out):
@@ -392,11 +405,11 @@
 
 
 def combine(line, before, begin):
-    curve, cross, norm = line[:, 0:1], line[:, 1:2], line[:, 2:3]
+    curve, cross, norm = (jnp.broadcast_to(line[:, k : k + 1], (1, N)) for k in range(3))
     if begin:
         return norm, jnp.zeros_like(norm), curve
-    beta = norm / before[NORM : NORM + 1, 0:1]
-    old = before[CURVE : CURVE + 1, 0:1]
+    beta = norm / before[NORM : NORM + 1, :]
+    old = before[CURVE : CURVE + 1, :]
     return norm, beta, curve + beta * (2.0 * cross + beta * old)
 
 
@@ -449,10 +462,10 @@
     return even, odd
 
 
-def tile_kernel(turn, ids, hot, tiles, got, kept, *refs):
+def tile_kernel(turn, hot_rows, hot, tiles, got, kept, *refs):
     spread = refs[-1]
     msg, applied_out = refs[-2], refs[-3]
-    transpose_apply(ids, tiles, got, spread, applied_out)
+    transpose_apply(hot_rows[...], tiles, got, applied_out)
     applied = applied_out[...]
     smoothed = kept[SMOOTHED : SMOOTHED + 1, :]
     curve = jnp.sum(applied * applied, axis=0, keepdims=True) + REGULAR * smoothed * smoothed
@@ -475,19 +488,19 @@
         msg[pl.ds(0, N, stride=2), :] = place_rows(hot[...], spread[...])
 
 
-def run_tile(turn, ids, hot, tiles, got, kept, *before):
+def run_tile(turn, hot_rows, hot, tiles, got, kept, *before):
     def kernel(*refs):
         tile_kernel(turn, *refs)
 
     return pl.pallas_call(
         kernel,
         out_shape=(f32(GROUPS, N), f32(N if turn == 2 else 2 * N, N)),
-        in_specs=[sspec()] + [vspec()] * (4 + len(before)),
+        in_specs=[vspec()] * (5 + len(before)),
         out_specs=(vspec(),) * 2,
         scratch_shapes=[pltpu.VMEM((TILES, N), jnp.float32)],
         compiler_params=params(),
         name="tile_last" if turn == 2 else "tile",
-    )(ids, hot, tiles, got, kept, *before)
+    )(hot_rows, hot, tiles, got, kept, *before)
 
 
 def final_kernel(
@@ -534,14 +547,14 @@
     for k in (1, 2, 3):
         parts.append(lax.ppermute(duals, "leg", [(i, (i + k) % 4) for i in range(4)]))
 
-    tiles, acc, other, small, root, hot, hot_place = run_gram(
+    tiles, acc, other, small, root, hot_rows, hot, hot_place = run_gram(
         coeffs, ids, col_counts, primal, slack
     )
     swap = [(0, 1), (1, 0)]
     other, *parts = lax.optimization_barrier((other, *parts))
     got_big = lax.ppermute(other, "core", swap)
     small, small_other, base, ratio = run_rhs(
-        ids, col_counts, hot_place, tiles, parts, primal, slack, cost, root, small
+        hot_rows, hot_place, tiles, parts, primal, slack, cost, root, small
     )
     got_small = lax.ppermute(small_other, "core", swap)
     joined = run_join(acc, got_big, small, got_small)
@@ -549,13 +562,13 @@
     inverse, kept0, mu, msg = run_first(blocks, demand)
 
     z0 = exchange(msg, ALL)
-    a0, msg = run_tile(0, ids, hot, tiles, z0, kept0)
+    a0, msg = run_tile(0, hot_rows, hot, tiles, z0, kept0)
     kept1, msg = run_owner(True, exchange(msg, ALL), kept0, inverse)
     z1 = exchange(msg, ALL)
-    a1, msg = run_tile(1, ids, hot, tiles, z1, kept1, a0)
+    a1, msg = run_tile(1, hot_rows, hot, tiles, z1, kept1, a0)
     kept2, msg = run_owner(False, exchange(msg, ALL), kept1, inverse)
     z2 = exchange(msg, ALL)
-    a2, msg = run_tile(2, ids, hot, tiles, z2, kept2, a1, a0)
+    a2, msg = run_tile(2, hot_rows, hot, tiles, z2, kept2, a1, a0)
     got = exchange(msg, ALL)
     return run_final(got, kept1, kept2, z0, z1, z2, a0, a1, a2, mu, root, base, ratio)
 

time: 153 us -> 151 us (0.987)
  Pallas kernels: 19 us -> 16.3 us
    pallas_call x3, Pallas kernels: 5.45 us -> 3.88 us  [run_tile(): pl.pallas_call(kernel, out_shape=(f32(GROUPS, N), f32(N if turn == 2 else...]
where the time goes in v7:
time: 151 us
  blocking collectives  123 us (81%)
  Pallas kernels  16.3 us (11%)
  starting transfers between devices  8.22 us (5%)
  waiting for transfers between devices  1.99 us (1%)
    all_to_all x7, blocking collectives, exchange(): return lax.all_to_all(rows, axes, split_axis=0, concat_axis=0, tiled=True)  123 us
    ppermute x3, starting transfers between devices, per_device(): lax.ppermute(duals, 'leg', [(i, (i + k) % 4) for i in range(4)])  6.5 us
    pallas_call x1, Pallas kernels, run_gram(): pl.pallas_call(gram_kernel, out_shape=(jax.ShapeDtypeStruct((GROUPS, SPAN...  4.56 us
    pallas_call x1, Pallas kernels, run_first(): pl.pallas_call(first_kernel, out_shape=(f32(N, N), f32(KEPT, N), f32(8, N...  4.34 us
    pallas_call x3, Pallas kernels, run_tile(): pl.pallas_call(kernel, out_shape=(f32(GROUPS, N), f32(N if turn == 2 else...  3.88 us
  transfers between devices with their start and end apart: 5, of which 1 were waited for; matrix products, arithmetic and copies ran while one was open for 0% of the time, Pallas kernels for 4%

profile of v7, /device:TPU:1, one launch (start us, length us, event | category | flops | bytes accessed | tf_op | source)
XLA Modules:
  0.0 150.7 jit_solution(10807770046012190532)
XLA Ops:
  0.6 0.0 copy-start.2
  0.6 0.0 copy-start.1
  0.7 0.0 copy-start
  0.7 0.0 copy-start.4
  0.7 3.8 %collective-permute-start.1 = (f32[32,128]{1,0:T(8,128)}, f32[32,128]{1,0:T(8,128)S(1)}, u32[]{:S(2)}, u32[]{:S(2)}) collective-permute-start(f32[32,128]{1,0:T(8,128)} %dual0), channel_id=1, source_target_pairs={{0,2},{1,3},{2,0},{3,1},{4,6},{5,7},{6,4},{7,5},{8,10},{9,11},{10,... | collective-permute-start | bytes 49160 | tf_op jit(solution)/shard_map/ppermute | solution.py:548
  4.5 0.4 collective-permute-start
  4.9 2.3 %collective-permute-start.2 = (f32[32,128]{1,0:T(8,128)}, f32[32,128]{1,0:T(8,128)S(1)}, u32[]{:S(2)}, u32[]{:S(2)}) collective-permute-start(f32[32,128]{1,0:T(8,128)} %dual0), channel_id=1, source_target_pairs={{0,3},{1,0},{2,1},{3,2},{4,7},{5,4},{6,5},{7,6},{8,11},{9,8},{10,9... | collective-permute-start | bytes 49160 | tf_op jit(solution)/shard_map/ppermute | solution.py:548
  7.2 4.6 %gram.1 = (bf16[16,512,256]{2,1,0:T(8,128)(2,1)S(1)}, f32[128,64,128]{2,1,0:T(8,128)S(1)}, f32[64,64,128]{2,1,0:T(8,128)S(1)}, f32[512,128]{1,0:T(8,128)S(1)}, f...) custom-call(f32[16,4,128,128]{3,2,1,0:T(8,128)} %coeffs_in.1, ...), custom_call_target="tpu_custom_call" | custom-call | flops 1073741824 | bytes 12582912 | tf_op jit(solution)/shard_map/gram/pallas_call | solution.py:120
  11.7 0.0 collective-permute-done.1.dual2
  11.8 0.0 collective-permute-done.dual1
  11.8 0.0 collective-permute-done.2.dual3
  11.8 1.6 %collective-permute-start.3 = (f32[64,64,128]{2,1,0:T(8,128)S(1)}, f32[64,64,128]{2,1,0:T(8,128)S(1)}, u32[]{:S(2)}, u32[]{:S(2)}) collective-permute-start(f32[64,64,128]{2,1,0:T(8,128)S(1)} %get-tuple-element.38), channel_id=1, source_target_pairs={{0,4},{4,0},{1,5},{5,1},{2,6},{6,2},{3,7},{7,3},{8,12},{12,8},{9,1... | collective-permute-start | bytes 6291464 | tf_op jit(solution)/shard_map/ppermute | solution.py:555
  13.4 0.0 copy-done.2
  13.4 0.0 copy-done.1
  13.4 0.0 copy-done
  13.4 0.0 copy-done.4
  13.4 1.9 %rhs.1 = (f32[256,128]{1,0:T(8,128)S(1)}, f32[256,128]{1,0:T(8,128)S(1)}, f32[16,128]{1,0:T(8,128)S(1)}, f32[16,128]{1,0:T(8,128)S(1)}) custom-call(bf16[64,128]{1,0:T(8,128)(2,1)S(1)} %get-tuple-element.33.hot_rows.refs_0_, bf16[128,128]{1,0:T(8,128)(2,1)S(1)} %get-tuple-element.39.hot_place, bf16[16,512,256]{2,1,0:T(8,128)(2,1)S(1)} %get-tuple-element.35.tiles.refs_2_, ...), custom_call_target="tpu_custom_call" | custom-call | flops 134217728 | bytes 6291456 | tf_op jit(solution)/shard_map/rhs/pallas_call | solution.py:249
  15.3 0.1 collective-permute-start.4
  15.4 2.0 %collective-permute-done.4.small_got = f32[256,128]{1,0:T(8,128)S(1)} collective-permute-done((f32[256,128]{1,0:T(8,128)S(1)}, f32[256,128]{1,0:T(8,128)S(1)}, u32[]{:S(2)}, u32[]{:S(2)}) %collective-permute-start.4) | collective-permute-done | bytes 131104 | tf_op jit(solution)/shard_map/ppermute | solution.py:559
  17.3 0.0 collective-permute-done.3.got
  17.4 0.3 join.1
  17.6 0.0 copy-start.3
  17.7 39.0 %all_to_all.71 = f32[1088,4,128]{2,1,0:T(4,128)S(1)} all-to-all(f32[1088,4,128]{2,1,0:T(4,128)S(1)} %bitcast.24), channel_id=1, replica_groups=mesh['x'=4,'z'=4,'core'=2,'leg'=4] {'x','z','leg'}, dimensions={0} | all-to-all | bytes 4456448 | tf_op jit(solution)/shard_map/all_to_all | solution.py:541
  56.7 0.0 copy-done.3
  56.7 4.3 %first.1 = (f32[128,128]{1,0:T(8,128)S(1)}, f32[16,128]{1,0:T(8,128)S(1)}, f32[8,128]{1,0:T(8,128)S(1)}, f32[128,128]{1,0:T(8,128)S(1)}) custom-call(f32[4352,128]{1,0:T(8,128)S(1)} %bitcast.23, f32[32,128]{1,0:T(8,128)S(1)} %copy-done.3), custom_call_target="tpu_custom_call" | custom-call | tf_op jit(solution)/shard_map/first/pallas_call | solution.py:390
  61.0 15.0 %all_to_all.72 = f32[128,1,128]{2,1,0:T(1,128)S(1)} all-to-all(f32[128,1,128]{2,1,0:T(1,128)S(1)} %bitcast.36), channel_id=1, replica_groups=mesh['x'=4,'z'=4,'core'=2,'leg'=4] {'leg','x','core','z'}, dimensions={0} | all-to-all | bytes 131072 | tf_op jit(solution)/shard_map/all_to_all | solution.py:541
  76.0 1.5 %tile.2 = (f32[16,128]{1,0:T(8,128)S(1)}, f32[256,128]{1,0:T(8,128)S(1)}) custom-call(bf16[64,128]{1,0:T(8,128)(2,1)S(1)} %get-tuple-element.33.hot_rows.refs_0_, bf16[128,128]{1,0:T(8,128)(2,1)S(1)} %get-tuple-element.34.refs_1_, bf16[16,512,256]{2,1,0:T(8,128)(2,1)S(1)} %get-tuple-element.35.tiles.refs_2_, f32[128,128]{1,0:T(8,128)S(1)} %bitcast.25, ...), custom_call_target="tpu_custom_call" | custom-call | tf_op jit(solution)/shard_map/tile/pallas_call | solution.py:495
  77.5 14.2 %all_to_all.73 = f32[128,2,128]{2,1,0:T(2,128)S(1)} all-to-all(f32[128,2,128]{2,1,0:T(2,128)S(1)} %bitcast.34), channel_id=1, replica_groups=mesh['x'=4,'z'=4,'core'=2,'leg'=4] {'leg','x','core','z'}, dimensions={0} | all-to-all | bytes 262144 | tf_op jit(solution)/shard_map/all_to_all | solution.py:541
  91.8 0.3 owner.2
  92.1 13.6 %all_to_all.74 = f32[128,1,128]{2,1,0:T(1,128)S(1)} all-to-all(f32[128,1,128]{2,1,0:T(1,128)S(1)} %bitcast.38), channel_id=1, replica_groups=mesh['x'=4,'z'=4,'core'=2,'leg'=4] {'leg','x','core','z'}, dimensions={0} | all-to-all | bytes 131072 | tf_op jit(solution)/shard_map/all_to_all | solution.py:541
  105.7 1.5 %tile.3 = (f32[16,128]{1,0:T(8,128)S(1)}, f32[256,128]{1,0:T(8,128)S(1)}) custom-call(bf16[64,128]{1,0:T(8,128)(2,1)S(1)} %get-tuple-element.33.hot_rows.refs_0_, bf16[128,128]{1,0:T(8,128)(2,1)S(1)} %get-tuple-element.34.refs_1_, bf16[16,512,256]{2,1,0:T(8,128)(2,1)S(1)} %get-tuple-element.35.tiles.refs_2_, f32[128,128]{1,0:T(8,128)S(1)} %bitcast.27, ...), custom_call_target="tpu_custom_call" | custom-call | tf_op jit(solution)/shard_map/tile/pallas_call | solution.py:495
  107.3 14.2 %all_to_all.75 = f32[128,2,128]{2,1,0:T(2,128)S(1)} all-to-all(f32[128,2,128]{2,1,0:T(2,128)S(1)} %bitcast.35), channel_id=1, replica_groups=mesh['x'=4,'z'=4,'core'=2,'leg'=4] {'leg','x','core','z'}, dimensions={0} | all-to-all | bytes 262144 | tf_op jit(solution)/shard_map/all_to_all | solution.py:541
  121.5 0.3 owner.3
  121.8 13.6 %all_to_all.76 = f32[128,1,128]{2,1,0:T(1,128)S(1)} all-to-all(f32[128,1,128]{2,1,0:T(1,128)S(1)} %bitcast.39), channel_id=1, replica_groups=mesh['x'=4,'z'=4,'core'=2,'leg'=4] {'leg','x','core','z'}, dimensions={0} | all-to-all | bytes 131072 | tf_op jit(solution)/shard_map/all_to_all | solution.py:541
  135.4 0.8 tile_last.1
  136.3 13.7 %all_to_all.77 = f32[128,1,128]{2,1,0:T(1,128)S(1)} all-to-all(f32[128,1,128]{2,1,0:T(1,128)S(1)} %bitcast.37), channel_id=1, replica_groups=mesh['x'=4,'z'=4,'core'=2,'leg'=4] {'leg','x','core','z'}, dimensions={0} | all-to-all | bytes 131072 | tf_op jit(solution)/shard_map/all_to_all | solution.py:541
  150.0 0.7 final.1
Async XLA Ops:
  0.6 12.7 %copy-start.2 = (f32[32,128]{1,0:T(8,128)S(1)}, f32[32,128]{1,0:T(8,128)}, u32[]{:S(2)}) copy-start(f32[32,128]{1,0:T(8,128)} %dual0) | copy-start | bytes 49156
  0.6 12.7 %copy-start.1 = (f32[16,128]{1,0:T(8,128)S(1)}, f32[16,128]{1,0:T(8,128)}, u32[]{:S(2)}) copy-start(f32[16,128]{1,0:T(8,128)} %slack.1) | copy-start | bytes 24580
  0.7 12.7 %copy-start = (f32[16,128]{1,0:T(8,128)S(1)}, f32[16,128]{1,0:T(8,128)}, u32[]{:S(2)}) copy-start(f32[16,128]{1,0:T(8,128)} %primal.1) | copy-start | bytes 24580
  0.7 12.7 %copy-start.4 = (f32[16,128]{1,0:T(8,128)S(1)}, f32[16,128]{1,0:T(8,128)}, u32[]{:S(2)}) copy-start(f32[16,128]{1,0:T(8,128)} %cost.1) | copy-start | bytes 24580
  0.7 11.1 %collective-permute-start.1 = (f32[32,128]{1,0:T(8,128)}, f32[32,128]{1,0:T(8,128)S(1)}, u32[]{:S(2)}, u32[]{:S(2)}) collective-permute-start(f32[32,128]{1,0:T(8,128)} %dual0), channel_id=1, source_target_pairs={{0,2},{1,3},{2,0},{3,1},{4,6},{5,7},{6,4},{7,5},{8,10},{9,11},{10,... | collective-permute-start | bytes 49160 | tf_op jit(solution)/shard_map/ppermute | solution.py:548
  4.5 7.3 %collective-permute-start = (f32[32,128]{1,0:T(8,128)}, f32[32,128]{1,0:T(8,128)S(1)}, u32[]{:S(2)}, u32[]{:S(2)}) collective-permute-start(f32[32,128]{1,0:T(8,128)} %dual0), channel_id=1, source_target_pairs={{0,1},{1,2},{2,3},{3,0},{4,5},{5,6},{6,7},{7,4},{8,9},{9,10},{10,1... | collective-permute-start | bytes 49160 | tf_op jit(solution)/shard_map/ppermute | solution.py:548
  4.9 6.9 %collective-permute-start.2 = (f32[32,128]{1,0:T(8,128)}, f32[32,128]{1,0:T(8,128)S(1)}, u32[]{:S(2)}, u32[]{:S(2)}) collective-permute-start(f32[32,128]{1,0:T(8,128)} %dual0), channel_id=1, source_target_pairs={{0,3},{1,0},{2,1},{3,2},{4,7},{5,4},{6,5},{7,6},{8,11},{9,8},{10,9... | collective-permute-start | bytes 49160 | tf_op jit(solution)/shard_map/ppermute | solution.py:548
  11.8 5.6 %collective-permute-start.3 = (f32[64,64,128]{2,1,0:T(8,128)S(1)}, f32[64,64,128]{2,1,0:T(8,128)S(1)}, u32[]{:S(2)}, u32[]{:S(2)}) collective-permute-start(f32[64,64,128]{2,1,0:T(8,128)S(1)} %get-tuple-element.38), channel_id=1, source_target_pairs={{0,4},{4,0},{1,5},{5,1},{2,6},{6,2},{3,7},{7,3},{8,12},{12,8},{9,1... | collective-permute-start | bytes 6291464 | tf_op jit(solution)/shard_map/ppermute | solution.py:555
  15.3 2.1 %collective-permute-start.4 = (f32[256,128]{1,0:T(8,128)S(1)}, f32[256,128]{1,0:T(8,128)S(1)}, u32[]{:S(2)}, u32[]{:S(2)}) collective-permute-start(f32[256,128]{1,0:T(8,128)S(1)} %get-tuple-element.47), channel_id=1, source_target_pairs={{0,4},{4,0},{1,5},{5,1},{2,6},{6,2},{3,7},{7,3},{8,12},{12,8},{9,1... | collective-permute-start | bytes 393224 | tf_op jit(solution)/shard_map/ppermute | solution.py:559
  17.6 39.0 %copy-start.3 = (f32[32,128]{1,0:T(8,128)S(1)}, f32[32,128]{1,0:T(8,128)}, u32[]{:S(2)}) copy-start(f32[32,128]{1,0:T(8,128)} %demand.1) | copy-start | bytes 49156

commit v8 on v7

--- a/solution.py
+++ b/solution.py
@@ -58,7 +58,7 @@
     return (full[:N, :N] + full[N:, N:]) + (full[:N, N:] + full[N:, :N])
 
 
-CHUNKS = (0, 2, 6)
+CHUNKS = (0, 5)
 
 
 def gram_kernel(
@@ -319,11 +319,13 @@
         for step in range(1, count):
             i = (k + step) % count
             old = panels[i]
-            new = jnp.where(mine, 0.0, old)
+            terms = []
             for m in range(8):
                 col = jnp.broadcast_to(old[:, 8 * k + m : 8 * k + m + 1], (8, N))
-                new = new - col * rows[m]
-            panels[i] = new
+                terms.append(col * rows[m])
+            while len(terms) > 1:
+                terms = [terms[j] + terms[j + 1] for j in range(0, len(terms), 2)]
+            panels[i] = jnp.where(mine, 0.0, old) - terms[0]
         panels[k] = total
     return panels
 

time: 151 us -> 151 us (level)
  no operation moved by 1% of the time
where the time goes in v8:
time: 151 us
  blocking collectives  124 us (82%)
  Pallas kernels  16.1 us (11%)
  starting transfers between devices  8.21 us (5%)
  waiting for transfers between devices  1.99 us (1%)
    all_to_all x7, blocking collectives, exchange(): return lax.all_to_all(rows, axes, split_axis=0, concat_axis=0, tiled=True)  124 us
    ppermute x3, starting transfers between devices, per_device(): lax.ppermute(duals, 'leg', [(i, (i + k) % 4) for i in range(4)])  6.5 us
    pallas_call x1, Pallas kernels, run_gram(): pl.pallas_call(gram_kernel, out_shape=(jax.ShapeDtypeStruct((GROUPS, SPAN...  4.4 us
    pallas_call x1, Pallas kernels, run_first(): pl.pallas_call(first_kernel, out_shape=(f32(N, N), f32(KEPT, N), f32(8, N...  4.33 us
    pallas_call x3, Pallas kernels, run_tile(): pl.pallas_call(kernel, out_shape=(f32(GROUPS, N), f32(N if turn == 2 else...  3.88 us
  transfers between devices with their start and end apart: 5, of which 1 were waited for; matrix products, arithmetic and copies ran while one was open for 0% of the time, Pallas kernels for 4%

profile of v8, /device:TPU:1, one launch (start us, length us, event | category | flops | bytes accessed | tf_op | source)
XLA Modules:
  0.0 150.6 jit_solution(6694432426494564)
XLA Ops:
  0.6 0.0 copy-start.2
  0.6 0.0 copy-start.1
  0.7 0.0 copy-start
  0.7 0.0 copy-start.4
  0.7 3.8 %collective-permute-start.1 = (f32[32,128]{1,0:T(8,128)}, f32[32,128]{1,0:T(8,128)S(1)}, u32[]{:S(2)}, u32[]{:S(2)}) collective-permute-start(f32[32,128]{1,0:T(8,128)} %dual0), channel_id=1, source_target_pairs={{0,2},{1,3},{2,0},{3,1},{4,6},{5,7},{6,4},{7,5},{8,10},{9,11},{10,... | collective-permute-start | bytes 49160 | tf_op jit(solution)/shard_map/ppermute | solution.py:550
  4.5 0.4 collective-permute-start
  4.9 2.3 %collective-permute-start.2 = (f32[32,128]{1,0:T(8,128)}, f32[32,128]{1,0:T(8,128)S(1)}, u32[]{:S(2)}, u32[]{:S(2)}) collective-permute-start(f32[32,128]{1,0:T(8,128)} %dual0), channel_id=1, source_target_pairs={{0,3},{1,0},{2,1},{3,2},{4,7},{5,4},{6,5},{7,6},{8,11},{9,8},{10,9... | collective-permute-start | bytes 49160 | tf_op jit(solution)/shard_map/ppermute | solution.py:550
  7.2 4.4 %gram.1 = (bf16[16,512,256]{2,1,0:T(8,128)(2,1)S(1)}, f32[128,64,128]{2,1,0:T(8,128)S(1)}, f32[64,64,128]{2,1,0:T(8,128)S(1)}, f32[512,128]{1,0:T(8,128)S(1)}, f...) custom-call(f32[16,4,128,128]{3,2,1,0:T(8,128)} %coeffs_in.1, ...), custom_call_target="tpu_custom_call" | custom-call | flops 1073741824 | bytes 12582912 | tf_op jit(solution)/shard_map/gram/pallas_call | solution.py:120
  11.6 0.0 collective-permute-done.1.dual2
  11.6 0.0 collective-permute-done.dual1
  11.6 0.0 collective-permute-done.2.dual3
  11.6 1.6 %collective-permute-start.3 = (f32[64,64,128]{2,1,0:T(8,128)S(1)}, f32[64,64,128]{2,1,0:T(8,128)S(1)}, u32[]{:S(2)}, u32[]{:S(2)}) collective-permute-start(f32[64,64,128]{2,1,0:T(8,128)S(1)} %get-tuple-element.38), channel_id=1, source_target_pairs={{0,4},{4,0},{1,5},{5,1},{2,6},{6,2},{3,7},{7,3},{8,12},{12,8},{9,1... | collective-permute-start | bytes 6291464 | tf_op jit(solution)/shard_map/ppermute | solution.py:557
  13.2 0.0 copy-done.2
  13.2 0.0 copy-done.1
  13.2 0.0 copy-done
  13.2 0.0 copy-done.4
  13.2 1.9 %rhs.1 = (f32[256,128]{1,0:T(8,128)S(1)}, f32[256,128]{1,0:T(8,128)S(1)}, f32[16,128]{1,0:T(8,128)S(1)}, f32[16,128]{1,0:T(8,128)S(1)}) custom-call(bf16[64,128]{1,0:T(8,128)(2,1)S(1)} %get-tuple-element.33.hot_rows.refs_0_, bf16[128,128]{1,0:T(8,128)(2,1)S(1)} %get-tuple-element.39.hot_place, bf16[16,512,256]{2,1,0:T(8,128)(2,1)S(1)} %get-tuple-element.35.tiles.refs_2_, ...), custom_call_target="tpu_custom_call" | custom-call | flops 134217728 | bytes 6291456 | tf_op jit(solution)/shard_map/rhs/pallas_call | solution.py:249
  15.1 0.1 collective-permute-start.4
  15.2 2.0 %collective-permute-done.4.small_got = f32[256,128]{1,0:T(8,128)S(1)} collective-permute-done((f32[256,128]{1,0:T(8,128)S(1)}, f32[256,128]{1,0:T(8,128)S(1)}, u32[]{:S(2)}, u32[]{:S(2)}) %collective-permute-start.4) | collective-permute-done | bytes 131104 | tf_op jit(solution)/shard_map/ppermute | solution.py:561
  17.2 0.0 collective-permute-done.3.got
  17.2 0.3 join.1
  17.5 0.0 copy-start.3
  17.5 39.1 %all_to_all.71 = f32[1088,4,128]{2,1,0:T(4,128)S(1)} all-to-all(f32[1088,4,128]{2,1,0:T(4,128)S(1)} %bitcast.24), channel_id=1, replica_groups=mesh['x'=4,'z'=4,'core'=2,'leg'=4] {'x','z','leg'}, dimensions={0} | all-to-all | bytes 4456448 | tf_op jit(solution)/shard_map/all_to_all | solution.py:543
  56.6 0.0 copy-done.3
  56.6 4.3 %first.1 = (f32[128,128]{1,0:T(8,128)S(1)}, f32[16,128]{1,0:T(8,128)S(1)}, f32[8,128]{1,0:T(8,128)S(1)}, f32[128,128]{1,0:T(8,128)S(1)}) custom-call(f32[4352,128]{1,0:T(8,128)S(1)} %bitcast.23, f32[32,128]{1,0:T(8,128)S(1)} %copy-done.3), custom_call_target="tpu_custom_call" | custom-call | tf_op jit(solution)/shard_map/first/pallas_call | solution.py:392
  60.9 15.0 %all_to_all.72 = f32[128,1,128]{2,1,0:T(1,128)S(1)} all-to-all(f32[128,1,128]{2,1,0:T(1,128)S(1)} %bitcast.36), channel_id=1, replica_groups=mesh['x'=4,'z'=4,'core'=2,'leg'=4] {'leg','x','core','z'}, dimensions={0} | all-to-all | bytes 131072 | tf_op jit(solution)/shard_map/all_to_all | solution.py:543
  75.9 1.5 %tile.2 = (f32[16,128]{1,0:T(8,128)S(1)}, f32[256,128]{1,0:T(8,128)S(1)}) custom-call(bf16[64,128]{1,0:T(8,128)(2,1)S(1)} %get-tuple-element.33.hot_rows.refs_0_, bf16[128,128]{1,0:T(8,128)(2,1)S(1)} %get-tuple-element.34.refs_1_, bf16[16,512,256]{2,1,0:T(8,128)(2,1)S(1)} %get-tuple-element.35.tiles.refs_2_, f32[128,128]{1,0:T(8,128)S(1)} %bitcast.25, ...), custom_call_target="tpu_custom_call" | custom-call | tf_op jit(solution)/shard_map/tile/pallas_call | solution.py:497
  77.5 14.2 %all_to_all.73 = f32[128,2,128]{2,1,0:T(2,128)S(1)} all-to-all(f32[128,2,128]{2,1,0:T(2,128)S(1)} %bitcast.34), channel_id=1, replica_groups=mesh['x'=4,'z'=4,'core'=2,'leg'=4] {'leg','x','core','z'}, dimensions={0} | all-to-all | bytes 262144 | tf_op jit(solution)/shard_map/all_to_all | solution.py:543
  91.7 0.3 owner.2
  92.0 13.6 %all_to_all.74 = f32[128,1,128]{2,1,0:T(1,128)S(1)} all-to-all(f32[128,1,128]{2,1,0:T(1,128)S(1)} %bitcast.38), channel_id=1, replica_groups=mesh['x'=4,'z'=4,'core'=2,'leg'=4] {'leg','x','core','z'}, dimensions={0} | all-to-all | bytes 131072 | tf_op jit(solution)/shard_map/all_to_all | solution.py:543
  105.6 1.5 %tile.3 = (f32[16,128]{1,0:T(8,128)S(1)}, f32[256,128]{1,0:T(8,128)S(1)}) custom-call(bf16[64,128]{1,0:T(8,128)(2,1)S(1)} %get-tuple-element.33.hot_rows.refs_0_, bf16[128,128]{1,0:T(8,128)(2,1)S(1)} %get-tuple-element.34.refs_1_, bf16[16,512,256]{2,1,0:T(8,128)(2,1)S(1)} %get-tuple-element.35.tiles.refs_2_, f32[128,128]{1,0:T(8,128)S(1)} %bitcast.27, ...), custom_call_target="tpu_custom_call" | custom-call | tf_op jit(solution)/shard_map/tile/pallas_call | solution.py:497
  107.2 14.2 %all_to_all.75 = f32[128,2,128]{2,1,0:T(2,128)S(1)} all-to-all(f32[128,2,128]{2,1,0:T(2,128)S(1)} %bitcast.35), channel_id=1, replica_groups=mesh['x'=4,'z'=4,'core'=2,'leg'=4] {'leg','x','core','z'}, dimensions={0} | all-to-all | bytes 262144 | tf_op jit(solution)/shard_map/all_to_all | solution.py:543
  121.4 0.3 owner.3
  121.7 13.6 %all_to_all.76 = f32[128,1,128]{2,1,0:T(1,128)S(1)} all-to-all(f32[128,1,128]{2,1,0:T(1,128)S(1)} %bitcast.39), channel_id=1, replica_groups=mesh['x'=4,'z'=4,'core'=2,'leg'=4] {'leg','x','core','z'}, dimensions={0} | all-to-all | bytes 131072 | tf_op jit(solution)/shard_map/all_to_all | solution.py:543
  135.4 0.8 tile_last.1
  136.2 13.7 %all_to_all.77 = f32[128,1,128]{2,1,0:T(1,128)S(1)} all-to-all(f32[128,1,128]{2,1,0:T(1,128)S(1)} %bitcast.37), channel_id=1, replica_groups=mesh['x'=4,'z'=4,'core'=2,'leg'=4] {'leg','x','core','z'}, dimensions={0} | all-to-all | bytes 131072 | tf_op jit(solution)/shard_map/all_to_all | solution.py:543
  149.9 0.7 final.1
Async XLA Ops:
  0.6 12.6 %copy-start.2 = (f32[32,128]{1,0:T(8,128)S(1)}, f32[32,128]{1,0:T(8,128)}, u32[]{:S(2)}) copy-start(f32[32,128]{1,0:T(8,128)} %dual0) | copy-start | bytes 49156
  0.6 12.6 %copy-start.1 = (f32[16,128]{1,0:T(8,128)S(1)}, f32[16,128]{1,0:T(8,128)}, u32[]{:S(2)}) copy-start(f32[16,128]{1,0:T(8,128)} %slack.1) | copy-start | bytes 24580
  0.7 12.6 %copy-start = (f32[16,128]{1,0:T(8,128)S(1)}, f32[16,128]{1,0:T(8,128)}, u32[]{:S(2)}) copy-start(f32[16,128]{1,0:T(8,128)} %primal.1) | copy-start | bytes 24580
  0.7 12.6 %copy-start.4 = (f32[16,128]{1,0:T(8,128)S(1)}, f32[16,128]{1,0:T(8,128)}, u32[]{:S(2)}) copy-start(f32[16,128]{1,0:T(8,128)} %cost.1) | copy-start | bytes 24580
  0.7 10.9 %collective-permute-start.1 = (f32[32,128]{1,0:T(8,128)}, f32[32,128]{1,0:T(8,128)S(1)}, u32[]{:S(2)}, u32[]{:S(2)}) collective-permute-start(f32[32,128]{1,0:T(8,128)} %dual0), channel_id=1, source_target_pairs={{0,2},{1,3},{2,0},{3,1},{4,6},{5,7},{6,4},{7,5},{8,10},{9,11},{10,... | collective-permute-start | bytes 49160 | tf_op jit(solution)/shard_map/ppermute | solution.py:550
  4.5 7.1 %collective-permute-start = (f32[32,128]{1,0:T(8,128)}, f32[32,128]{1,0:T(8,128)S(1)}, u32[]{:S(2)}, u32[]{:S(2)}) collective-permute-start(f32[32,128]{1,0:T(8,128)} %dual0), channel_id=1, source_target_pairs={{0,1},{1,2},{2,3},{3,0},{4,5},{5,6},{6,7},{7,4},{8,9},{9,10},{10,1... | collective-permute-start | bytes 49160 | tf_op jit(solution)/shard_map/ppermute | solution.py:550
  4.9 6.7 %collective-permute-start.2 = (f32[32,128]{1,0:T(8,128)}, f32[32,128]{1,0:T(8,128)S(1)}, u32[]{:S(2)}, u32[]{:S(2)}) collective-permute-start(f32[32,128]{1,0:T(8,128)} %dual0), channel_id=1, source_target_pairs={{0,3},{1,0},{2,1},{3,2},{4,7},{5,4},{6,5},{7,6},{8,11},{9,8},{10,9... | collective-permute-start | bytes 49160 | tf_op jit(solution)/shard_map/ppermute | solution.py:550
  11.6 5.6 %collective-permute-start.3 = (f32[64,64,128]{2,1,0:T(8,128)S(1)}, f32[64,64,128]{2,1,0:T(8,128)S(1)}, u32[]{:S(2)}, u32[]{:S(2)}) collective-permute-start(f32[64,64,128]{2,1,0:T(8,128)S(1)} %get-tuple-element.38), channel_id=1, source_target_pairs={{0,4},{4,0},{1,5},{5,1},{2,6},{6,2},{3,7},{7,3},{8,12},{12,8},{9,1... | collective-permute-start | bytes 6291464 | tf_op jit(solution)/shard_map/ppermute | solution.py:557
  15.1 2.1 %collective-permute-start.4 = (f32[256,128]{1,0:T(8,128)S(1)}, f32[256,128]{1,0:T(8,128)S(1)}, u32[]{:S(2)}, u32[]{:S(2)}) collective-permute-start(f32[256,128]{1,0:T(8,128)S(1)} %get-tuple-element.47), channel_id=1, source_target_pairs={{0,4},{4,0},{1,5},{5,1},{2,6},{6,2},{3,7},{7,3},{8,12},{12,8},{9,1... | collective-permute-start | bytes 393224 | tf_op jit(solution)/shard_map/ppermute | solution.py:561
  17.5 39.1 %copy-start.3 = (f32[32,128]{1,0:T(8,128)S(1)}, f32[32,128]{1,0:T(8,128)}, u32[]{:S(2)}) copy-start(f32[32,128]{1,0:T(8,128)} %demand.1) | copy-start | bytes 49156

commit v9 on v8

--- a/solution.py
+++ b/solution.py
@@ -103,12 +103,13 @@
             packed = jnp.where(lower, gram[:HALF], rolled)
             line = jnp.sum(jnp.where(row == lane, rolled, 0.0), axis=0, keepdims=True)
             block = ids[s, g]
+            owner = (block & 4) << 4 | (block >> 5) << 4 | ((block >> 3) & 3) << 2 | block & 3
             chip = (((block >> 3) & 3) << 4) | ((block & 3) << 2) | (block >> 5)
             place = (((block >> 2) & 1) ^ core) * HALF + chip
             acc[place] += packed
             small[pl.ds(place * EXTRA, 1), :] += line
             t = g * SPAN + s
-            hot[t : t + 1, :] = (line_lane == block).astype(jnp.float32)
+            hot[t : t + 1, :] = (line_lane == owner).astype(jnp.float32)
             hot2[t : t + 1, :] = (line_lane == place).astype(jnp.float32)
     other[...] = acc[pl.ds(HALF, HALF)]
     hot_rows[...] = hot[:TILES, :].astype(jnp.bfloat16)
@@ -220,7 +221,10 @@
     leg = lax.axis_index("leg")
     for k, part in enumerate((dual0, dual1, dual2, dual3)):
         at = pl.multiple_of(((leg - k) & 3) * 32, 32)
-        duals[pl.ds(at, 32), :] = part[...]
+        at = pl.multiple_of(at // 2, 16)
+        for core in range(2):
+            rows = [part[8 * x + 4 * core : 8 * x + 4 * core + 4, :] for x in range(4)]
+            duals[pl.ds(HALF * core + at, 16), :] = jnp.concatenate(rows, axis=0)
     used = root[...] > 0.0
     valid = used.astype(jnp.float32)
     transpose_apply(hot_rows[...], tiles, duals, applied)
@@ -513,13 +517,18 @@
     len2 = norm / curve
     len0, len1 = kept1[STEP : STEP + 1, :], kept2[STEP : STEP + 1, :]
     beta1 = kept2[BETA : BETA + 1, :]
-    at = pl.ds(pl.multiple_of(lax.axis_index("leg") * 32, 32), 32)
+    at = pl.multiple_of(lax.axis_index("leg") * 16, 16)
 
     def step(v0, v1, v2):
         second = v1 + beta1 * v0
         return len0 * v0 + len1 * second + len2 * (v2 + beta2 * second)
 
-    step_dual[...] = step(z0[at, :], z1[at, :], z2[at, :])
+    for core in range(2):
+        mine = pl.ds(HALF * core + at, 16)
+        part = step(z0[mine, :], z1[mine, :], z2[mine, :])
+        for x in range(4):
+            row = 8 * x + 4 * core
+            step_dual[row : row + 4, :] = part[4 * x : 4 * x + 4]
     applied = step(a0[...], a1[...], a2[...])
     step_primal[...] = root[...] * applied + (mu[0:1, :] * ratio[...] + base[...])
 
@@ -535,7 +544,7 @@
     )(*args)
 
 
-ALL = ("leg", "x", "core", "z")
+ALL = ("core", "leg", "x", "z")
 CHIPS = ("x", "z", "leg")
 
 

time: 151 us -> 150 us (level)
  no operation moved by 1% of the time
where the time goes in v9:
time: 150 us
  blocking collectives  123 us (82%)
  Pallas kernels  16.2 us (11%)
  starting transfers between devices  8.22 us (5%)
  waiting for transfers between devices  1.98 us (1%)
    all_to_all x7, blocking collectives, exchange(): return lax.all_to_all(rows, axes, split_axis=0, concat_axis=0, tiled=True)  123 us
    ppermute x3, starting transfers between devices, per_device(): lax.ppermute(duals, 'leg', [(i, (i + k) % 4) for i in range(4)])  6.5 us
    pallas_call x1, Pallas kernels, run_gram(): pl.pallas_call(gram_kernel, out_shape=(jax.ShapeDtypeStruct((GROUPS, SPAN...  4.44 us
    pallas_call x1, Pallas kernels, run_first(): pl.pallas_call(first_kernel, out_shape=(f32(N, N), f32(KEPT, N), f32(8, N...  4.33 us
    pallas_call x3, Pallas kernels, run_tile(): pl.pallas_call(kernel, out_shape=(f32(GROUPS, N), f32(N if turn == 2 else...  3.88 us
  transfers between devices with their start and end apart: 5, of which 1 were waited for; matrix products, arithmetic and copies ran while one was open for 0% of the time, Pallas kernels for 4%

profile of v9, /device:TPU:1, one launch (start us, length us, event | category | flops | bytes accessed | tf_op | source)
XLA Modules:
  0.0 150.0 jit_solution(12024532160781780057)
XLA Ops:
  0.6 0.0 copy-start.2
  0.6 0.0 copy-start.1
  0.7 0.0 copy-start
  0.7 0.0 copy-start.4
  0.7 3.8 %collective-permute-start.1 = (f32[32,128]{1,0:T(8,128)}, f32[32,128]{1,0:T(8,128)S(1)}, u32[]{:S(2)}, u32[]{:S(2)}) collective-permute-start(f32[32,128]{1,0:T(8,128)} %dual0), channel_id=1, source_target_pairs={{0,2},{1,3},{2,0},{3,1},{4,6},{5,7},{6,4},{7,5},{8,10},{9,11},{10,... | collective-permute-start | bytes 49160 | tf_op jit(solution)/shard_map/ppermute | solution.py:559
  4.5 0.4 collective-permute-start
  4.9 2.3 %collective-permute-start.2 = (f32[32,128]{1,0:T(8,128)}, f32[32,128]{1,0:T(8,128)S(1)}, u32[]{:S(2)}, u32[]{:S(2)}) collective-permute-start(f32[32,128]{1,0:T(8,128)} %dual0), channel_id=1, source_target_pairs={{0,3},{1,0},{2,1},{3,2},{4,7},{5,4},{6,5},{7,6},{8,11},{9,8},{10,9... | collective-permute-start | bytes 49160 | tf_op jit(solution)/shard_map/ppermute | solution.py:559
  7.2 4.4 %gram.1 = (bf16[16,512,256]{2,1,0:T(8,128)(2,1)S(1)}, f32[128,64,128]{2,1,0:T(8,128)S(1)}, f32[64,64,128]{2,1,0:T(8,128)S(1)}, f32[512,128]{1,0:T(8,128)S(1)}, f...) custom-call(f32[16,4,128,128]{3,2,1,0:T(8,128)} %coeffs_in.1, ...), custom_call_target="tpu_custom_call" | custom-call | flops 1073741824 | bytes 12582912 | tf_op jit(solution)/shard_map/gram/pallas_call | solution.py:121
  11.6 0.0 collective-permute-done.1.dual2
  11.6 0.0 collective-permute-done.dual1
  11.6 0.0 collective-permute-done.2.dual3
  11.7 1.6 %collective-permute-start.3 = (f32[64,64,128]{2,1,0:T(8,128)S(1)}, f32[64,64,128]{2,1,0:T(8,128)S(1)}, u32[]{:S(2)}, u32[]{:S(2)}) collective-permute-start(f32[64,64,128]{2,1,0:T(8,128)S(1)} %get-tuple-element.38), channel_id=1, source_target_pairs={{0,4},{4,0},{1,5},{5,1},{2,6},{6,2},{3,7},{7,3},{8,12},{12,8},{9,1... | collective-permute-start | bytes 6291464 | tf_op jit(solution)/shard_map/ppermute | solution.py:566
  13.3 0.0 copy-done.2
  13.3 0.0 copy-done.1
  13.3 0.0 copy-done
  13.3 0.0 copy-done.4
  13.3 1.9 %rhs.1 = (f32[256,128]{1,0:T(8,128)S(1)}, f32[256,128]{1,0:T(8,128)S(1)}, f32[16,128]{1,0:T(8,128)S(1)}, f32[16,128]{1,0:T(8,128)S(1)}) custom-call(bf16[64,128]{1,0:T(8,128)(2,1)S(1)} %get-tuple-element.33.hot_rows.refs_0_, bf16[128,128]{1,0:T(8,128)(2,1)S(1)} %get-tuple-element.39.hot_place, bf16[16,512,256]{2,1,0:T(8,128)(2,1)S(1)} %get-tuple-element.35.tiles.refs_2_, ...), custom_call_target="tpu_custom_call" | custom-call | flops 134217728 | bytes 6291456 | tf_op jit(solution)/shard_map/rhs/pallas_call | solution.py:253
  15.1 0.1 collective-permute-start.4
  15.3 2.0 %collective-permute-done.4.small_got = f32[256,128]{1,0:T(8,128)S(1)} collective-permute-done((f32[256,128]{1,0:T(8,128)S(1)}, f32[256,128]{1,0:T(8,128)S(1)}, u32[]{:S(2)}, u32[]{:S(2)}) %collective-permute-start.4) | collective-permute-done | bytes 131104 | tf_op jit(solution)/shard_map/ppermute | solution.py:570
  17.2 0.0 collective-permute-done.3.got
  17.2 0.3 join.1
  17.5 0.0 copy-start.3
  17.5 39.0 %all_to_all.71 = f32[1088,4,128]{2,1,0:T(4,128)S(1)} all-to-all(f32[1088,4,128]{2,1,0:T(4,128)S(1)} %bitcast.24), channel_id=1, replica_groups=mesh['x'=4,'z'=4,'core'=2,'leg'=4] {'x','z','leg'}, dimensions={0} | all-to-all | bytes 4456448 | tf_op jit(solution)/shard_map/all_to_all | solution.py:552
  56.6 0.0 copy-done.3
  56.6 4.3 %first.1 = (f32[128,128]{1,0:T(8,128)S(1)}, f32[16,128]{1,0:T(8,128)S(1)}, f32[8,128]{1,0:T(8,128)S(1)}, f32[128,128]{1,0:T(8,128)S(1)}) custom-call(f32[4352,128]{1,0:T(8,128)S(1)} %bitcast.23, f32[32,128]{1,0:T(8,128)S(1)} %copy-done.3), custom_call_target="tpu_custom_call" | custom-call | tf_op jit(solution)/shard_map/first/pallas_call | solution.py:396
  60.9 14.7 %all_to_all.72 = f32[128,1,128]{2,1,0:T(1,128)S(1)} all-to-all(f32[128,1,128]{2,1,0:T(1,128)S(1)} %bitcast.36), channel_id=1, replica_groups=mesh['x'=4,'z'=4,'core'=2,'leg'=4] {'core','leg','x','z'}, dimensions={0} | all-to-all | bytes 131072 | tf_op jit(solution)/shard_map/all_to_all | solution.py:552
  75.6 1.5 %tile.2 = (f32[16,128]{1,0:T(8,128)S(1)}, f32[256,128]{1,0:T(8,128)S(1)}) custom-call(bf16[64,128]{1,0:T(8,128)(2,1)S(1)} %get-tuple-element.33.hot_rows.refs_0_, bf16[128,128]{1,0:T(8,128)(2,1)S(1)} %get-tuple-element.34.refs_1_, bf16[16,512,256]{2,1,0:T(8,128)(2,1)S(1)} %get-tuple-element.35.tiles.refs_2_, f32[128,128]{1,0:T(8,128)S(1)} %bitcast.25, ...), custom_call_target="tpu_custom_call" | custom-call | tf_op jit(solution)/shard_map/tile/pallas_call | solution.py:501
  77.2 14.2 %all_to_all.73 = f32[128,2,128]{2,1,0:T(2,128)S(1)} all-to-all(f32[128,2,128]{2,1,0:T(2,128)S(1)} %bitcast.34), channel_id=1, replica_groups=mesh['x'=4,'z'=4,'core'=2,'leg'=4] {'core','leg','x','z'}, dimensions={0} | all-to-all | bytes 262144 | tf_op jit(solution)/shard_map/all_to_all | solution.py:552
  91.4 0.3 owner.2
  91.7 13.5 %all_to_all.74 = f32[128,1,128]{2,1,0:T(1,128)S(1)} all-to-all(f32[128,1,128]{2,1,0:T(1,128)S(1)} %bitcast.38), channel_id=1, replica_groups=mesh['x'=4,'z'=4,'core'=2,'leg'=4] {'core','leg','x','z'}, dimensions={0} | all-to-all | bytes 131072 | tf_op jit(solution)/shard_map/all_to_all | solution.py:552
  105.2 1.5 %tile.3 = (f32[16,128]{1,0:T(8,128)S(1)}, f32[256,128]{1,0:T(8,128)S(1)}) custom-call(bf16[64,128]{1,0:T(8,128)(2,1)S(1)} %get-tuple-element.33.hot_rows.refs_0_, bf16[128,128]{1,0:T(8,128)(2,1)S(1)} %get-tuple-element.34.refs_1_, bf16[16,512,256]{2,1,0:T(8,128)(2,1)S(1)} %get-tuple-element.35.tiles.refs_2_, f32[128,128]{1,0:T(8,128)S(1)} %bitcast.27, ...), custom_call_target="tpu_custom_call" | custom-call | tf_op jit(solution)/shard_map/tile/pallas_call | solution.py:501
  106.7 14.2 %all_to_all.75 = f32[128,2,128]{2,1,0:T(2,128)S(1)} all-to-all(f32[128,2,128]{2,1,0:T(2,128)S(1)} %bitcast.35), channel_id=1, replica_groups=mesh['x'=4,'z'=4,'core'=2,'leg'=4] {'core','leg','x','z'}, dimensions={0} | all-to-all | bytes 262144 | tf_op jit(solution)/shard_map/all_to_all | solution.py:552
  120.9 0.3 owner.3
  121.3 13.5 %all_to_all.76 = f32[128,1,128]{2,1,0:T(1,128)S(1)} all-to-all(f32[128,1,128]{2,1,0:T(1,128)S(1)} %bitcast.39), channel_id=1, replica_groups=mesh['x'=4,'z'=4,'core'=2,'leg'=4] {'core','leg','x','z'}, dimensions={0} | all-to-all | bytes 131072 | tf_op jit(solution)/shard_map/all_to_all | solution.py:552
  134.7 0.8 tile_last.1
  135.6 13.7 %all_to_all.77 = f32[128,1,128]{2,1,0:T(1,128)S(1)} all-to-all(f32[128,1,128]{2,1,0:T(1,128)S(1)} %bitcast.37), channel_id=1, replica_groups=mesh['x'=4,'z'=4,'core'=2,'leg'=4] {'core','leg','x','z'}, dimensions={0} | all-to-all | bytes 131072 | tf_op jit(solution)/shard_map/all_to_all | solution.py:552
  149.3 0.7 final.1
Async XLA Ops:
  0.6 12.6 %copy-start.2 = (f32[32,128]{1,0:T(8,128)S(1)}, f32[32,128]{1,0:T(8,128)}, u32[]{:S(2)}) copy-start(f32[32,128]{1,0:T(8,128)} %dual0) | copy-start | bytes 49156
  0.6 12.6 %copy-start.1 = (f32[16,128]{1,0:T(8,128)S(1)}, f32[16,128]{1,0:T(8,128)}, u32[]{:S(2)}) copy-start(f32[16,128]{1,0:T(8,128)} %slack.1) | copy-start | bytes 24580
  0.7 12.6 %copy-start = (f32[16,128]{1,0:T(8,128)S(1)}, f32[16,128]{1,0:T(8,128)}, u32[]{:S(2)}) copy-start(f32[16,128]{1,0:T(8,128)} %primal.1) | copy-start | bytes 24580
  0.7 12.6 %copy-start.4 = (f32[16,128]{1,0:T(8,128)S(1)}, f32[16,128]{1,0:T(8,128)}, u32[]{:S(2)}) copy-start(f32[16,128]{1,0:T(8,128)} %cost.1) | copy-start | bytes 24580
  0.7 11.0 %collective-permute-start.1 = (f32[32,128]{1,0:T(8,128)}, f32[32,128]{1,0:T(8,128)S(1)}, u32[]{:S(2)}, u32[]{:S(2)}) collective-permute-start(f32[32,128]{1,0:T(8,128)} %dual0), channel_id=1, source_target_pairs={{0,2},{1,3},{2,0},{3,1},{4,6},{5,7},{6,4},{7,5},{8,10},{9,11},{10,... | collective-permute-start | bytes 49160 | tf_op jit(solution)/shard_map/ppermute | solution.py:559
  4.5 7.1 %collective-permute-start = (f32[32,128]{1,0:T(8,128)}, f32[32,128]{1,0:T(8,128)S(1)}, u32[]{:S(2)}, u32[]{:S(2)}) collective-permute-start(f32[32,128]{1,0:T(8,128)} %dual0), channel_id=1, source_target_pairs={{0,1},{1,2},{2,3},{3,0},{4,5},{5,6},{6,7},{7,4},{8,9},{9,10},{10,1... | collective-permute-start | bytes 49160 | tf_op jit(solution)/shard_map/ppermute | solution.py:559
  4.9 6.8 %collective-permute-start.2 = (f32[32,128]{1,0:T(8,128)}, f32[32,128]{1,0:T(8,128)S(1)}, u32[]{:S(2)}, u32[]{:S(2)}) collective-permute-start(f32[32,128]{1,0:T(8,128)} %dual0), channel_id=1, source_target_pairs={{0,3},{1,0},{2,1},{3,2},{4,7},{5,4},{6,5},{7,6},{8,11},{9,8},{10,9... | collective-permute-start | bytes 49160 | tf_op jit(solution)/shard_map/ppermute | solution.py:559
  11.7 5.6 %collective-permute-start.3 = (f32[64,64,128]{2,1,0:T(8,128)S(1)}, f32[64,64,128]{2,1,0:T(8,128)S(1)}, u32[]{:S(2)}, u32[]{:S(2)}) collective-permute-start(f32[64,64,128]{2,1,0:T(8,128)S(1)} %get-tuple-element.38), channel_id=1, source_target_pairs={{0,4},{4,0},{1,5},{5,1},{2,6},{6,2},{3,7},{7,3},{8,12},{12,8},{9,1... | collective-permute-start | bytes 6291464 | tf_op jit(solution)/shard_map/ppermute | solution.py:566
  15.1 2.1 %collective-permute-start.4 = (f32[256,128]{1,0:T(8,128)S(1)}, f32[256,128]{1,0:T(8,128)S(1)}, u32[]{:S(2)}, u32[]{:S(2)}) collective-permute-start(f32[256,128]{1,0:T(8,128)S(1)} %get-tuple-element.47), channel_id=1, source_target_pairs={{0,4},{4,0},{1,5},{5,1},{2,6},{6,2},{3,7},{7,3},{8,12},{12,8},{9,1... | collective-permute-start | bytes 393224 | tf_op jit(solution)/shard_map/ppermute | solution.py:570
  17.5 39.1 %copy-start.3 = (f32[32,128]{1,0:T(8,128)S(1)}, f32[32,128]{1,0:T(8,128)}, u32[]{:S(2)}) copy-start(f32[32,128]{1,0:T(8,128)} %demand.1) | copy-start | bytes 49156

commit v10 on v9

--- a/solution.py
+++ b/solution.py
@@ -219,7 +219,7 @@
     own_out, other_out, base_out, scale_out, spread, spread2, duals, applied,
 ):
     leg = lax.axis_index("leg")
-    for k, part in enumerate((dual0, dual1, dual2, dual3)):
+    for k, part in ((0, dual0), (2, dual1), (1, dual2), (3, dual3)):
         at = pl.multiple_of(((leg - k) & 3) * 32, 32)
         at = pl.multiple_of(at // 2, 16)
         for core in range(2):
@@ -555,7 +555,7 @@
 def per_device(coeffs, block_ids, col_counts, primal, slack, cost, duals, demand):
     ids = block_ids.T
     parts = [duals]
-    for k in (1, 2, 3):
+    for k in (2, 1, 3):
         parts.append(lax.ppermute(duals, "leg", [(i, (i + k) % 4) for i in range(4)]))
 
     tiles, acc, other, small, root, hot_rows, hot, hot_place = run_gram(

time: 150 us -> 150 us (level)
  no operation moved by 1% of the time
where the time goes in v10:
time: 150 us; the launch traced here: 149 us
  blocking collectives  123 us (82%)
  Pallas kernels  16.2 us (11%)
  starting transfers between devices  7.59 us (5%)
  waiting for transfers between devices  1.98 us (1%)
    all_to_all x7, blocking collectives, exchange(): return lax.all_to_all(rows, axes, split_axis=0, concat_axis=0, tiled=True)  123 us
    ppermute x3, starting transfers between devices, per_device(): lax.ppermute(duals, 'leg', [(i, (i + k) % 4) for i in range(4)])  5.88 us
    pallas_call x1, Pallas kernels, run_gram(): pl.pallas_call(gram_kernel, out_shape=(jax.ShapeDtypeStruct((GROUPS, SPAN...  4.46 us
    pallas_call x1, Pallas kernels, run_first(): pl.pallas_call(first_kernel, out_shape=(f32(N, N), f32(KEPT, N), f32(8, N...  4.33 us
    pallas_call x3, Pallas kernels, run_tile(): pl.pallas_call(kernel, out_shape=(f32(GROUPS, N), f32(N if turn == 2 else...  3.88 us
  transfers between devices with their start and end apart: 5, of which 1 were waited for; matrix products, arithmetic and copies ran while one was open for 0% of the time, Pallas kernels for 4%

profile of v10, /device:TPU:1, one launch (start us, length us, event | category | flops | bytes accessed | tf_op | source)
XLA Modules:
  0.0 149.4 jit_solution(12467797090158000472)
XLA Ops:
  0.6 0.0 copy-start.2
  0.6 0.0 copy-start.1
  0.7 0.0 copy-start
  0.7 0.0 copy-start.4
  0.7 2.2 %collective-permute-start.1 = (f32[32,128]{1,0:T(8,128)}, f32[32,128]{1,0:T(8,128)S(1)}, u32[]{:S(2)}, u32[]{:S(2)}) collective-permute-start(f32[32,128]{1,0:T(8,128)} %dual0), channel_id=1, source_target_pairs={{0,1},{1,2},{2,3},{3,0},{4,5},{5,6},{6,7},{7,4},{8,9},{9,10},{10,1... | collective-permute-start | bytes 49160 | tf_op jit(solution)/shard_map/ppermute | solution.py:559
  2.9 2.6 %collective-permute-start = (f32[32,128]{1,0:T(8,128)}, f32[32,128]{1,0:T(8,128)S(1)}, u32[]{:S(2)}, u32[]{:S(2)}) collective-permute-start(f32[32,128]{1,0:T(8,128)} %dual0), channel_id=1, source_target_pairs={{0,2},{1,3},{2,0},{3,1},{4,6},{5,7},{6,4},{7,5},{8,10},{9,11},{10,... | collective-permute-start | bytes 49160 | tf_op jit(solution)/shard_map/ppermute | solution.py:559
  5.5 1.1 collective-permute-start.2
  6.6 4.5 %gram.1 = (bf16[16,512,256]{2,1,0:T(8,128)(2,1)S(1)}, f32[128,64,128]{2,1,0:T(8,128)S(1)}, f32[64,64,128]{2,1,0:T(8,128)S(1)}, f32[512,128]{1,0:T(8,128)S(1)}, f...) custom-call(f32[16,4,128,128]{3,2,1,0:T(8,128)} %coeffs_in.1, ...), custom_call_target="tpu_custom_call" | custom-call | flops 1073741824 | bytes 12582912 | tf_op jit(solution)/shard_map/gram/pallas_call | solution.py:121
  11.0 0.0 collective-permute-done.1.dual2
  11.0 0.0 collective-permute-done.dual1
  11.0 0.0 collective-permute-done.2.dual3
  11.1 1.6 %collective-permute-start.3 = (f32[64,64,128]{2,1,0:T(8,128)S(1)}, f32[64,64,128]{2,1,0:T(8,128)S(1)}, u32[]{:S(2)}, u32[]{:S(2)}) collective-permute-start(f32[64,64,128]{2,1,0:T(8,128)S(1)} %get-tuple-element.38), channel_id=1, source_target_pairs={{0,4},{4,0},{1,5},{5,1},{2,6},{6,2},{3,7},{7,3},{8,12},{12,8},{9,1... | collective-permute-start | bytes 6291464 | tf_op jit(solution)/shard_map/ppermute | solution.py:566
  12.6 0.0 copy-done.2
  12.6 0.0 copy-done.1
  12.6 0.0 copy-done
  12.6 0.0 copy-done.4
  12.7 1.9 %rhs.1 = (f32[256,128]{1,0:T(8,128)S(1)}, f32[256,128]{1,0:T(8,128)S(1)}, f32[16,128]{1,0:T(8,128)S(1)}, f32[16,128]{1,0:T(8,128)S(1)}) custom-call(bf16[64,128]{1,0:T(8,128)(2,1)S(1)} %get-tuple-element.33.hot_rows.refs_0_, bf16[128,128]{1,0:T(8,128)(2,1)S(1)} %get-tuple-element.39.hot_place, bf16[16,512,256]{2,1,0:T(8,128)(2,1)S(1)} %get-tuple-element.35.tiles.refs_2_, ...), custom_call_target="tpu_custom_call" | custom-call | flops 134217728 | bytes 6291456 | tf_op jit(solution)/shard_map/rhs/pallas_call | solution.py:253
  14.5 0.1 collective-permute-start.4
  14.6 2.0 %collective-permute-done.4.small_got = f32[256,128]{1,0:T(8,128)S(1)} collective-permute-done((f32[256,128]{1,0:T(8,128)S(1)}, f32[256,128]{1,0:T(8,128)S(1)}, u32[]{:S(2)}, u32[]{:S(2)}) %collective-permute-start.4) | collective-permute-done | bytes 131104 | tf_op jit(solution)/shard_map/ppermute | solution.py:570
  16.6 0.0 collective-permute-done.3.got
  16.6 0.3 join.1
  16.9 0.0 copy-start.3
  16.9 39.1 %all_to_all.71 = f32[1088,4,128]{2,1,0:T(4,128)S(1)} all-to-all(f32[1088,4,128]{2,1,0:T(4,128)S(1)} %bitcast.24), channel_id=1, replica_groups=mesh['x'=4,'z'=4,'core'=2,'leg'=4] {'x','z','leg'}, dimensions={0} | all-to-all | bytes 4456448 | tf_op jit(solution)/shard_map/all_to_all | solution.py:552
  56.0 0.0 copy-done.3
  56.0 4.3 %first.1 = (f32[128,128]{1,0:T(8,128)S(1)}, f32[16,128]{1,0:T(8,128)S(1)}, f32[8,128]{1,0:T(8,128)S(1)}, f32[128,128]{1,0:T(8,128)S(1)}) custom-call(f32[4352,128]{1,0:T(8,128)S(1)} %bitcast.23, f32[32,128]{1,0:T(8,128)S(1)} %copy-done.3), custom_call_target="tpu_custom_call" | custom-call | tf_op jit(solution)/shard_map/first/pallas_call | solution.py:396
  60.4 14.7 %all_to_all.72 = f32[128,1,128]{2,1,0:T(1,128)S(1)} all-to-all(f32[128,1,128]{2,1,0:T(1,128)S(1)} %bitcast.36), channel_id=1, replica_groups=mesh['x'=4,'z'=4,'core'=2,'leg'=4] {'core','leg','x','z'}, dimensions={0} | all-to-all | bytes 131072 | tf_op jit(solution)/shard_map/all_to_all | solution.py:552
  75.1 1.5 %tile.2 = (f32[16,128]{1,0:T(8,128)S(1)}, f32[256,128]{1,0:T(8,128)S(1)}) custom-call(bf16[64,128]{1,0:T(8,128)(2,1)S(1)} %get-tuple-element.33.hot_rows.refs_0_, bf16[128,128]{1,0:T(8,128)(2,1)S(1)} %get-tuple-element.34.refs_1_, bf16[16,512,256]{2,1,0:T(8,128)(2,1)S(1)} %get-tuple-element.35.tiles.refs_2_, f32[128,128]{1,0:T(8,128)S(1)} %bitcast.25, ...), custom_call_target="tpu_custom_call" | custom-call | tf_op jit(solution)/shard_map/tile/pallas_call | solution.py:501
  76.6 14.2 %all_to_all.73 = f32[128,2,128]{2,1,0:T(2,128)S(1)} all-to-all(f32[128,2,128]{2,1,0:T(2,128)S(1)} %bitcast.34), channel_id=1, replica_groups=mesh['x'=4,'z'=4,'core'=2,'leg'=4] {'core','leg','x','z'}, dimensions={0} | all-to-all | bytes 262144 | tf_op jit(solution)/shard_map/all_to_all | solution.py:552
  90.8 0.3 owner.2
  91.2 13.5 %all_to_all.74 = f32[128,1,128]{2,1,0:T(1,128)S(1)} all-to-all(f32[128,1,128]{2,1,0:T(1,128)S(1)} %bitcast.38), channel_id=1, replica_groups=mesh['x'=4,'z'=4,'core'=2,'leg'=4] {'core','leg','x','z'}, dimensions={0} | all-to-all | bytes 131072 | tf_op jit(solution)/shard_map/all_to_all | solution.py:552
  104.6 1.5 %tile.3 = (f32[16,128]{1,0:T(8,128)S(1)}, f32[256,128]{1,0:T(8,128)S(1)}) custom-call(bf16[64,128]{1,0:T(8,128)(2,1)S(1)} %get-tuple-element.33.hot_rows.refs_0_, bf16[128,128]{1,0:T(8,128)(2,1)S(1)} %get-tuple-element.34.refs_1_, bf16[16,512,256]{2,1,0:T(8,128)(2,1)S(1)} %get-tuple-element.35.tiles.refs_2_, f32[128,128]{1,0:T(8,128)S(1)} %bitcast.27, ...), custom_call_target="tpu_custom_call" | custom-call | tf_op jit(solution)/shard_map/tile/pallas_call | solution.py:501
  106.2 14.2 %all_to_all.75 = f32[128,2,128]{2,1,0:T(2,128)S(1)} all-to-all(f32[128,2,128]{2,1,0:T(2,128)S(1)} %bitcast.35), channel_id=1, replica_groups=mesh['x'=4,'z'=4,'core'=2,'leg'=4] {'core','leg','x','z'}, dimensions={0} | all-to-all | bytes 262144 | tf_op jit(solution)/shard_map/all_to_all | solution.py:552
  120.4 0.3 owner.3
  120.7 13.5 %all_to_all.76 = f32[128,1,128]{2,1,0:T(1,128)S(1)} all-to-all(f32[128,1,128]{2,1,0:T(1,128)S(1)} %bitcast.39), channel_id=1, replica_groups=mesh['x'=4,'z'=4,'core'=2,'leg'=4] {'core','leg','x','z'}, dimensions={0} | all-to-all | bytes 131072 | tf_op jit(solution)/shard_map/all_to_all | solution.py:552
  134.2 0.8 tile_last.1
  135.0 13.7 %all_to_all.77 = f32[128,1,128]{2,1,0:T(1,128)S(1)} all-to-all(f32[128,1,128]{2,1,0:T(1,128)S(1)} %bitcast.37), channel_id=1, replica_groups=mesh['x'=4,'z'=4,'core'=2,'leg'=4] {'core','leg','x','z'}, dimensions={0} | all-to-all | bytes 131072 | tf_op jit(solution)/shard_map/all_to_all | solution.py:552
  148.7 0.7 final.1
Async XLA Ops:
  0.6 12.0 %copy-start.2 = (f32[32,128]{1,0:T(8,128)S(1)}, f32[32,128]{1,0:T(8,128)}, u32[]{:S(2)}) copy-start(f32[32,128]{1,0:T(8,128)} %dual0) | copy-start | bytes 49156
  0.6 12.0 %copy-start.1 = (f32[16,128]{1,0:T(8,128)S(1)}, f32[16,128]{1,0:T(8,128)}, u32[]{:S(2)}) copy-start(f32[16,128]{1,0:T(8,128)} %slack.1) | copy-start | bytes 24580
  0.7 12.0 %copy-start = (f32[16,128]{1,0:T(8,128)S(1)}, f32[16,128]{1,0:T(8,128)}, u32[]{:S(2)}) copy-start(f32[16,128]{1,0:T(8,128)} %primal.1) | copy-start | bytes 24580
  0.7 12.0 %copy-start.4 = (f32[16,128]{1,0:T(8,128)S(1)}, f32[16,128]{1,0:T(8,128)}, u32[]{:S(2)}) copy-start(f32[16,128]{1,0:T(8,128)} %cost.1) | copy-start | bytes 24580
  0.7 10.4 %collective-permute-start.1 = (f32[32,128]{1,0:T(8,128)}, f32[32,128]{1,0:T(8,128)S(1)}, u32[]{:S(2)}, u32[]{:S(2)}) collective-permute-start(f32[32,128]{1,0:T(8,128)} %dual0), channel_id=1, source_target_pairs={{0,1},{1,2},{2,3},{3,0},{4,5},{5,6},{6,7},{7,4},{8,9},{9,10},{10,1... | collective-permute-start | bytes 49160 | tf_op jit(solution)/shard_map/ppermute | solution.py:559
  2.9 8.2 %collective-permute-start = (f32[32,128]{1,0:T(8,128)}, f32[32,128]{1,0:T(8,128)S(1)}, u32[]{:S(2)}, u32[]{:S(2)}) collective-permute-start(f32[32,128]{1,0:T(8,128)} %dual0), channel_id=1, source_target_pairs={{0,2},{1,3},{2,0},{3,1},{4,6},{5,7},{6,4},{7,5},{8,10},{9,11},{10,... | collective-permute-start | bytes 49160 | tf_op jit(solution)/shard_map/ppermute | solution.py:559
  5.5 5.6 %collective-permute-start.2 = (f32[32,128]{1,0:T(8,128)}, f32[32,128]{1,0:T(8,128)S(1)}, u32[]{:S(2)}, u32[]{:S(2)}) collective-permute-start(f32[32,128]{1,0:T(8,128)} %dual0), channel_id=1, source_target_pairs={{0,3},{1,0},{2,1},{3,2},{4,7},{5,4},{6,5},{7,6},{8,11},{9,8},{10,9... | collective-permute-start | bytes 49160 | tf_op jit(solution)/shard_map/ppermute | solution.py:559
  11.1 5.6 %collective-permute-start.3 = (f32[64,64,128]{2,1,0:T(8,128)S(1)}, f32[64,64,128]{2,1,0:T(8,128)S(1)}, u32[]{:S(2)}, u32[]{:S(2)}) collective-permute-start(f32[64,64,128]{2,1,0:T(8,128)S(1)} %get-tuple-element.38), channel_id=1, source_target_pairs={{0,4},{4,0},{1,5},{5,1},{2,6},{6,2},{3,7},{7,3},{8,12},{12,8},{9,1... | collective-permute-start | bytes 6291464 | tf_op jit(solution)/shard_map/ppermute | solution.py:566
  14.5 2.1 %collective-permute-start.4 = (f32[256,128]{1,0:T(8,128)S(1)}, f32[256,128]{1,0:T(8,128)S(1)}, u32[]{:S(2)}, u32[]{:S(2)}) collective-permute-start(f32[256,128]{1,0:T(8,128)S(1)} %get-tuple-element.47), channel_id=1, source_target_pairs={{0,4},{4,0},{1,5},{5,1},{2,6},{6,2},{3,7},{7,3},{8,12},{12,8},{9,1... | collective-permute-start | bytes 393224 | tf_op jit(solution)/shard_map/ppermute | solution.py:570
  16.9 39.1 %copy-start.3 = (f32[32,128]{1,0:T(8,128)S(1)}, f32[32,128]{1,0:T(8,128)}, u32[]{:S(2)}) copy-start(f32[32,128]{1,0:T(8,128)} %demand.1) | copy-start | bytes 49156
